TPU v7x, 1024 devices: a whole 8x8x8 slice. The times are simulated.
1024 devices in a mesh: segment: 4 (over x_lo), dp: 64 (over y, z), tensor: 4 (over x_hi, core).
Axes of the slice: x: 8 (x_hi: 2, x_lo: 4; x = x_hi * 4 + x_lo), y: 8, z: 8, core: 2. Of those that a mesh axis runs over, the one named last changes fastest.
Arguments:
- queries: bfloat16 [4, 16384, 1536], P('segment', 'dp', 'tensor'), as said below
- context: bfloat16 [4, 2, 16384, 1536], P('segment', None, 'dp', 'tensor'), as said below
- vis_blocks: int32 [4, 128, 2], P('segment', 'dp'), may hold values from 0 to 1, all different within a row
- vis_count: int32 [4, 128], P('segment', 'dp'), may hold values from 1 to 2
- w_out: bfloat16 [4, 1536, 1536], P('segment', 'dp', 'tensor'), may hold values from -0.15625 to 0.15625
- grad_out: bfloat16 [4, 16384, 1536], P('segment', 'dp'), may hold values from -16 to 16
Outputs:
- grad_queries: bfloat16 [4, 16384, 1536], P('segment', 'dp', 'tensor')
- grad_context: bfloat16 [4, 2, 16384, 1536], P('segment', None, 'dp', 'tensor')
- grad_w_out: float32 [4, 1536, 1536], P('segment', 'dp', 'tensor')
Inputs may be any that keep to these rules, and one draw needn't show every extreme that they name: `vis_blocks`: each row names 2 different context blocks of its scene. `queries`: entries lie within -5 and 5. `context`: entries lie within -5 and 5.
All inputs are finite; a program needn't handle non-finite values.
Results may differ from a plain program's by a relative error of at most 0.034.
Values may be sent and summed in bfloat16 or wider, within the bound.
No kernel may reach another device: no remote copies, remote signals or barrier semaphores. Data moves between devices by JAX's collectives and lax.ppermute only.
A program may use at most 32 MiB of HBM per device.

v0:
```python
import jax
import jax.numpy as jnp
from jax import lax
from jax.sharding import PartitionSpec as P

HD = 128
BLK = 128
CTX_BLK = 2
VIS = 2
TOK_DEV = 256
QB = 2


def from_behind(x, axis, by):
    count = lax.axis_size(axis)
    return lax.ppermute(x, axis, [(i, (i + by) % count) for i in range(count)])


def shards(queries, context, vis_blocks, vis_count, w_out, grad_out):
    heads = queries.shape[2] // HD
    width = queries.shape[2]
    scale = 1.0 / HD**0.5
    used = from_behind(context, "segment", 1)
    qry = queries[0].reshape(QB, BLK, heads, HD)
    keys_all = used[0, 0].reshape(CTX_BLK, BLK, heads, HD)
    vals_all = used[0, 1].reshape(CTX_BLK, BLK, heads, HD)
    ids = vis_blocks[0]
    counts = vis_count[0]
    keys = keys_all[ids]
    vals = vals_all[ids]
    score = jnp.einsum("qihd,qvjhd->qhivj", qry, keys, preferred_element_type=jnp.float32) * scale
    live = jnp.arange(VIS)[None, :] < counts[:, None]
    score = jnp.where(live[:, None, None, :, None], score, jnp.float32(-1e30))
    top = jnp.max(score, axis=(3, 4), keepdims=True)
    expo = jnp.exp(score - top)
    prob = expo / jnp.sum(expo, axis=(3, 4), keepdims=True)
    prob_b = prob.astype(jnp.bfloat16)
    attn = jnp.einsum("qhivj,qvjhd->qihd", prob_b, vals, preferred_element_type=jnp.float32).astype(
        jnp.bfloat16
    )
    attn_rows = attn.reshape(TOK_DEV, width)
    cotan = grad_out[0]
    d_attn = jnp.dot(
        cotan,
        lax.all_gather(w_out, "dp", axis=1, tiled=True)[0],
        preferred_element_type=jnp.float32,
    ).astype(jnp.bfloat16)
    groups = lax.axis_size("dp")
    block_rows = cotan.shape[1] // groups
    attn_whole = lax.all_gather(attn_rows, "tensor", axis=1, tiled=True)
    ranks = lax.axis_size("tensor")
    sub_rows = block_rows // ranks
    picked = lax.dynamic_index_in_dim(
        cotan.reshape(TOK_DEV, groups, ranks, sub_rows), lax.axis_index("tensor"), 2, keepdims=False
    )
    picked = picked.reshape(TOK_DEV, groups * sub_rows)
    summed = lax.psum_scatter(
        lax.dot_general(
            picked, attn_whole, (((0,), (0,)), ((), ())), preferred_element_type=jnp.float32
        ),
        "dp",
        scatter_dimension=0,
        tiled=True,
    )
    grad_weight = (
        lax.all_to_all(
            summed.astype(jnp.bfloat16), "tensor", split_axis=1, concat_axis=0, tiled=True
        )
        .astype(summed.dtype)
        .reshape(1, block_rows, width)
    )
    da4 = d_attn.reshape(QB, BLK, heads, HD)
    delta = jnp.sum(da4.astype(jnp.float32) * attn.astype(jnp.float32), axis=-1).transpose(0, 2, 1)
    dprob = jnp.einsum("qihd,qvjhd->qhivj", da4, vals, preferred_element_type=jnp.float32)
    dscore = (prob * (dprob - delta[:, :, :, None, None])).astype(jnp.bfloat16)
    grad_q = (
        jnp.einsum("qhivj,qvjhd->qihd", dscore, keys, preferred_element_type=jnp.float32) * scale
    ).astype(jnp.bfloat16)
    dkey = jnp.einsum("qhivj,qihd->qvjhd", dscore, qry, preferred_element_type=jnp.float32) * scale
    dval = jnp.einsum("qhivj,qihd->qvjhd", prob_b, da4, preferred_element_type=jnp.float32)
    onehot = (ids.reshape(-1)[:, None] == jnp.arange(CTX_BLK)[None, :]).astype(jnp.float32)
    gkey = jnp.einsum(
        "sc,sjhd->cjhd",
        onehot,
        dkey.reshape(QB * VIS, BLK, heads, HD),
        precision=lax.Precision.HIGHEST,
    )
    gval = jnp.einsum(
        "sc,sjhd->cjhd",
        onehot,
        dval.reshape(QB * VIS, BLK, heads, HD),
        precision=lax.Precision.HIGHEST,
    )
    grad_used = jnp.stack([gkey, gval]).reshape(1, 2, CTX_BLK * BLK, width).astype(jnp.bfloat16)
    grad_context = from_behind(grad_used, "segment", -1)
    return (grad_q.reshape(1, TOK_DEV, width), grad_context, grad_weight)


def solution(mesh):
    in_specs = (
        P("segment", "dp", "tensor"),
        P("segment", None, "dp", "tensor"),
        P("segment", "dp", None),
        P("segment", "dp"),
        P("segment", "dp", "tensor"),
        P("segment", "dp", None),
    )
    out_specs = (
        P("segment", "dp", "tensor"),
        P("segment", None, "dp", "tensor"),
        P("segment", "dp", "tensor"),
    )
    return jax.shard_map(shards, mesh=mesh, in_specs=in_specs, out_specs=out_specs, check_vma=False)
```

profile of v0, /device:TPU:14, one launch (start us, length us, event | category | flops | bytes accessed | tf_op | source)
XLA Modules:
  0.0 463.6 jit_solution(7241132090064873817)
XLA Ops:
  7.2 0.7 all-gather.2.cloned.1.call-update
  7.9 5.1 %collective-permute-start = (bf16[1,2,256,384]{3,2,1,0:T(8,128)(2,1)}, bf16[1,2,256,384]{3,2,1,0:T(8,128)(2,1)S(1)}, u32[]{:S(2)}, u32[]{:S(2)}) collective-permute-start(bf16[1,2,256,384]{3,2,1,0:T(8,128)(2,1)} %param.7), channel_id=1, source_target_pairs={{0,256},{256,512},{512,768},{768,0},{1,257},{257,513},{513,769},{7... | collective-permute-start | bytes 1179656 | tf_op jit(solution)/shard_map/ppermute | solution.py:16
  13.0 1.4 copy.109
  14.4 0.3 reshape_squeeze.15
  14.7 0.4 copy-done.4
  15.8 1.3 dynamic-slice
  17.9 3.8 collective-permute-done
  21.9 0.6 gather_fusion
  22.5 0.6 gather_fusion.1
  23.2 0.3 fusion.34
  23.6 89.4 %all-gather.2.cloned.1.call-done = bf16[1,1536,384]{2,1,0:T(8,128)(2,1)} async-done(((bf16[1,24,384]{2,1,0:T(8,128)(2,1)}), bf16[1,1536,384]{2,1,0:T(8,128)(2,1)}) %all-gather.2.cloned.1.call-update) | async-done | bytes 1179664 | tf_op jit(solution)/shard_map/all_gather | solution.py:45
  113.0 1.9 fusion.8
  115.1 0.4 multiply_reduce_fusion
  115.5 0.3 convolution_bitcast_fusion
  115.8 0.6 copy-done.2
  116.5 0.3 fusion.4
  116.8 0.2 fusion
  117.1 1.3 convolution_convert_fusion.1
  118.7 0.3 copy.106
  119.0 1.3 convolution_convert_fusion
  120.6 0.8 pad_maximum_fusion
  121.4 3.4 collective-permute-start.1
  125.0 15.2 %all_gather.7 = bf16[256,1536]{0,1:T(8,128)(2,1)S(1)} all-gather(bf16[256,384]{0,1:T(8,128)(2,1)S(1)} %bitcast.94), channel_id=1, replica_groups=mesh['segment'=4,'dp'=64,'tensor'=4] {'tensor'}, dimensions={1}, use_global_device_ids=true | all-gather | bytes 983040 | tf_op jit(solution)/shard_map/all_gather | solution.py:50
  140.2 0.5 fusion.35
  140.7 302.1 %all-reduce.2 = bf16[384,1536]{1,0:T(8,128)(2,1)} all-reduce(f32[384,1536]{1,0:T(8,128)S(1)} %fusion.35), channel_id=2, replica_groups=mesh['segment'=4,'dp'=64,'tensor'=4] {'dp'}, use_global_device_ids=true, to_apply=%region_3.4.clone | all-reduce | flops 589824 | bytes 3538944
  442.8 1.4 dynamic-slice_convert_fusion
  444.2 8.1 %all-to-all-start = ((bf16[6,4,384]{2,0,1:T(8,128)(2,1)}), bf16[6,4,384]{2,0,1:T(8,128)(2,1)S(1)}, u32[]{:S(2)}, u32[]{:S(2)}) async-start(bf16[6,4,384]{2,0,1:T(8,128)(2,1)} %bitcast.25), calls=%async_computation | async-start | bytes 49152 | tf_op jit(solution)/shard_map/all_to_all | solution.py:66
  452.3 0.3 fusion.14
  452.8 0.9 reshape.170
  453.7 0.5 all-to-all-done
  454.2 0.6 reshape.142
  454.8 1.9 copy.113
  (39 shorter events, 2.5 us)
Async XLA Ops:
  7.2 105.9 %all-gather.2.cloned.1.call-start = ((), (), s32[]{:S(2)}) async-start(), calls=%async_computation.1 | async-start | bytes 1198080 | tf_op jit(solution)/shard_map/all_gather | solution.py:45
  7.9 13.8 %collective-permute-start = (bf16[1,2,256,384]{3,2,1,0:T(8,128)(2,1)}, bf16[1,2,256,384]{3,2,1,0:T(8,128)(2,1)S(1)}, u32[]{:S(2)}, u32[]{:S(2)}) collective-permute-start(bf16[1,2,256,384]{3,2,1,0:T(8,128)(2,1)} %param.7), channel_id=1, source_target_pairs={{0,256},{256,512},{512,768},{768,0},{1,257},{257,513},{513,769},{7... | collective-permute-start | bytes 1179656 | tf_op jit(solution)/shard_map/ppermute | solution.py:16
  14.4 0.7 copy-start.4
  14.4 0.9 copy-start.3
  14.7 3.1 copy-start.5
  23.2 91.9 %copy-start.1 = (bf16[4,128,3,128]{3,1,2,0:T(8,128)(2,1)}, bf16[4,128,3,128]{3,1,2,0:T(8,128)(2,1)S(1)}, u32[]{:S(2)}) copy-start(bf16[4,128,3,128]{3,1,2,0:T(8,128)(2,1)S(1)} %gather_fusion.1) | copy-start | bytes 1179652
  23.2 89.8 %copy-start = (bf16[1,256,1536]{2,1,0:T(8,128)(2,1)S(1)}, bf16[1,256,1536]{2,1,0:T(8,128)(2,1)}, u32[]{:S(2)}) copy-start(bf16[1,256,1536]{2,1,0:T(8,128)(2,1)} %param.11) | copy-start | bytes 2359300
  115.5 1.0 copy-start.2
  121.4 333.4 %collective-permute-start.1 = (bf16[1,2,256,384]{2,3,1,0:T(8,128)(2,1)}, bf16[1,2,256,384]{2,3,1,0:T(8,128)(2,1)}, u32[]{:S(2)}, u32[]{:S(2)}) collective-permute-start(bf16[1,2,256,384]{2,3,1,0:T(8,128)(2,1)} %pad_maximum_fusion), channel_id=1, source_target_pairs={{0,768},{256,0},{512,256},{768,512},{1,769},{257,1},{513,257},{769... | collective-permute-start | bytes 1179656 | tf_op jit(solution)/shard_map/ppermute | solution.py:16
  444.2 10.0 %all-to-all-start = ((bf16[6,4,384]{2,0,1:T(8,128)(2,1)}), bf16[6,4,384]{2,0,1:T(8,128)(2,1)S(1)}, u32[]{:S(2)}, u32[]{:S(2)}) async-start(bf16[6,4,384]{2,0,1:T(8,128)(2,1)} %bitcast.25), calls=%async_computation | async-start | bytes 49152 | tf_op jit(solution)/shard_map/all_to_all | solution.py:66
Sparse Core Ops, SparseCore 0:
  12.2 100.7 all-gather.1
where the time goes:
time: 470 us; the launch traced here: 464 us
  blocking collectives  317 us (67%)
  waiting for transfers between devices  94.4 us (20%)
  starting transfers between devices  16.5 us (4%)
  between operations  15 us (3%)
  local copies, waits for them, and re-layouts  12.5 us (3%)
  matrix products  6.8 us (1%)
    unnamed x1, blocking collectives  302 us
    all_gather x1, waiting for transfers between devices, shards(): lax.all_gather(w_out, 'dp', axis=1, tiled=True)[0]  89.4 us
    all_gather x1, blocking collectives, shards(): attn_whole = lax.all_gather(attn_rows, 'tensor', axis=1, tiled=True)  15.2 us
  transfers between devices with their start and end apart: 4, of which 3 were waited for; matrix products, arithmetic and copies ran while one was open for 2% of the time, Pallas kernels for 0%

commit v1 on v0

v1 whole, which is shorter than its diff:
```python
import jax
import jax.numpy as jnp
from jax import lax
from jax.experimental import pallas as pl
from jax.experimental.pallas import tpu as pltpu
from jax.sharding import Mesh, PartitionSpec as P

HD = 128
BLK = 128
VMEM_LIMIT = 48 * 1024 * 1024
DP = ("y", "z")


def from_behind(x, axis, by):
    count = lax.axis_size(axis)
    return lax.ppermute(x, axis, [(i, (i + by) % count) for i in range(count)])


def swap(x, axis):
    return lax.all_to_all(x, axis, split_axis=0, concat_axis=0, tiled=True)


def dot(a, b, dims):
    return lax.dot_general(a, b, (dims, ((), ())), preferred_element_type=jnp.float32)


def live_mask(ids_ref, cnt_ref, tokens, ctx):
    row = lax.broadcasted_iota(jnp.int32, (tokens, ctx), 0) // BLK
    col = lax.broadcasted_iota(jnp.int32, (tokens, ctx), 1) // BLK
    live = None
    for b in range(tokens // BLK):
        for k in range(ids_ref.shape[2]):
            block = jnp.where(k < cnt_ref[0, b], ids_ref[0, b, k], -1)
            here = (row == b) & (col == block)
            live = here if live is None else live | here
    return live


def forward_kernel(ids_ref, cnt_ref, q_ref, kv_ref, cot_ref, attn_ref, prob_ref, part_ref):
    tokens, width = q_ref.shape[1:]
    ctx = kv_ref.shape[2]
    live = live_mask(ids_ref, cnt_ref, tokens, ctx)
    scale = 1.0 / HD**0.5
    for h in range(width // HD):
        cols = slice(h * HD, (h + 1) * HD)
        score = dot(q_ref[0, :, cols], kv_ref[0, 0, :, cols], ((1,), (1,))) * scale
        score = jnp.where(live, score, jnp.float32(-1e30))
        expo = jnp.exp(score - jnp.max(score, axis=1, keepdims=True))
        prob = expo / jnp.sum(expo, axis=1, keepdims=True)
        prob_ref[h] = prob
        attn_ref[:, cols] = dot(
            prob.astype(jnp.bfloat16), kv_ref[0, 1, :, cols], ((1,), (0,))
        ).astype(jnp.bfloat16)
    first, second, rows, _ = part_ref.shape
    attn = attn_ref[...]
    for j in range(second):
        span = first * rows
        part = dot(cot_ref[0, :, j * span : (j + 1) * span], attn, ((0,), (0,)))
        for i in range(first):
            part_ref[i, j] = part[i * rows : (i + 1) * rows].astype(jnp.bfloat16)


def backward_kernel(q_ref, kv_ref, cot_ref, attn_ref, prob_ref, w_ref, gq_ref, gkv_ref):
    width = q_ref.shape[2]
    scale = 1.0 / HD**0.5
    d_attn = dot(cot_ref[0], w_ref[...], ((1,), (0,))).astype(jnp.bfloat16)
    for h in range(width // HD):
        cols = slice(h * HD, (h + 1) * HD)
        da = d_attn[:, cols]
        q, k, v = q_ref[0, :, cols], kv_ref[0, 0, :, cols], kv_ref[0, 1, :, cols]
        prob = prob_ref[h]
        delta = jnp.sum(
            da.astype(jnp.float32) * attn_ref[:, cols].astype(jnp.float32), axis=1, keepdims=True
        )
        dprob = dot(da, v, ((1,), (1,)))
        dscore = (prob * (dprob - delta)).astype(jnp.bfloat16)
        gq_ref[0, :, cols] = (dot(dscore, k, ((1,), (0,))) * scale).astype(jnp.bfloat16)
        gkv_ref[0, 0, :, cols] = (dot(dscore, q, ((0,), (0,))) * scale).astype(jnp.bfloat16)
        gkv_ref[0, 1, :, cols] = dot(prob.astype(jnp.bfloat16), da, ((0,), (0,))).astype(jnp.bfloat16)


def fold_kernel(parts_ref, total_ref):
    total = parts_ref[0].astype(jnp.float32)
    for i in range(1, parts_ref.shape[0]):
        total += parts_ref[i].astype(jnp.float32)
    total_ref[...] = total.astype(total_ref.dtype)


def fold(parts, dtype):
    vmem = pl.BlockSpec(memory_space=pltpu.VMEM)
    return pl.pallas_call(
        fold_kernel,
        name="fold",
        out_shape=jax.ShapeDtypeStruct(parts.shape[1:], dtype),
        in_specs=[vmem],
        out_specs=vmem,
        compiler_params=pltpu.CompilerParams(vmem_limit_bytes=VMEM_LIMIT),
        cost_estimate=pl.CostEstimate(flops=parts.size, bytes_accessed=2 * parts.size, transcendentals=0),
    )(parts)


def shards(queries, context, vis_blocks, vis_count, w_out, grad_out):
    tokens, width = queries.shape[1:]
    ctx = context.shape[2]
    heads = width // HD
    model = grad_out.shape[2]
    ny, nz = (lax.axis_size(a) for a in DP)
    rows = w_out.shape[1]
    smem = pl.BlockSpec(memory_space=pltpu.SMEM)
    vmem = pl.BlockSpec(memory_space=pltpu.VMEM)
    params = pltpu.CompilerParams(vmem_limit_bytes=VMEM_LIMIT)

    used = from_behind(context, "segment", 1)
    near = swap(jnp.broadcast_to(w_out, (nz, rows, width)), "z")
    weight = swap(jnp.broadcast_to(near[None], (ny, nz, rows, width)), "y").reshape(model, width)

    attn, prob, part = pl.pallas_call(
        forward_kernel,
        name="forward",
        out_shape=(
            jax.ShapeDtypeStruct((tokens, width), jnp.bfloat16),
            jax.ShapeDtypeStruct((heads, tokens, ctx), jnp.float32),
            jax.ShapeDtypeStruct((nz, ny, rows, width), jnp.bfloat16),
        ),
        in_specs=[smem, smem, vmem, vmem, vmem],
        out_specs=(vmem, vmem, vmem),
        compiler_params=params,
        cost_estimate=pl.CostEstimate(
            flops=2 * tokens * width * (2 * ctx + model), bytes_accessed=4 << 20, transcendentals=heads * tokens * ctx
        ),
    )(vis_blocks, vis_count, queries, used, grad_out)

    over_z = fold(swap(part, "z"), jnp.bfloat16)
    grad_weight = fold(swap(over_z, "y"), jnp.float32)[None]

    grad_q, grad_used = pl.pallas_call(
        backward_kernel,
        name="backward",
        out_shape=(
            jax.ShapeDtypeStruct(queries.shape, jnp.bfloat16),
            jax.ShapeDtypeStruct(context.shape, jnp.bfloat16),
        ),
        in_specs=[vmem] * 6,
        out_specs=(vmem, vmem),
        compiler_params=params,
        cost_estimate=pl.CostEstimate(
            flops=2 * tokens * width * (4 * ctx + model), bytes_accessed=4 << 20, transcendentals=0
        ),
    )(queries, used, grad_out, attn, prob, weight)
    grad_context = from_behind(grad_used, "segment", -1)
    return grad_q, grad_context, grad_weight


def solution(mesh):
    fine = Mesh(mesh.devices.reshape(4, 8, 8, 4), ("segment", "y", "z", "tensor"))
    in_specs = (
        P("segment", DP, "tensor"),
        P("segment", None, DP, "tensor"),
        P("segment", DP, None),
        P("segment", DP),
        P("segment", DP, "tensor"),
        P("segment", DP, None),
    )
    out_specs = (
        P("segment", DP, "tensor"),
        P("segment", None, DP, "tensor"),
        P("segment", DP, "tensor"),
    )
    return jax.shard_map(shards, mesh=fine, in_specs=in_specs, out_specs=out_specs, check_vma=False)
```

time: 470 us -> 115 us (0.24); the launches traced: 464 us -> 114 us
  blocking collectives: 317 us -> 38.2 us
  waiting for transfers between devices: 94.4 us -> 42 us
  between operations: 15 us -> 0.7 us
  matrix products: 6.8 us -> 0 us
  Pallas kernels: 0 us -> 6.5 us
  local copies, waits for them, and re-layouts: 12.5 us -> 7.21 us
    unnamed x1 -> x0, blocking collectives: 302 us -> none
    all_gather x1 -> x0, waiting for transfers between devices: 89.4 us -> none  [shards(): lax.all_gather(w_out, 'dp', axis=1, tiled=True)[0]]
    all_to_all x0 -> x2, blocking collectives: none -> 38.2 us  [swap(): return lax.all_to_all(x, axis, split_axis=0, concat_axis=0, tiled=True)]
    all_to_all x1 -> x2, waiting for transfers between devices: 0.52 us -> 35.7 us  [swap(): return lax.all_to_all(x, axis, split_axis=0, concat_axis=0, tiled=True)]
    all_gather x1 -> x0, blocking collectives: 15.2 us -> none  [shards(): attn_whole = lax.all_gather(attn_rows, 'tensor', axis=1, tiled=True)]
    dot_general x10 -> x0, matrix products: 6.8 us -> none  [the longest x1 1.85 us: shards(): jnp.dot(cotan, lax.all_gather(w_out, 'dp', axis=1, tiled=True)[0], prefer...]
    pallas_call x0 -> x4, Pallas kernels: none -> 6.5 us  [the longest x1 3.43 us: shards(): pl.pallas_call(forward_kernel, name='forward', out_shape=(jax.ShapeDtypeS...]
    all_to_all x1 -> x2, starting transfers between devices: 8.06 us -> 11.3 us  [swap(): return lax.all_to_all(x, axis, split_axis=0, concat_axis=0, tiled=True)]
  transfers between devices with their start and end apart: 4 -> 4, of which waited for: 3 -> 3; matrix products, arithmetic and copies ran while one was open for 2% -> 0% of each run, Pallas kernels for 0% -> 6%
where the time goes in v1:
time: 115 us; the launch traced here: 114 us
  waiting for transfers between devices  42 us (37%)
  blocking collectives  38.2 us (33%)
  starting transfers between devices  19.7 us (17%)
  local copies, waits for them, and re-layouts  7.21 us (6%)
  Pallas kernels  6.5 us (6%)
    all_to_all x2, blocking collectives, swap(): return lax.all_to_all(x, axis, split_axis=0, concat_axis=0, tiled=True)  38.2 us
    all_to_all x2, waiting for transfers between devices, swap(): return lax.all_to_all(x, axis, split_axis=0, concat_axis=0, tiled=True)  35.7 us
    all_to_all x2, starting transfers between devices, swap(): return lax.all_to_all(x, axis, split_axis=0, concat_axis=0, tiled=True)  11.3 us
    ppermute x2, starting transfers between devices, from_behind(): return lax.ppermute(x, axis, [(i, (i + by) % count) for i in range(count)])  8.42 us
    ppermute x2, waiting for transfers between devices, from_behind(): return lax.ppermute(x, axis, [(i, (i + by) % count) for i in range(count)])  6.3 us
    unnamed x21, local copies, waits for them, and re-layouts  5.3 us
    pallas_call x1, Pallas kernels, shards(): pl.pallas_call(forward_kernel, name='forward', out_shape=(jax.ShapeDtypeS...  3.43 us
  transfers between devices with their start and end apart: 4, of which 3 were waited for; matrix products, arithmetic and copies ran while one was open for 0% of the time, Pallas kernels for 6%

profile of v1, /device:TPU:14, one launch (start us, length us, event | category | flops | bytes accessed | tf_op | source)
XLA Modules:
  0.0 114.2 jit_solution(466366761747779822)
XLA Ops:
  0.6 0.7 broadcast_in_dim.17
  1.4 25.9 %all_to_all.20 = bf16[8,24,384]{2,1,0:T(8,128)(2,1)S(1)} all-to-all(bf16[8,24,384]{2,1,0:T(8,128)(2,1)S(1)} %broadcast_in_dim.17), channel_id=1, replica_groups=mesh['segment'=4,'y'=8,'z'=8,'tensor'=4] {'z'}, dimensions={0} | all-to-all | bytes 294912 | tf_op jit(solution)/shard_map/all_to_all | solution.py:20
  27.3 1.2 %broadcast_in_dim.18 = bf16[8,8,24,384]{3,2,1,0:T(8,128)(2,1)} broadcast(bf16[8,24,384]{2,1,0:T(8,128)(2,1)S(1)} %all_to_all.20), dimensions={1,2,3} | broadcast | bytes 1327104 | tf_op jit(solution)/shard_map/broadcast_in_dim | solution.py:115
  28.4 0.0 copy-start.9
  28.4 0.0 copy-start
  28.4 0.0 copy-start.3
  28.4 0.0 copy-start.8
  28.5 7.7 %all-to-all-start.1 = ((bf16[8,8,24,384]{3,2,1,0:T(8,128)(2,1)}), bf16[8,8,24,384]{3,2,1,0:T(8,128)(2,1)S(1)}, u32[]{:S(2)}, u32[]{:S(2)}) async-start(bf16[8,8,24,384]{3,2,1,0:T(8,128)(2,1)} %broadcast_in_dim.18), calls=%async_computation.1 | async-start | bytes 2359296 | tf_op jit(solution)/shard_map/all_to_all | solution.py:20
  36.2 0.0 copy-done.9
  36.2 5.1 %collective-permute-start = (bf16[1,2,256,384]{3,2,1,0:T(8,128)(2,1)S(1)}, bf16[1,2,256,384]{3,2,1,0:T(8,128)(2,1)S(1)}, u32[]{:S(2)}, u32[]{:S(2)}) collective-permute-start(bf16[1,2,256,384]{3,2,1,0:T(8,128)(2,1)S(1)} %copy-done.9), channel_id=1, source_target_pairs={{0,256},{256,512},{512,768},{768,0},{1,257},{257,513},{513,769},{7... | collective-permute-start | bytes 1179656 | tf_op jit(solution)/shard_map/ppermute | solution.py:16
  41.3 6.3 %collective-permute-done.kv_ref = bf16[1,2,256,384]{3,2,1,0:T(8,128)(2,1)S(1)} collective-permute-done((bf16[1,2,256,384]{3,2,1,0:T(8,128)(2,1)S(1)}, bf16[1,2,256,384]{3,2,1,0:T(8,128)(2,1)S(1)}, u32[]{:S(2)}, u32[]{:S(2)}) %collective-permute-start) | collective-permute-done | bytes 393248 | tf_op jit(solution)/shard_map/ppermute | solution.py:16
  47.5 0.0 copy-done
  47.6 0.0 copy-done.3
  47.6 0.0 copy-done.7
  47.6 0.0 copy-done.8
  47.6 3.4 %forward.1 = (bf16[256,384]{1,0:T(8,128)(2,1)S(1)}, f32[3,256,256]{2,1,0:T(8,128)S(1)}, bf16[8,8,24,384]{3,2,1,0:T(8,128)(2,1)}) custom-call(s32[1,2,2]{2,1,0:T(2,128)S(1)} %copy-done.7, s32[1,2]{1,0:T(1,128)S(1)} %copy-done.8, bf16[1,256,384]{2,1,0:T(8,128)(2,1)S(1)} %copy-done.3, bf16[1,2,256,384]{3,2,1,0:T(8,128)(2,1)S(1)} %collective-permute-done.kv_ref, ...), custom_call_target="tpu_custom_call" | custom-call | flops 402653184 | bytes 4194304 | tf_op jit(solution)/shard_map/forward/pallas_call | solution.py:117
  51.0 0.9 copy-done.1
  51.9 0.7 copy-done.5
  52.5 13.4 %all-to-all-done.1 = bf16[8,8,24,384]{3,2,1,0:T(8,128)(2,1)S(1)} async-done(((bf16[8,8,24,384]{3,2,1,0:T(8,128)(2,1)}), bf16[8,8,24,384]{3,2,1,0:T(8,128)(2,1)S(1)}, u32[]{:S(2)}, u32[]{:S(2)}) %all-to-all-start.1) | async-done | bytes 1179680 | tf_op jit(solution)/shard_map/all_to_all | solution.py:20
  65.9 3.6 %all-to-all-start.2 = ((bf16[8,8,24,384]{3,2,1,0:T(8,128)(2,1)}), bf16[8,8,24,384]{3,2,1,0:T(8,128)(2,1)S(1)}, u32[]{:S(2)}, u32[]{:S(2)}) async-start(bf16[8,8,24,384]{3,2,1,0:T(8,128)(2,1)} %get-tuple-element.12), calls=%async_computation.2 | async-start | bytes 2359296 | tf_op jit(solution)/shard_map/all_to_all | solution.py:20
  69.5 0.0 copy-start.2
  69.5 1.1 copy-done.2
  70.6 0.9 copy-done.4
  71.6 0.9 copy-done.6
  72.5 2.3 %backward.1 = (bf16[1,256,384]{2,1,0:T(8,128)(2,1)}, bf16[1,2,256,384]{3,2,1,0:T(8,128)(2,1)}) custom-call(bf16[1,256,384]{2,1,0:T(8,128)(2,1)S(1)} %copy-done.4, bf16[1,2,256,384]{3,2,1,0:T(8,128)(2,1)S(1)} %collective-permute-done.kv_ref, bf16[1,256,1536]{2,1,0:T(8,128)(2,1)S(1)} %copy-done, bf16[256,384]{1,0:T(8,128)(2,1)S(1)} %copy-done.6, ...), custom_call_target="tpu_custom_call" | custom-call | flops 503316480 | bytes 4194304 | tf_op jit(solution)/shard_map/backward/pallas_call | solution.py:136
  74.8 3.3 %collective-permute-start.1 = (bf16[1,2,256,384]{3,2,1,0:T(8,128)(2,1)}, bf16[1,2,256,384]{3,2,1,0:T(8,128)(2,1)S(1)}, u32[]{:S(2)}, u32[]{:S(2)}) collective-permute-start(bf16[1,2,256,384]{3,2,1,0:T(8,128)(2,1)} %get-tuple-element.11), channel_id=1, source_target_pairs={{0,768},{256,0},{512,256},{768,512},{1,769},{257,1},{513,257},{769... | collective-permute-start | bytes 1179656 | tf_op jit(solution)/shard_map/ppermute | solution.py:16
  78.1 22.3 %all-to-all-done.2.parts_ref = bf16[8,8,24,384]{3,2,1,0:T(8,128)(2,1)S(1)} async-done(((bf16[8,8,24,384]{3,2,1,0:T(8,128)(2,1)}), bf16[8,8,24,384]{3,2,1,0:T(8,128)(2,1)S(1)}, u32[]{:S(2)}, u32[]{:S(2)}) %all-to-all-start.2) | async-done | bytes 1179680 | tf_op jit(solution)/shard_map/all_to_all | solution.py:20
  100.4 0.2 fold.2
  100.6 12.3 %all_to_all.21.parts_ref = bf16[8,24,384]{2,1,0:T(8,128)(2,1)S(1)} all-to-all(bf16[8,24,384]{2,1,0:T(8,128)(2,1)S(1)} %fold.2), channel_id=1, replica_groups=mesh['segment'=4,'y'=8,'z'=8,'tensor'=4] {'y'}, dimensions={0} | all-to-all | bytes 294912 | tf_op jit(solution)/shard_map/all_to_all | solution.py:20
  112.8 0.6 fold.3
  113.5 0.0 collective-permute-done.1
  113.5 0.7 copy.10
  (5 shorter events, 0.0 us)
Async XLA Ops:
  28.4 7.7 %copy-start.9 = (bf16[1,2,256,384]{3,2,1,0:T(8,128)(2,1)S(1)}, bf16[1,2,256,384]{3,2,1,0:T(8,128)(2,1)}, u32[]{:S(2)}) copy-start(bf16[1,2,256,384]{3,2,1,0:T(8,128)(2,1)} %param.7) | copy-start | bytes 1179652
  28.4 19.1 %copy-start = (bf16[1,256,1536]{2,1,0:T(8,128)(2,1)S(1)}, bf16[1,256,1536]{2,1,0:T(8,128)(2,1)}, u32[]{:S(2)}) copy-start(bf16[1,256,1536]{2,1,0:T(8,128)(2,1)} %cot_ref.3) | copy-start | bytes 2359300
  28.4 19.1 %copy-start.3 = (bf16[1,256,384]{2,1,0:T(8,128)(2,1)S(1)}, bf16[1,256,384]{2,1,0:T(8,128)(2,1)}, u32[]{:S(2)}) copy-start(bf16[1,256,384]{2,1,0:T(8,128)(2,1)} %q_ref.3) | copy-start | bytes 589828
  28.4 19.1 %copy-start.7 = (s32[1,2,2]{2,1,0:T(2,128)S(1)}, s32[1,2,2]{2,1,0:T(2,128)}, u32[]{:S(2)}) copy-start(s32[1,2,2]{2,1,0:T(2,128)} %ids_ref.1) | copy-start | bytes 52
  28.4 19.1 %copy-start.8 = (s32[1,2]{1,0:T(1,128)S(1)}, s32[1,2]{1,0:T(1,128)}, u32[]{:S(2)}) copy-start(s32[1,2]{1,0:T(1,128)} %cnt_ref.1) | copy-start | bytes 28
  28.5 37.5 %all-to-all-start.1 = ((bf16[8,8,24,384]{3,2,1,0:T(8,128)(2,1)}), bf16[8,8,24,384]{3,2,1,0:T(8,128)(2,1)S(1)}, u32[]{:S(2)}, u32[]{:S(2)}) async-start(bf16[8,8,24,384]{3,2,1,0:T(8,128)(2,1)} %broadcast_in_dim.18), calls=%async_computation.1 | async-start | bytes 2359296 | tf_op jit(solution)/shard_map/all_to_all | solution.py:20
  36.2 11.4 %collective-permute-start = (bf16[1,2,256,384]{3,2,1,0:T(8,128)(2,1)S(1)}, bf16[1,2,256,384]{3,2,1,0:T(8,128)(2,1)S(1)}, u32[]{:S(2)}, u32[]{:S(2)}) collective-permute-start(bf16[1,2,256,384]{3,2,1,0:T(8,128)(2,1)S(1)} %copy-done.9), channel_id=1, source_target_pairs={{0,256},{256,512},{512,768},{768,0},{1,257},{257,513},{513,769},{7... | collective-permute-start | bytes 1179656 | tf_op jit(solution)/shard_map/ppermute | solution.py:16
  51.0 0.9 copy-start.1
  51.9 0.7 copy-start.5
  65.9 34.5 %all-to-all-start.2 = ((bf16[8,8,24,384]{3,2,1,0:T(8,128)(2,1)}), bf16[8,8,24,384]{3,2,1,0:T(8,128)(2,1)S(1)}, u32[]{:S(2)}, u32[]{:S(2)}) async-start(bf16[8,8,24,384]{3,2,1,0:T(8,128)(2,1)} %get-tuple-element.12), calls=%async_computation.2 | async-start | bytes 2359296 | tf_op jit(solution)/shard_map/all_to_all | solution.py:20
  69.5 1.1 copy-start.2
  70.6 0.9 copy-start.4
  71.6 0.9 copy-start.6
  74.8 38.7 %collective-permute-start.1 = (bf16[1,2,256,384]{3,2,1,0:T(8,128)(2,1)}, bf16[1,2,256,384]{3,2,1,0:T(8,128)(2,1)S(1)}, u32[]{:S(2)}, u32[]{:S(2)}) collective-permute-start(bf16[1,2,256,384]{3,2,1,0:T(8,128)(2,1)} %get-tuple-element.11), channel_id=1, source_target_pairs={{0,768},{256,0},{512,256},{768,512},{1,769},{257,1},{513,257},{769... | collective-permute-start | bytes 1179656 | tf_op jit(solution)/shard_map/ppermute | solution.py:16

commit v2 on v1

--- a/solution.py
+++ b/solution.py
@@ -7,8 +7,9 @@
 
 HD = 128
 BLK = 128
-VMEM_LIMIT = 48 * 1024 * 1024
+VMEM_LIMIT = 16 * 1024 * 1024
 DP = ("y", "z")
+PLANE = ("y", "z", "tensor")
 
 
 def from_behind(x, axis, by):
@@ -16,8 +17,21 @@
     return lax.ppermute(x, axis, [(i, (i + by) % count) for i in range(count)])
 
 
-def swap(x, axis):
-    return lax.all_to_all(x, axis, split_axis=0, concat_axis=0, tiled=True)
+def lines(first):
+    ny, nz, nt = (lax.axis_size(a) for a in PLANE)
+    groups = []
+    for t in range(nt):
+        if (t % 2 == 0) == first:
+            groups += [[(y * nz + z) * nt + t for z in range(nz)] for y in range(ny)]
+        else:
+            groups += [[(y * nz + z) * nt + t for y in range(ny)] for z in range(nz)]
+    return groups
+
+
+def swap(x, first):
+    return lax.all_to_all(
+        x, PLANE, split_axis=0, concat_axis=0, axis_index_groups=lines(first), tiled=True
+    )
 
 
 def dot(a, b, dims):
@@ -51,19 +65,45 @@
         attn_ref[:, cols] = dot(
             prob.astype(jnp.bfloat16), kv_ref[0, 1, :, cols], ((1,), (0,))
         ).astype(jnp.bfloat16)
-    first, second, rows, _ = part_ref.shape
+    side, _, rows, _ = part_ref.shape
     attn = attn_ref[...]
-    for j in range(second):
-        span = first * rows
-        part = dot(cot_ref[0, :, j * span : (j + 1) * span], attn, ((0,), (0,)))
-        for i in range(first):
-            part_ref[i, j] = part[i * rows : (i + 1) * rows].astype(jnp.bfloat16)
-
-
-def backward_kernel(q_ref, kv_ref, cot_ref, attn_ref, prob_ref, w_ref, gq_ref, gkv_ref):
+    odd = lax.axis_index("tensor") % 2 == 1
+    for y in range(side):
+        span = side * rows
+        part = dot(cot_ref[0, :, y * span : (y + 1) * span], attn, ((0,), (0,)))
+        for z in range(side):
+            block = part[z * rows : (z + 1) * rows].astype(jnp.bfloat16)
+            part_ref[jnp.where(odd, y, z), jnp.where(odd, z, y)] = block
+
+
+def backward_kernel(q_ref, kv_ref, cot_ref, attn_ref, prob_ref, w_ref, gq_ref, gkv_ref, rows_ref, sem):
     width = q_ref.shape[2]
     scale = 1.0 / HD**0.5
-    d_attn = dot(cot_ref[0], w_ref[...], ((1,), (0,))).astype(jnp.bfloat16)
+    side, _, rows, _ = w_ref.shape
+    odd = lax.axis_index("tensor") % 2 == 1
+    copies = [
+        [
+            pltpu.make_async_copy(
+                w_ref.at[:, y] if turned else w_ref.at[y], rows_ref.at[y], sem.at[y]
+            )
+            for y in range(side)
+        ]
+        for turned in range(2)
+    ]
+    for turned in range(2):
+
+        @pl.when(odd == (turned == 1))
+        def _(turned=turned):
+            for copy in copies[turned]:
+                copy.start()
+
+    d_attn = jnp.zeros((q_ref.shape[1], width), jnp.float32)
+    span = side * rows
+    for y in range(side):
+        copies[0][y].wait()
+        block = rows_ref[y].reshape(span, width)
+        d_attn += dot(cot_ref[0, :, y * span : (y + 1) * span], block, ((1,), (0,)))
+    d_attn = d_attn.astype(jnp.bfloat16)
     for h in range(width // HD):
         cols = slice(h * HD, (h + 1) * HD)
         da = d_attn[:, cols]
@@ -111,8 +151,8 @@
     params = pltpu.CompilerParams(vmem_limit_bytes=VMEM_LIMIT)
 
     used = from_behind(context, "segment", 1)
-    near = swap(jnp.broadcast_to(w_out, (nz, rows, width)), "z")
-    weight = swap(jnp.broadcast_to(near[None], (ny, nz, rows, width)), "y").reshape(model, width)
+    near = swap(jnp.broadcast_to(w_out, (nz, rows, width)), True)
+    weight = swap(jnp.broadcast_to(near[None], (ny, nz, rows, width)), False)
 
     attn, prob, part = pl.pallas_call(
         forward_kernel,
@@ -130,8 +170,8 @@
         ),
     )(vis_blocks, vis_count, queries, used, grad_out)
 
-    over_z = fold(swap(part, "z"), jnp.bfloat16)
-    grad_weight = fold(swap(over_z, "y"), jnp.float32)[None]
+    once = fold(swap(part, True), jnp.bfloat16)
+    grad_weight = fold(swap(once, False), jnp.float32)[None]
 
     grad_q, grad_used = pl.pallas_call(
         backward_kernel,
@@ -140,8 +180,12 @@
             jax.ShapeDtypeStruct(queries.shape, jnp.bfloat16),
             jax.ShapeDtypeStruct(context.shape, jnp.bfloat16),
         ),
-        in_specs=[vmem] * 6,
+        in_specs=[vmem] * 5 + [pl.BlockSpec(memory_space=pl.ANY)],
         out_specs=(vmem, vmem),
+        scratch_shapes=[
+            pltpu.VMEM((ny, nz, rows, width), jnp.bfloat16),
+            pltpu.SemaphoreType.DMA((ny,)),
+        ],
         compiler_params=params,
         cost_estimate=pl.CostEstimate(
             flops=2 * tokens * width * (4 * ctx + model), bytes_accessed=4 << 20, transcendentals=0

time: 115 us -> 94.6 us (0.82)
  waiting for transfers between devices: 42 us -> 19.8 us
  Pallas kernels: 6.5 us -> 8.62 us
    all_to_all x2, waiting for transfers between devices: 35.7 us -> 13.1 us  [swap(): lax.all_to_all(x, PLANE, split_axis=0, concat_axis=0, axis_index_groups=l...]
    pallas_call x1, Pallas kernels: 2.28 us -> 4.39 us  [shards(): pl.pallas_call(backward_kernel, name='backward', out_shape=(jax.ShapeDtyp...]
  transfers between devices with their start and end apart: 4 -> 4, of which waited for: 3 -> 3; matrix products, arithmetic and copies ran while one was open for 0% -> 0% of each run, Pallas kernels for 6% -> 9%
where the time goes in v2:
time: 94.6 us; the launch traced here: 93.4 us
  blocking collectives  37.4 us (40%)
  waiting for transfers between devices  19.8 us (21%)
  starting transfers between devices  19.7 us (21%)
  Pallas kernels  8.62 us (9%)
  local copies, waits for them, and re-layouts  7.21 us (8%)
    all_to_all x2, blocking collectives, swap(): lax.all_to_all(x, PLANE, split_axis=0, concat_axis=0, axis_index_groups=l...  37.4 us
    all_to_all x2, waiting for transfers between devices, swap(): lax.all_to_all(x, PLANE, split_axis=0, concat_axis=0, axis_index_groups=l...  13.1 us
    all_to_all x2, starting transfers between devices, swap(): lax.all_to_all(x, PLANE, split_axis=0, concat_axis=0, axis_index_groups=l...  11.3 us
    ppermute x2, starting transfers between devices, from_behind(): return lax.ppermute(x, axis, [(i, (i + by) % count) for i in range(count)])  8.42 us
    ppermute x2, waiting for transfers between devices, from_behind(): return lax.ppermute(x, axis, [(i, (i + by) % count) for i in range(count)])  6.65 us
    unnamed x21, local copies, waits for them, and re-layouts  5.3 us
    pallas_call x1, Pallas kernels, shards(): pl.pallas_call(backward_kernel, name='backward', out_shape=(jax.ShapeDtyp...  4.39 us
    pallas_call x1, Pallas kernels, shards(): pl.pallas_call(forward_kernel, name='forward', out_shape=(jax.ShapeDtypeS...  3.43 us
  transfers between devices with their start and end apart: 4, of which 3 were waited for; matrix products, arithmetic and copies ran while one was open for 0% of the time, Pallas kernels for 9%

profile of v2, /device:TPU:14, one launch (start us, length us, event | category | flops | bytes accessed | tf_op | source)
XLA Modules:
  0.0 93.4 jit_solution(10885300122211844467)
XLA Ops:
  0.6 0.7 broadcast_in_dim.17
  1.4 25.7 %all_to_all.20 = bf16[8,24,384]{2,1,0:T(8,128)(2,1)S(1)} all-to-all(bf16[8,24,384]{2,1,0:T(8,128)(2,1)S(1)} %broadcast_in_dim.17), channel_id=1, replica_groups={{0,4,8,12,16,20,24,28},{32,36,40,44,48,52,56,60},{64,68,72,76,80,84,88,..., dimensions={0} | all-to-all | bytes 294912 | tf_op jit(solution)/shard_map/all_to_all | solution.py:32
  27.1 1.2 %broadcast_in_dim.18 = bf16[8,8,24,384]{3,2,1,0:T(8,128)(2,1)} broadcast(bf16[8,24,384]{2,1,0:T(8,128)(2,1)S(1)} %all_to_all.20), dimensions={1,2,3} | broadcast | bytes 1327104 | tf_op jit(solution)/shard_map/broadcast_in_dim | solution.py:155
  28.3 0.0 copy-start.9
  28.3 0.0 copy-start.3
  28.3 0.0 copy-start.7
  28.3 0.0 copy-start.8
  28.3 7.7 %all-to-all-start.1 = ((bf16[8,8,24,384]{3,2,1,0:T(8,128)(2,1)}), bf16[8,8,24,384]{3,2,1,0:T(8,128)(2,1)S(1)}, u32[]{:S(2)}, u32[]{:S(2)}) async-start(bf16[8,8,24,384]{3,2,1,0:T(8,128)(2,1)} %broadcast_in_dim.18), calls=%async_computation.1 | async-start | bytes 2359296 | tf_op jit(solution)/shard_map/all_to_all | solution.py:32
  36.0 0.0 copy-done.9
  36.0 5.1 %collective-permute-start = (bf16[1,2,256,384]{3,2,1,0:T(8,128)(2,1)S(1)}, bf16[1,2,256,384]{3,2,1,0:T(8,128)(2,1)S(1)}, u32[]{:S(2)}, u32[]{:S(2)}) collective-permute-start(bf16[1,2,256,384]{3,2,1,0:T(8,128)(2,1)S(1)} %copy-done.9), channel_id=1, source_target_pairs={{0,256},{256,512},{512,768},{768,0},{1,257},{257,513},{513,769},{7... | collective-permute-start | bytes 1179656 | tf_op jit(solution)/shard_map/ppermute | solution.py:17
  41.1 6.6 %collective-permute-done.kv_ref = bf16[1,2,256,384]{3,2,1,0:T(8,128)(2,1)S(1)} collective-permute-done((bf16[1,2,256,384]{3,2,1,0:T(8,128)(2,1)S(1)}, bf16[1,2,256,384]{3,2,1,0:T(8,128)(2,1)S(1)}, u32[]{:S(2)}, u32[]{:S(2)}) %collective-permute-start) | collective-permute-done | bytes 393248 | tf_op jit(solution)/shard_map/ppermute | solution.py:17
  47.8 0.0 copy-done
  47.8 0.0 copy-done.3
  47.8 0.0 copy-done.7
  47.8 0.0 copy-done.8
  47.8 3.4 %forward.1 = (bf16[256,384]{1,0:T(8,128)(2,1)S(1)}, f32[3,256,256]{2,1,0:T(8,128)S(1)}, bf16[8,8,24,384]{3,2,1,0:T(8,128)(2,1)}) custom-call(s32[1,2,2]{2,1,0:T(2,128)S(1)} %copy-done.7, s32[1,2]{1,0:T(1,128)S(1)} %copy-done.8, bf16[1,256,384]{2,1,0:T(8,128)(2,1)S(1)} %copy-done.3, bf16[1,2,256,384]{3,2,1,0:T(8,128)(2,1)S(1)} %collective-permute-done.kv_ref, ...), custom_call_target="tpu_custom_call" | custom-call | flops 402653184 | bytes 4194304 | tf_op jit(solution)/shard_map/forward/pallas_call | solution.py:157
  51.2 0.9 copy-done.1
  52.1 0.7 copy-done.5
  52.8 3.6 %all-to-all-done.1.w_ref = bf16[8,8,24,384]{3,2,1,0:T(8,128)(2,1)S(1)} async-done(((bf16[8,8,24,384]{3,2,1,0:T(8,128)(2,1)}), bf16[8,8,24,384]{3,2,1,0:T(8,128)(2,1)S(1)}, u32[]{:S(2)}, u32[]{:S(2)}) %all-to-all-start.1) | async-done | bytes 1179680 | tf_op jit(solution)/shard_map/all_to_all | solution.py:32
  56.4 3.6 %all-to-all-start.2 = ((bf16[8,8,24,384]{3,2,1,0:T(8,128)(2,1)}), bf16[8,8,24,384]{3,2,1,0:T(8,128)(2,1)S(1)}, u32[]{:S(2)}, u32[]{:S(2)}) async-start(bf16[8,8,24,384]{3,2,1,0:T(8,128)(2,1)} %get-tuple-element.12), calls=%async_computation.2 | async-start | bytes 2359296 | tf_op jit(solution)/shard_map/all_to_all | solution.py:32
  59.9 0.0 copy-start.2
  59.9 1.1 %copy-done.2 = f32[3,256,256]{2,1,0:T(8,128)S(1)} copy-done((f32[3,256,256]{2,1,0:T(8,128)S(1)}, f32[3,256,256]{2,1,0:T(8,128)}, u32[]{:S(2)}) %copy-start.2) | copy-done | bytes 786456
  61.1 0.9 copy-done.4
  62.0 0.9 copy-done.6
  62.9 4.4 %backward.1 = (bf16[1,256,384]{2,1,0:T(8,128)(2,1)}, bf16[1,2,256,384]{3,2,1,0:T(8,128)(2,1)}) custom-call(bf16[1,256,384]{2,1,0:T(8,128)(2,1)S(1)} %copy-done.4, bf16[1,2,256,384]{3,2,1,0:T(8,128)(2,1)S(1)} %collective-permute-done.kv_ref, bf16[1,256,1536]{2,1,0:T(8,128)(2,1)S(1)} %copy-done, bf16[256,384]{1,0:T(8,128)(2,1)S(1)} %copy-done.6, ...), custom_call_target="tpu_custom_call" | custom-call | flops 503316480 | bytes 4194304 | tf_op jit(solution)/shard_map/backward/pallas_call | solution.py:176
  67.3 3.3 %collective-permute-start.1 = (bf16[1,2,256,384]{3,2,1,0:T(8,128)(2,1)}, bf16[1,2,256,384]{3,2,1,0:T(8,128)(2,1)S(1)}, u32[]{:S(2)}, u32[]{:S(2)}) collective-permute-start(bf16[1,2,256,384]{3,2,1,0:T(8,128)(2,1)} %get-tuple-element.11), channel_id=1, source_target_pairs={{0,768},{256,0},{512,256},{768,512},{1,769},{257,1},{513,257},{769... | collective-permute-start | bytes 1179656 | tf_op jit(solution)/shard_map/ppermute | solution.py:17
  70.7 9.5 %all-to-all-done.2.parts_ref = bf16[8,8,24,384]{3,2,1,0:T(8,128)(2,1)S(1)} async-done(((bf16[8,8,24,384]{3,2,1,0:T(8,128)(2,1)}), bf16[8,8,24,384]{3,2,1,0:T(8,128)(2,1)S(1)}, u32[]{:S(2)}, u32[]{:S(2)}) %all-to-all-start.2) | async-done | bytes 1179680 | tf_op jit(solution)/shard_map/all_to_all | solution.py:32
  80.2 0.2 fold.2
  80.4 11.6 %all_to_all.21.parts_ref = bf16[8,24,384]{2,1,0:T(8,128)(2,1)S(1)} all-to-all(bf16[8,24,384]{2,1,0:T(8,128)(2,1)S(1)} %fold.2), channel_id=1, replica_groups={{0,32,64,96,128,160,192,224},{4,36,68,100,132,164,196,228},{8,40,72,104..., dimensions={0} | all-to-all | bytes 294912 | tf_op jit(solution)/shard_map/all_to_all | solution.py:32
  92.0 0.6 fold.3
  92.6 0.0 collective-permute-done.1
  92.7 0.7 copy.10
  (5 shorter events, 0.0 us)
Async XLA Ops:
  28.3 7.7 %copy-start.9 = (bf16[1,2,256,384]{3,2,1,0:T(8,128)(2,1)S(1)}, bf16[1,2,256,384]{3,2,1,0:T(8,128)(2,1)}, u32[]{:S(2)}) copy-start(bf16[1,2,256,384]{3,2,1,0:T(8,128)(2,1)} %param.7) | copy-start | bytes 1179652
  28.3 19.5 %copy-start = (bf16[1,256,1536]{2,1,0:T(8,128)(2,1)S(1)}, bf16[1,256,1536]{2,1,0:T(8,128)(2,1)}, u32[]{:S(2)}) copy-start(bf16[1,256,1536]{2,1,0:T(8,128)(2,1)} %cot_ref.3) | copy-start | bytes 2359300
  28.3 19.5 %copy-start.3 = (bf16[1,256,384]{2,1,0:T(8,128)(2,1)S(1)}, bf16[1,256,384]{2,1,0:T(8,128)(2,1)}, u32[]{:S(2)}) copy-start(bf16[1,256,384]{2,1,0:T(8,128)(2,1)} %q_ref.3) | copy-start | bytes 589828
  28.3 19.5 %copy-start.7 = (s32[1,2,2]{2,1,0:T(2,128)S(1)}, s32[1,2,2]{2,1,0:T(2,128)}, u32[]{:S(2)}) copy-start(s32[1,2,2]{2,1,0:T(2,128)} %ids_ref.1) | copy-start | bytes 52
  28.3 19.5 %copy-start.8 = (s32[1,2]{1,0:T(1,128)S(1)}, s32[1,2]{1,0:T(1,128)}, u32[]{:S(2)}) copy-start(s32[1,2]{1,0:T(1,128)} %cnt_ref.1) | copy-start | bytes 28
  28.3 28.1 %all-to-all-start.1 = ((bf16[8,8,24,384]{3,2,1,0:T(8,128)(2,1)}), bf16[8,8,24,384]{3,2,1,0:T(8,128)(2,1)S(1)}, u32[]{:S(2)}, u32[]{:S(2)}) async-start(bf16[8,8,24,384]{3,2,1,0:T(8,128)(2,1)} %broadcast_in_dim.18), calls=%async_computation.1 | async-start | bytes 2359296 | tf_op jit(solution)/shard_map/all_to_all | solution.py:32
  36.0 11.7 %collective-permute-start = (bf16[1,2,256,384]{3,2,1,0:T(8,128)(2,1)S(1)}, bf16[1,2,256,384]{3,2,1,0:T(8,128)(2,1)S(1)}, u32[]{:S(2)}, u32[]{:S(2)}) collective-permute-start(bf16[1,2,256,384]{3,2,1,0:T(8,128)(2,1)S(1)} %copy-done.9), channel_id=1, source_target_pairs={{0,256},{256,512},{512,768},{768,0},{1,257},{257,513},{513,769},{7... | collective-permute-start | bytes 1179656 | tf_op jit(solution)/shard_map/ppermute | solution.py:17
  51.2 0.9 copy-start.1
  52.1 0.7 copy-start.5
  56.4 23.8 %all-to-all-start.2 = ((bf16[8,8,24,384]{3,2,1,0:T(8,128)(2,1)}), bf16[8,8,24,384]{3,2,1,0:T(8,128)(2,1)S(1)}, u32[]{:S(2)}, u32[]{:S(2)}) async-start(bf16[8,8,24,384]{3,2,1,0:T(8,128)(2,1)} %get-tuple-element.12), calls=%async_computation.2 | async-start | bytes 2359296 | tf_op jit(solution)/shard_map/all_to_all | solution.py:32
  59.9 1.1 %copy-start.2 = (f32[3,256,256]{2,1,0:T(8,128)S(1)}, f32[3,256,256]{2,1,0:T(8,128)}, u32[]{:S(2)}) copy-start(f32[3,256,256]{2,1,0:T(8,128)} %copy-done.1) | copy-start | bytes 2359300
  61.1 0.9 copy-start.4
  62.0 0.9 copy-start.6
  67.3 25.3 %collective-permute-start.1 = (bf16[1,2,256,384]{3,2,1,0:T(8,128)(2,1)}, bf16[1,2,256,384]{3,2,1,0:T(8,128)(2,1)S(1)}, u32[]{:S(2)}, u32[]{:S(2)}) collective-permute-start(bf16[1,2,256,384]{3,2,1,0:T(8,128)(2,1)} %get-tuple-element.11), channel_id=1, source_target_pairs={{0,768},{256,0},{512,256},{768,512},{1,769},{257,1},{513,257},{769... | collective-permute-start | bytes 1179656 | tf_op jit(solution)/shard_map/ppermute | solution.py:17

commit v3 on v2

--- a/solution.py
+++ b/solution.py
@@ -152,7 +152,7 @@
 
     used = from_behind(context, "segment", 1)
     near = swap(jnp.broadcast_to(w_out, (nz, rows, width)), True)
-    weight = swap(jnp.broadcast_to(near[None], (ny, nz, rows, width)), False)
+    weight = lax.all_gather(near, PLANE, axis=0, axis_index_groups=lines(False))
 
     attn, prob, part = pl.pallas_call(
         forward_kernel,

time: 94.6 us -> 110 us (1.16)
  blocking collectives: 37.4 us -> 14.3 us
  starting transfers between devices: 19.7 us -> 34 us
  between operations: 0.7 us -> 14.1 us
  waiting for transfers between devices: 19.8 us -> 29.5 us
    all_gather x0 -> x1, waiting for transfers between devices: none -> 24.6 us  [shards(): weight = lax.all_gather(near, PLANE, axis=0, axis_index_groups=lines(False))]
    all_to_all x2 -> x1, blocking collectives: 37.4 us -> 14.3 us  [swap(): lax.all_to_all(x, PLANE, split_axis=0, concat_axis=0, axis_index_groups=l...]
    all_to_all x2, starting transfers between devices: 11.3 us -> 26.2 us  [swap(): lax.all_to_all(x, PLANE, split_axis=0, concat_axis=0, axis_index_groups=l...]
    all_to_all x2, waiting for transfers between devices: 13.1 us -> 4.12 us  [swap(): lax.all_to_all(x, PLANE, split_axis=0, concat_axis=0, axis_index_groups=l...]
    ppermute x2, waiting for transfers between devices: 6.65 us -> 0.79 us  [from_behind(): return lax.ppermute(x, axis, [(i, (i + by) % count) for i in range(count)])]
    broadcast_in_dim x1 -> x0, local copies, waits for them, and re-layouts: 1.17 us -> none  [shards(): weight = swap(jnp.broadcast_to(near[None], (ny, nz, rows, width)), False)]
    unnamed x21 -> x17, local copies, waits for them, and re-layouts: 5.3 us -> 6.08 us
  transfers between devices with their start and end apart: 4 -> 5, of which waited for: 3 -> 3; matrix products, arithmetic and copies ran while one was open for 0% -> 0% of each run, Pallas kernels for 9% -> 8%
where the time goes in v3:
time: 110 us; the launch traced here: 108 us
  starting transfers between devices  34 us (31%)
  waiting for transfers between devices  29.5 us (27%)
  blocking collectives  14.3 us (13%)
  between operations  14.1 us (13%)
  Pallas kernels  8.59 us (8%)
  local copies, waits for them, and re-layouts  7.47 us (7%)
    all_to_all x2, starting transfers between devices, swap(): lax.all_to_all(x, PLANE, split_axis=0, concat_axis=0, axis_index_groups=l...  26.2 us
    all_gather x1, waiting for transfers between devices, shards(): weight = lax.all_gather(near, PLANE, axis=0, axis_index_groups=lines(False))  24.6 us
    all_to_all x1, blocking collectives, swap(): lax.all_to_all(x, PLANE, split_axis=0, concat_axis=0, axis_index_groups=l...  14.3 us
    ppermute x2, starting transfers between devices, from_behind(): return lax.ppermute(x, axis, [(i, (i + by) % count) for i in range(count)])  7.69 us
    unnamed x17, local copies, waits for them, and re-layouts  6.08 us
    pallas_call x1, Pallas kernels, shards(): pl.pallas_call(backward_kernel, name='backward', out_shape=(jax.ShapeDtyp...  4.39 us
    all_to_all x2, waiting for transfers between devices, swap(): lax.all_to_all(x, PLANE, split_axis=0, concat_axis=0, axis_index_groups=l...  4.12 us
    pallas_call x1, Pallas kernels, shards(): pl.pallas_call(forward_kernel, name='forward', out_shape=(jax.ShapeDtypeS...  3.4 us
  transfers between devices with their start and end apart: 5, of which 3 were waited for; matrix products, arithmetic and copies ran while one was open for 0% of the time, Pallas kernels for 8%

profile of v3, /device:TPU:14, one launch (start us, length us, event | category | flops | bytes accessed | tf_op | source)
XLA Modules:
  0.0 107.9 jit_solution(6080382606381779203)
XLA Ops:
  7.2 1.4 %broadcast_in_dim.11 = bf16[8,24,384]{2,1,0:T(8,128)(2,1)} broadcast(bf16[24,384]{1,0:T(8,128)(2,1)} %bitcast.5), dimensions={1,2} | broadcast | bytes 165888 | tf_op jit(solution)/shard_map/broadcast_in_dim | solution.py:154
  8.6 16.7 %all-to-all-start = ((bf16[8,24,384]{2,1,0:T(8,128)(2,1)}), bf16[8,24,384]{2,1,0:T(8,128)(2,1)S(1)}, u32[]{:S(2)}, u32[]{:S(2)}) async-start(bf16[8,24,384]{2,1,0:T(8,128)(2,1)} %broadcast_in_dim.11), calls=%async_computation | async-start | bytes 294912 | tf_op jit(solution)/shard_map/all_to_all | solution.py:32
  25.2 0.0 all-gather.3.cloned.1.call-start
  25.3 5.1 %collective-permute-start = (bf16[1,2,256,384]{3,2,1,0:T(8,128)(2,1)}, bf16[1,2,256,384]{3,2,1,0:T(8,128)(2,1)S(1)}, u32[]{:S(2)}, u32[]{:S(2)}) collective-permute-start(bf16[1,2,256,384]{3,2,1,0:T(8,128)(2,1)} %param.7), channel_id=1, source_target_pairs={{0,256},{256,512},{512,768},{768,0},{1,257},{257,513},{513,769},{7... | collective-permute-start | bytes 1179656 | tf_op jit(solution)/shard_map/ppermute | solution.py:17
  30.4 4.1 %all-to-all-done = bf16[8,24,384]{2,1,0:T(8,128)(2,1)S(1)} async-done(((bf16[8,24,384]{2,1,0:T(8,128)(2,1)}), bf16[8,24,384]{2,1,0:T(8,128)(2,1)S(1)}, u32[]{:S(2)}, u32[]{:S(2)}) %all-to-all-start) | async-done | bytes 147488 | tf_op jit(solution)/shard_map/all_to_all | solution.py:32
  34.5 0.0 copy-start.7
  34.5 0.7 copy-done.7
  35.2 0.0 all-gather.3.cloned.1.call-update
  35.2 0.8 collective-permute-done.kv_ref
  36.0 0.0 copy-start.1
  36.0 1.1 %copy-done.1 = bf16[1,256,1536]{2,1,0:T(8,128)(2,1)S(1)} copy-done((bf16[1,256,1536]{2,1,0:T(8,128)(2,1)S(1)}, bf16[1,256,1536]{2,1,0:T(8,128)(2,1)}, u32[]{:S(2)}) %copy-start.1) | copy-done | bytes 786456
  37.1 0.0 copy-start.3
  37.1 0.9 copy-done.3
  38.0 0.0 copy-start.5
  38.0 0.7 copy-done.5
  38.7 0.0 copy-start.6
  38.7 0.7 copy-done.6
  39.4 3.4 %forward.1 = (bf16[256,384]{1,0:T(8,128)(2,1)S(1)}, f32[3,256,256]{2,1,0:T(8,128)S(1)}, bf16[8,8,24,384]{3,2,1,0:T(8,128)(2,1)}) custom-call(s32[1,2,2]{2,1,0:T(2,128)S(1)} %copy-done.5, s32[1,2]{1,0:T(1,128)S(1)} %copy-done.6, bf16[1,256,384]{2,1,0:T(8,128)(2,1)S(1)} %copy-done.3, bf16[1,2,256,384]{3,2,1,0:T(8,128)(2,1)S(1)} %collective-permute-done.kv_ref, ...), custom_call_target="tpu_custom_call" | custom-call | flops 402653184 | bytes 4194304 | tf_op jit(solution)/shard_map/forward/pallas_call | solution.py:157
  42.8 0.0 copy-start.2
  42.8 9.6 %all-to-all-start.1 = ((bf16[8,8,24,384]{3,2,1,0:T(8,128)(2,1)}), bf16[8,8,24,384]{3,2,1,0:T(8,128)(2,1)S(1)}, u32[]{:S(2)}, u32[]{:S(2)}) async-start(bf16[8,8,24,384]{3,2,1,0:T(8,128)(2,1)} %get-tuple-element.12), calls=%async_computation.1 | async-start | bytes 2359296 | tf_op jit(solution)/shard_map/all_to_all | solution.py:32
  52.3 24.6 %all-gather.3.cloned.1.call-done = bf16[64,24,384]{2,1,0:T(8,128)(2,1)} async-done(((bf16[8,24,384]{2,1,0:T(8,128)(2,1)}), bf16[64,24,384]{2,1,0:T(8,128)(2,1)}) %all-gather.3.cloned.1.call-update) | async-done | bytes 1179664 | tf_op jit(solution)/shard_map/all_gather | solution.py:155
  76.9 0.0 copy-done.2
  76.9 0.0 copy-done.4
  76.9 1.3 %copy-done = bf16[64,24,384]{2,1,0:T(8,128)(2,1)S(1)} copy-done((bf16[64,24,384]{2,1,0:T(8,128)(2,1)S(1)}, bf16[64,24,384]{2,1,0:T(8,128)(2,1)}, u32[]{:S(2)}) %copy-start) | copy-done | bytes 1179672
  78.2 4.4 %backward.1 = (bf16[1,256,384]{2,1,0:T(8,128)(2,1)}, bf16[1,2,256,384]{3,2,1,0:T(8,128)(2,1)}) custom-call(bf16[1,256,384]{2,1,0:T(8,128)(2,1)S(1)} %copy-done.4, bf16[1,2,256,384]{3,2,1,0:T(8,128)(2,1)S(1)} %collective-permute-done.kv_ref, bf16[1,256,1536]{2,1,0:T(8,128)(2,1)S(1)} %copy-done.2, bf16[256,384]{1,0:T(8,128)(2,1)S(1)} %get-tuple-element.8.attn_ref, ...), custom_call_target="tpu_custom_call" | custom-call | flops 503316480 | bytes 4194304 | tf_op jit(solution)/shard_map/backward/pallas_call | solution.py:176
  82.6 2.6 %collective-permute-start.1 = (bf16[1,2,256,384]{3,2,1,0:T(8,128)(2,1)}, bf16[1,2,256,384]{3,2,1,0:T(8,128)(2,1)S(1)}, u32[]{:S(2)}, u32[]{:S(2)}) collective-permute-start(bf16[1,2,256,384]{3,2,1,0:T(8,128)(2,1)} %get-tuple-element.11), channel_id=1, source_target_pairs={{0,768},{256,0},{512,256},{768,512},{1,769},{257,1},{513,257},{769... | collective-permute-start | bytes 1179656 | tf_op jit(solution)/shard_map/ppermute | solution.py:17
  85.2 0.0 all-to-all-done.1.parts_ref
  85.2 0.2 fold.2
  85.4 14.3 %all_to_all.15.parts_ref = bf16[8,24,384]{2,1,0:T(8,128)(2,1)S(1)} all-to-all(bf16[8,24,384]{2,1,0:T(8,128)(2,1)S(1)} %fold.2), channel_id=1, replica_groups={{0,32,64,96,128,160,192,224},{4,36,68,100,132,164,196,228},{8,40,72,104..., dimensions={0} | all-to-all | bytes 294912 | tf_op jit(solution)/shard_map/all_to_all | solution.py:32
  99.7 0.6 fold.3
  100.3 0.0 collective-permute-done.1
  100.3 0.7 copy.10
  (2 shorter events, 0.0 us)
Async XLA Ops:
  8.6 25.9 %all-to-all-start = ((bf16[8,24,384]{2,1,0:T(8,128)(2,1)}), bf16[8,24,384]{2,1,0:T(8,128)(2,1)S(1)}, u32[]{:S(2)}, u32[]{:S(2)}) async-start(bf16[8,24,384]{2,1,0:T(8,128)(2,1)} %broadcast_in_dim.11), calls=%async_computation | async-start | bytes 294912 | tf_op jit(solution)/shard_map/all_to_all | solution.py:32
  25.2 51.7 %all-gather.3.cloned.1.call-start = ((), (), s32[]{:S(2)}) async-start(), calls=%async_computation.3 | async-start | bytes 1327104 | tf_op jit(solution)/shard_map/all_gather | solution.py:155
  25.3 10.7 %collective-permute-start = (bf16[1,2,256,384]{3,2,1,0:T(8,128)(2,1)}, bf16[1,2,256,384]{3,2,1,0:T(8,128)(2,1)S(1)}, u32[]{:S(2)}, u32[]{:S(2)}) collective-permute-start(bf16[1,2,256,384]{3,2,1,0:T(8,128)(2,1)} %param.7), channel_id=1, source_target_pairs={{0,256},{256,512},{512,768},{768,0},{1,257},{257,513},{513,769},{7... | collective-permute-start | bytes 1179656 | tf_op jit(solution)/shard_map/ppermute | solution.py:17
  34.5 0.7 copy-start.7
  36.0 1.1 %copy-start.1 = (bf16[1,256,1536]{2,1,0:T(8,128)(2,1)S(1)}, bf16[1,256,1536]{2,1,0:T(8,128)(2,1)}, u32[]{:S(2)}) copy-start(bf16[1,256,1536]{2,1,0:T(8,128)(2,1)} %cot_ref.3) | copy-start | bytes 2359300
  37.1 0.9 copy-start.3
  38.0 0.7 copy-start.5
  38.7 0.7 copy-start.6
  42.8 34.1 %copy-start.2 = (bf16[1,256,1536]{2,1,0:T(8,128)(2,1)S(1)}, bf16[1,256,1536]{2,1,0:T(8,128)(2,1)}, u32[]{:S(2)}) copy-start(bf16[1,256,1536]{2,1,0:T(8,128)(2,1)} %cot_ref.3) | copy-start | bytes 2359300
  42.8 34.2 %copy-start.4 = (bf16[1,256,384]{2,1,0:T(8,128)(2,1)S(1)}, bf16[1,256,384]{2,1,0:T(8,128)(2,1)}, u32[]{:S(2)}) copy-start(bf16[1,256,384]{2,1,0:T(8,128)(2,1)} %q_ref.3) | copy-start | bytes 589828
  42.8 42.4 %all-to-all-start.1 = ((bf16[8,8,24,384]{3,2,1,0:T(8,128)(2,1)}), bf16[8,8,24,384]{3,2,1,0:T(8,128)(2,1)S(1)}, u32[]{:S(2)}, u32[]{:S(2)}) async-start(bf16[8,8,24,384]{3,2,1,0:T(8,128)(2,1)} %get-tuple-element.12), calls=%async_computation.1 | async-start | bytes 2359296 | tf_op jit(solution)/shard_map/all_to_all | solution.py:32
  76.9 1.3 %copy-start = (bf16[64,24,384]{2,1,0:T(8,128)(2,1)S(1)}, bf16[64,24,384]{2,1,0:T(8,128)(2,1)}, u32[]{:S(2)}) copy-start(bf16[64,24,384]{2,1,0:T(8,128)(2,1)} %all-gather.3.cloned.1.call-done) | copy-start | bytes 3538948
  82.6 17.7 %collective-permute-start.1 = (bf16[1,2,256,384]{3,2,1,0:T(8,128)(2,1)}, bf16[1,2,256,384]{3,2,1,0:T(8,128)(2,1)S(1)}, u32[]{:S(2)}, u32[]{:S(2)}) collective-permute-start(bf16[1,2,256,384]{3,2,1,0:T(8,128)(2,1)} %get-tuple-element.11), channel_id=1, source_target_pairs={{0,768},{256,0},{512,256},{768,512},{1,769},{257,1},{513,257},{769... | collective-permute-start | bytes 1179656 | tf_op jit(solution)/shard_map/ppermute | solution.py:17
Sparse Core Ops, SparseCore 0:
  35.3 41.5 all-gather.2

commit v4 on v3

v4 whole, which is shorter than its diff:
```python
import jax
import jax.numpy as jnp
from jax import lax
from jax.experimental import pallas as pl
from jax.experimental.pallas import tpu as pltpu
from jax.sharding import Mesh, PartitionSpec as P

HD = 128
BLK = 128
VMEM_LIMIT = 16 * 1024 * 1024
SCALE = 1.0 / HD**0.5
DP = ("y", "z")
PLANE = ("y", "z", "tensor")


def from_behind(x, axis, by):
    count = lax.axis_size(axis)
    return lax.ppermute(x, axis, [(i, (i + by) % count) for i in range(count)])


def lines(first):
    ny, nz, nt = (lax.axis_size(a) for a in PLANE)
    groups = []
    for t in range(nt):
        if (t % 2 == 0) == first:
            groups += [[(y * nz + z) * nt + t for z in range(nz)] for y in range(ny)]
        else:
            groups += [[(y * nz + z) * nt + t for y in range(ny)] for z in range(nz)]
    return groups


def swap(x, first):
    return lax.all_to_all(
        x, PLANE, split_axis=0, concat_axis=0, axis_index_groups=lines(first), tiled=True
    )


def mirror(x, distance):
    pairs = [(line[i], line[i ^ distance]) for line in lines(False) for i in range(len(line))]
    return lax.ppermute(x, PLANE, pairs)


def gather_slots(near):
    pieces = [(near[None], [0])]
    distance = len(lines(False)[0]) // 2
    while distance:
        if len(pieces) == 2 and distance > 1:
            pieces = [(jnp.concatenate([a for a, _ in pieces]), [s for _, k in pieces for s in k])]
        pieces += [(mirror(a, distance), [s ^ distance for s in k]) for a, k in pieces]
        distance //= 2
    return pieces


def dot(a, b, dims):
    return lax.dot_general(a, b, (dims, ((), ())), preferred_element_type=jnp.float32)


def live_mask(ids_ref, cnt_ref, tokens, ctx):
    row = lax.broadcasted_iota(jnp.int32, (tokens, ctx), 0) // BLK
    col = lax.broadcasted_iota(jnp.int32, (tokens, ctx), 1) // BLK
    live = None
    for b in range(tokens // BLK):
        for k in range(ids_ref.shape[2]):
            block = jnp.where(k < cnt_ref[0, b], ids_ref[0, b, k], -1)
            here = (row == b) & (col == block)
            live = here if live is None else live | here
    return live


def softmax(q, k, live):
    score = jnp.where(live, dot(q, k, ((1,), (1,))) * SCALE, jnp.float32(-1e30))
    expo = jnp.exp(score - jnp.max(score, axis=1, keepdims=True))
    return expo / jnp.sum(expo, axis=1, keepdims=True)


def forward_kernel(
    ids_hbm, cnt_hbm, q_hbm, kv_hbm, cot_hbm, part_ref, ids_ref, cnt_ref, q_ref, kv_ref, cot_ref, attn_ref, sem
):
    copies = [
        pltpu.make_async_copy(src, dst, sem.at[i])
        for i, (src, dst) in enumerate(
            [(ids_hbm, ids_ref), (cnt_hbm, cnt_ref), (q_hbm, q_ref), (kv_hbm, kv_ref), (cot_hbm, cot_ref)]
        )
    ]
    for copy in copies:
        copy.start()
    tokens, width = q_ref.shape[1:]
    for copy in copies[:4]:
        copy.wait()
    live = live_mask(ids_ref, cnt_ref, tokens, kv_ref.shape[2])
    for h in range(width // HD):
        cols = slice(h * HD, (h + 1) * HD)
        prob = softmax(q_ref[0, :, cols], kv_ref[0, 0, :, cols], live).astype(jnp.bfloat16)
        attn_ref[:, cols] = dot(prob, kv_ref[0, 1, :, cols], ((1,), (0,))).astype(jnp.bfloat16)
    copies[4].wait()
    side, _, rows, _ = part_ref.shape
    attn = attn_ref[...]
    odd = lax.axis_index("tensor") % 2 == 1
    for y in range(side):
        span = side * rows
        part = dot(cot_ref[0, :, y * span : (y + 1) * span], attn, ((0,), (0,)))
        for z in range(side):
            block = part[z * rows : (z + 1) * rows].astype(jnp.bfloat16)
            part_ref[jnp.where(odd, y, z), jnp.where(odd, z, y)] = block


def backward_kernel(slots, ids_hbm, cnt_hbm, q_hbm, kv_hbm, cot_hbm, *refs):
    pieces = refs[: len(slots)]
    gq_ref, gkv_ref, ids_ref, cnt_ref, q_ref, kv_ref, cot_ref, rows_ref, sem, slot_sem = refs[len(slots) :]
    copies = [
        pltpu.make_async_copy(src, dst, sem.at[i])
        for i, (src, dst) in enumerate(
            [(ids_hbm, ids_ref), (cnt_hbm, cnt_ref), (q_hbm, q_ref), (kv_hbm, kv_ref), (cot_hbm, cot_ref)]
        )
    ]
    for copy in copies:
        copy.start()
    odd = lax.axis_index("tensor") % 2 == 1
    placed = []
    for turned in range(2):
        place = lax.axis_index(DP[1] if turned else DP[0])
        moves = []
        for piece, held in zip(pieces, slots):
            for i, k in enumerate(held):
                at = place ^ k
                target = rows_ref.at[:, at] if turned else rows_ref.at[at]
                moves.append(pltpu.make_async_copy(piece.at[i], target, slot_sem.at[k]))
        placed.append(moves)

        @pl.when(odd == (turned == 1))
        def _(moves=moves):
            for move in moves:
                move.start()

    tokens, width = q_ref.shape[1:]
    for copy in copies[:4]:
        copy.wait()
    live = live_mask(ids_ref, cnt_ref, tokens, kv_ref.shape[2])
    side, _, rows, _ = rows_ref.shape
    probs = []
    attns = []
    for h in range(width // HD):
        cols = slice(h * HD, (h + 1) * HD)
        prob = softmax(q_ref[0, :, cols], kv_ref[0, 0, :, cols], live)
        probs.append(prob)
        attns.append(
            dot(prob.astype(jnp.bfloat16), kv_ref[0, 1, :, cols], ((1,), (0,))).astype(jnp.bfloat16)
        )
    copies[4].wait()
    for move in placed[0]:
        move.wait()
    weight = rows_ref[...].reshape(side * side * rows, width)
    d_attn = dot(cot_ref[0], weight, ((1,), (0,))).astype(jnp.bfloat16)
    for h in range(width // HD):
        cols = slice(h * HD, (h + 1) * HD)
        da = d_attn[:, cols]
        q, k, v = q_ref[0, :, cols], kv_ref[0, 0, :, cols], kv_ref[0, 1, :, cols]
        prob = probs[h]
        delta = jnp.sum(da.astype(jnp.float32) * attns[h].astype(jnp.float32), axis=1, keepdims=True)
        dprob = dot(da, v, ((1,), (1,)))
        dscore = (prob * (dprob - delta)).astype(jnp.bfloat16)
        gq_ref[0, :, cols] = (dot(dscore, k, ((1,), (0,))) * SCALE).astype(jnp.bfloat16)
        gkv_ref[0, 0, :, cols] = (dot(dscore, q, ((0,), (0,))) * SCALE).astype(jnp.bfloat16)
        gkv_ref[0, 1, :, cols] = dot(prob.astype(jnp.bfloat16), da, ((0,), (0,))).astype(jnp.bfloat16)


def fold_kernel(parts_ref, total_ref):
    total = parts_ref[0].astype(jnp.float32)
    for i in range(1, parts_ref.shape[0]):
        total += parts_ref[i].astype(jnp.float32)
    total_ref[...] = total.astype(total_ref.dtype)


def fold(parts, dtype):
    vmem = pl.BlockSpec(memory_space=pltpu.VMEM)
    return pl.pallas_call(
        fold_kernel,
        name="fold",
        out_shape=jax.ShapeDtypeStruct(parts.shape[1:], dtype),
        in_specs=[vmem],
        out_specs=vmem,
        compiler_params=pltpu.CompilerParams(vmem_limit_bytes=VMEM_LIMIT),
        cost_estimate=pl.CostEstimate(flops=parts.size, bytes_accessed=2 * parts.size, transcendentals=0),
    )(parts)


def shards(queries, context, vis_blocks, vis_count, w_out, grad_out):
    tokens, width = queries.shape[1:]
    ctx = context.shape[2]
    heads = width // HD
    model = grad_out.shape[2]
    ny, nz = (lax.axis_size(a) for a in DP)
    rows = w_out.shape[1]
    hbm = pl.BlockSpec(memory_space=pltpu.HBM)
    anywhere = pl.BlockSpec(memory_space=pl.ANY)
    vmem = pl.BlockSpec(memory_space=pltpu.VMEM)
    params = pltpu.CompilerParams(vmem_limit_bytes=VMEM_LIMIT)
    small = [
        pltpu.SMEM(vis_blocks.shape, jnp.int32),
        pltpu.SMEM(vis_count.shape, jnp.int32),
        pltpu.VMEM(queries.shape, jnp.bfloat16),
        pltpu.VMEM(context.shape, jnp.bfloat16),
        pltpu.VMEM(grad_out.shape, jnp.bfloat16),
    ]

    used = from_behind(context, "segment", 1)
    near = swap(jnp.broadcast_to(w_out, (nz, rows, width)), True)
    used, near = lax.optimization_barrier((used, near))
    fixed = [pltpu.with_memory_space_constraint(a, pltpu.HBM) for a in (vis_blocks, vis_count, queries)]
    cotan = pltpu.with_memory_space_constraint(grad_out, pltpu.HBM)

    part = pl.pallas_call(
        forward_kernel,
        name="forward",
        out_shape=jax.ShapeDtypeStruct((nz, ny, rows, width), jnp.bfloat16),
        in_specs=[hbm, hbm, hbm, anywhere, hbm],
        out_specs=vmem,
        scratch_shapes=small + [pltpu.VMEM((tokens, width), jnp.bfloat16), pltpu.SemaphoreType.DMA((5,))],
        compiler_params=params,
        cost_estimate=pl.CostEstimate(
            flops=2 * tokens * width * (2 * ctx + model), bytes_accessed=3 << 20, transcendentals=heads * tokens * ctx
        ),
    )(*fixed, used, cotan)

    once = fold(swap(part, True), jnp.bfloat16)
    grad_weight = fold(swap(once, False), jnp.float32)[None]

    pieces = gather_slots(near)
    slots = [k for _, k in pieces]
    grad_q, grad_used = pl.pallas_call(
        lambda *refs: backward_kernel(slots, *refs),
        name="backward",
        out_shape=(
            jax.ShapeDtypeStruct(queries.shape, jnp.bfloat16),
            jax.ShapeDtypeStruct(context.shape, jnp.bfloat16),
        ),
        in_specs=[hbm, hbm, hbm, anywhere, hbm] + [anywhere] * len(pieces),
        out_specs=(vmem, vmem),
        scratch_shapes=small
        + [
            pltpu.VMEM((ny, nz, rows, width), jnp.bfloat16),
            pltpu.SemaphoreType.DMA((5,)),
            pltpu.SemaphoreType.DMA((ny,)),
        ],
        compiler_params=params,
        cost_estimate=pl.CostEstimate(
            flops=2 * tokens * width * (6 * ctx + model), bytes_accessed=4 << 20, transcendentals=heads * tokens * ctx
        ),
    )(*fixed, used, cotan, *(a for a, _ in pieces))
    grad_context = from_behind(grad_used, "segment", -1)
    return grad_q, grad_context, grad_weight


def solution(mesh):
    fine = Mesh(mesh.devices.reshape(4, 8, 8, 4), ("segment", "y", "z", "tensor"))
    in_specs = (
        P("segment", DP, "tensor"),
        P("segment", None, DP, "tensor"),
        P("segment", DP, None),
        P("segment", DP),
        P("segment", DP, "tensor"),
        P("segment", DP, None),
    )
    out_specs = (
        P("segment", DP, "tensor"),
        P("segment", None, DP, "tensor"),
        P("segment", DP, "tensor"),
    )
    return jax.shard_map(shards, mesh=fine, in_specs=in_specs, out_specs=out_specs, check_vma=False)
```

time: 110 us -> 99.8 us (0.907)
  between operations: 14.1 us -> 0.72 us
  blocking collectives: 14.3 us -> 25.7 us
  local copies, waits for them, and re-layouts: 7.47 us -> 1.48 us
  waiting for transfers between devices: 29.5 us -> 25.8 us
  Pallas kernels: 8.59 us -> 10.5 us
    all_gather x1 -> x0, waiting for transfers between devices: 24.6 us -> none  [shards(): weight = lax.all_gather(near, PLANE, axis=0, axis_index_groups=lines(False))]
    ppermute x0 -> x4, starting transfers between devices: none -> 17 us  [mirror(): return lax.ppermute(x, PLANE, pairs)]
    ppermute x0 -> x4, waiting for transfers between devices: none -> 16.6 us  [mirror(): return lax.ppermute(x, PLANE, pairs)]
    all_to_all x2, starting transfers between devices: 26.2 us -> 10.3 us  [swap(): lax.all_to_all(x, PLANE, split_axis=0, concat_axis=0, axis_index_groups=l...]
    all_to_all x1, blocking collectives: 14.3 us -> 25.7 us  [swap(): lax.all_to_all(x, PLANE, split_axis=0, concat_axis=0, axis_index_groups=l...]
    unnamed x17 -> x1, local copies, waits for them, and re-layouts: 6.08 us -> 0.75 us
    ppermute x2, waiting for transfers between devices: 0.79 us -> 5.78 us  [from_behind(): return lax.ppermute(x, axis, [(i, (i + by) % count) for i in range(count)])]
    pallas_call x2, Pallas kernels: 7.79 us -> 9.09 us  [the longest x1 5.05 us: shards(): pl.pallas_call(lambda *refs: backward_kernel(slots, *refs), name='backwar...]
  transfers between devices with their start and end apart: 5 -> 8, of which waited for: 3 -> 6; matrix products, arithmetic and copies ran while one was open for 0% -> 1% of each run, Pallas kernels for 8% -> 6%
where the time goes in v4:
time: 99.8 us; the launch traced here: 98.6 us
  starting transfers between devices  34.3 us (34%)
  waiting for transfers between devices  25.8 us (26%)
  blocking collectives  25.7 us (26%)
  Pallas kernels  10.5 us (11%)
  local copies, waits for them, and re-layouts  1.48 us (1%)
    all_to_all x1, blocking collectives, swap(): lax.all_to_all(x, PLANE, split_axis=0, concat_axis=0, axis_index_groups=l...  25.7 us
    ppermute x4, starting transfers between devices, mirror(): return lax.ppermute(x, PLANE, pairs)  17 us
    ppermute x4, waiting for transfers between devices, mirror(): return lax.ppermute(x, PLANE, pairs)  16.6 us
    all_to_all x2, starting transfers between devices, swap(): lax.all_to_all(x, PLANE, split_axis=0, concat_axis=0, axis_index_groups=l...  10.3 us
    ppermute x2, starting transfers between devices, from_behind(): return lax.ppermute(x, axis, [(i, (i + by) % count) for i in range(count)])  7 us
    ppermute x2, waiting for transfers between devices, from_behind(): return lax.ppermute(x, axis, [(i, (i + by) % count) for i in range(count)])  5.78 us
    pallas_call x1, Pallas kernels, shards(): pl.pallas_call(lambda *refs: backward_kernel(slots, *refs), name='backwar...  5.05 us
    pallas_call x1, Pallas kernels, shards(): pl.pallas_call(forward_kernel, name='forward', out_shape=jax.ShapeDtypeSt...  4.04 us
  transfers between devices with their start and end apart: 8, of which 6 were waited for; matrix products, arithmetic and copies ran while one was open for 1% of the time, Pallas kernels for 6%

profile of v4, /device:TPU:14, one launch (start us, length us, event | category | flops | bytes accessed | tf_op | source)
XLA Modules:
  0.0 98.6 jit_solution(8898789925487070759)
XLA Ops:
  0.6 5.1 %collective-permute-start = (bf16[1,2,256,384]{3,2,1,0:T(8,128)(2,1)}, bf16[1,2,256,384]{3,2,1,0:T(8,128)(2,1)S(1)}, u32[]{:S(2)}, u32[]{:S(2)}) collective-permute-start(bf16[1,2,256,384]{3,2,1,0:T(8,128)(2,1)} %param.7), channel_id=1, source_target_pairs={{0,256},{256,512},{512,768},{768,0},{1,257},{257,513},{513,769},{7... | collective-permute-start | bytes 1179656 | tf_op jit(solution)/shard_map/ppermute | solution.py:18
  5.7 0.7 broadcast_in_dim.14
  6.5 25.7 %all_to_all.15 = bf16[8,24,384]{2,1,0:T(8,128)(2,1)S(1)} all-to-all(bf16[8,24,384]{2,1,0:T(8,128)(2,1)S(1)} %broadcast_in_dim.14), channel_id=1, replica_groups={{0,4,8,12,16,20,24,28},{32,36,40,44,48,52,56,60},{64,68,72,76,80,84,88,..., dimensions={0} | all-to-all | bytes 294912 | tf_op jit(solution)/shard_map/all_to_all | solution.py:33
  32.2 0.0 collective-permute-done.refs_3_.kv_hbm
  32.2 4.0 %forward.1 = bf16[8,8,24,384]{3,2,1,0:T(8,128)(2,1)} custom-call(s32[1,2,2]{2,1,0:T(2,128)} %ids_hbm.1, s32[1,2]{1,0:T(1,128)} %cnt_hbm.1, bf16[1,256,384]{2,1,0:T(8,128)(2,1)} %q_hbm.1, bf16[1,2,256,384]{3,2,1,0:T(8,128)(2,1)S(1)} %collective-permute-done.refs_3_.kv_hbm, bf16[1,256,1536]{2,1,0:T(8,128)(2,1)} %cot_hbm.1), custom_call_target="tpu_custom_call" | custom-call | flops 402653184 | bytes 3145728 | tf_op jit(solution)/shard_map/forward/pallas_call | solution.py:212
  36.2 3.6 %all-to-all-start.1 = ((bf16[8,8,24,384]{3,2,1,0:T(8,128)(2,1)}), bf16[8,8,24,384]{3,2,1,0:T(8,128)(2,1)S(1)}, u32[]{:S(2)}, u32[]{:S(2)}) async-start(bf16[8,8,24,384]{3,2,1,0:T(8,128)(2,1)} %forward.1), calls=%async_computation.1 | async-start | bytes 2359296 | tf_op jit(solution)/shard_map/all_to_all | solution.py:33
  39.8 8.2 %collective-permute-start.1 = (bf16[1,8,24,384]{3,2,1,0:T(8,128)(2,1)S(1)}, bf16[1,8,24,384]{3,2,1,0:T(8,128)(2,1)S(1)}, u32[]{:S(2)}, u32[]{:S(2)}) collective-permute-start(bf16[1,8,24,384]{3,2,1,0:T(8,128)(2,1)S(1)} %bitcast.3), channel_id=1, source_target_pairs={{0,128},{32,160},{64,192},{96,224},{128,0},{160,32},{192,64},{224,... | collective-permute-start | bytes 442376 | tf_op jit(solution)/shard_map/ppermute | solution.py:40
  48.0 4.2 %collective-permute-done.1 = bf16[1,8,24,384]{3,2,1,0:T(8,128)(2,1)S(1)} collective-permute-done((bf16[1,8,24,384]{3,2,1,0:T(8,128)(2,1)S(1)}, bf16[1,8,24,384]{3,2,1,0:T(8,128)(2,1)S(1)}, u32[]{:S(2)}, u32[]{:S(2)}) %collective-permute-start.1) | collective-permute-done | bytes 147488 | tf_op jit(solution)/shard_map/ppermute | solution.py:40
  52.3 4.9 %collective-permute-start.2 = (bf16[2,8,24,384]{3,2,1,0:T(8,128)(2,1)S(1)}, bf16[2,8,24,384]{3,2,1,0:T(8,128)(2,1)S(1)}, u32[]{:S(2)}, u32[]{:S(2)}) collective-permute-start(bf16[2,8,24,384]{3,2,1,0:T(8,128)(2,1)S(1)} %pad_maximum_fusion.refs_5_), channel_id=1, source_target_pairs={{0,64},{32,96},{64,0},{96,32},{128,192},{160,224},{192,128},{224,1... | collective-permute-start | bytes 884744 | tf_op jit(solution)/shard_map/ppermute | solution.py:40
  57.2 2.0 %collective-permute-start.3 = (bf16[2,8,24,384]{3,2,1,0:T(8,128)(2,1)S(1)}, bf16[2,8,24,384]{3,2,1,0:T(8,128)(2,1)S(1)}, u32[]{:S(2)}, u32[]{:S(2)}) collective-permute-start(bf16[2,8,24,384]{3,2,1,0:T(8,128)(2,1)S(1)} %pad_maximum_fusion.refs_5_), channel_id=1, source_target_pairs={{0,32},{32,0},{64,96},{96,64},{128,160},{160,128},{192,224},{224,1... | collective-permute-start | bytes 884744 | tf_op jit(solution)/shard_map/ppermute | solution.py:40
  59.2 5.7 %collective-permute-done.2.refs_6_ = bf16[2,8,24,384]{3,2,1,0:T(8,128)(2,1)S(1)} collective-permute-done((bf16[2,8,24,384]{3,2,1,0:T(8,128)(2,1)S(1)}, bf16[2,8,24,384]{3,2,1,0:T(8,128)(2,1)S(1)}, u32[]{:S(2)}, u32[]{:S(2)}) %collective-permute-start.2) | collective-permute-done | bytes 294944 | tf_op jit(solution)/shard_map/ppermute | solution.py:40
  64.8 1.9 %collective-permute-start.4 = (bf16[2,8,24,384]{3,2,1,0:T(8,128)(2,1)S(1)}, bf16[2,8,24,384]{3,2,1,0:T(8,128)(2,1)S(1)}, u32[]{:S(2)}, u32[]{:S(2)}) collective-permute-start(bf16[2,8,24,384]{3,2,1,0:T(8,128)(2,1)S(1)} %collective-permute-done.2.refs_6_), channel_id=1, source_target_pairs={{0,32},{32,0},{64,96},{96,64},{128,160},{160,128},{192,224},{224,1... | collective-permute-start | bytes 884744 | tf_op jit(solution)/shard_map/ppermute | solution.py:40
  66.7 1.1 %collective-permute-done.3.refs_7_ = bf16[2,8,24,384]{3,2,1,0:T(8,128)(2,1)S(1)} collective-permute-done((bf16[2,8,24,384]{3,2,1,0:T(8,128)(2,1)S(1)}, bf16[2,8,24,384]{3,2,1,0:T(8,128)(2,1)S(1)}, u32[]{:S(2)}, u32[]{:S(2)}) %collective-permute-start.3) | collective-permute-done | bytes 294944 | tf_op jit(solution)/shard_map/ppermute | solution.py:40
  67.9 5.5 %collective-permute-done.4.refs_8_ = bf16[2,8,24,384]{3,2,1,0:T(8,128)(2,1)S(1)} collective-permute-done((bf16[2,8,24,384]{3,2,1,0:T(8,128)(2,1)S(1)}, bf16[2,8,24,384]{3,2,1,0:T(8,128)(2,1)S(1)}, u32[]{:S(2)}, u32[]{:S(2)}) %collective-permute-start.4) | collective-permute-done | bytes 294944 | tf_op jit(solution)/shard_map/ppermute | solution.py:40
  73.4 5.0 %backward.1 = (bf16[1,256,384]{2,1,0:T(8,128)(2,1)}, bf16[1,2,256,384]{3,2,1,0:T(8,128)(2,1)S(1)}) custom-call(s32[1,2,2]{2,1,0:T(2,128)} %ids_hbm.1, s32[1,2]{1,0:T(1,128)} %cnt_hbm.1, bf16[1,256,384]{2,1,0:T(8,128)(2,1)} %q_hbm.1, bf16[1,2,256,384]{3,2,1,0:T(8,128)(2,1)S(1)} %collective-permute-done.refs_3_.kv_hbm, bf16[1,256,1536]{2,1,0:T(8,128)(2,1)} %cot_hbm.1, ...), custom_call_target="tpu_custom_call" | custom-call | flops 603979776 | bytes 4194304 | tf_op jit(solution)/shard_map/backward/pallas_call | solution.py:230
  78.5 1.9 %collective-permute-start.5 = (bf16[1,2,256,384]{3,2,1,0:T(8,128)(2,1)S(1)}, bf16[1,2,256,384]{3,2,1,0:T(8,128)(2,1)S(1)}, u32[]{:S(2)}, u32[]{:S(2)}) collective-permute-start(bf16[1,2,256,384]{3,2,1,0:T(8,128)(2,1)S(1)} %get-tuple-element.10), channel_id=1, source_target_pairs={{0,768},{256,0},{512,256},{768,512},{1,769},{257,1},{513,257},{769... | collective-permute-start | bytes 1179656 | tf_op jit(solution)/shard_map/ppermute | solution.py:18
  80.4 0.0 all-to-all-done.1.parts_ref
  80.4 0.8 fold.2
  81.2 6.7 %all-to-all-start.2 = ((bf16[8,24,384]{2,1,0:T(8,128)(2,1)}), bf16[8,24,384]{2,1,0:T(8,128)(2,1)S(1)}, u32[]{:S(2)}, u32[]{:S(2)}) async-start(bf16[8,24,384]{2,1,0:T(8,128)(2,1)} %fold.2), calls=%async_computation.2 | async-start | bytes 294912 | tf_op jit(solution)/shard_map/all_to_all | solution.py:33
  88.0 5.8 %collective-permute-done.5 = bf16[1,2,256,384]{3,2,1,0:T(8,128)(2,1)S(1)} collective-permute-done((bf16[1,2,256,384]{3,2,1,0:T(8,128)(2,1)S(1)}, bf16[1,2,256,384]{3,2,1,0:T(8,128)(2,1)S(1)}, u32[]{:S(2)}, u32[]{:S(2)}) %collective-permute-start.5) | collective-permute-done | bytes 393248 | tf_op jit(solution)/shard_map/ppermute | solution.py:18
  93.8 3.5 %all-to-all-done.2.parts_ref = bf16[8,24,384]{2,1,0:T(8,128)(2,1)S(1)} async-done(((bf16[8,24,384]{2,1,0:T(8,128)(2,1)}), bf16[8,24,384]{2,1,0:T(8,128)(2,1)S(1)}, u32[]{:S(2)}, u32[]{:S(2)}) %all-to-all-start.2) | async-done | bytes 147488 | tf_op jit(solution)/shard_map/all_to_all | solution.py:33
  97.2 0.6 fold.3
  97.9 0.7 copy.10
  (1 shorter events, 0.0 us)
Async XLA Ops:
  0.6 31.6 %collective-permute-start = (bf16[1,2,256,384]{3,2,1,0:T(8,128)(2,1)}, bf16[1,2,256,384]{3,2,1,0:T(8,128)(2,1)S(1)}, u32[]{:S(2)}, u32[]{:S(2)}) collective-permute-start(bf16[1,2,256,384]{3,2,1,0:T(8,128)(2,1)} %param.7), channel_id=1, source_target_pairs={{0,256},{256,512},{512,768},{768,0},{1,257},{257,513},{513,769},{7... | collective-permute-start | bytes 1179656 | tf_op jit(solution)/shard_map/ppermute | solution.py:18
  36.2 44.2 %all-to-all-start.1 = ((bf16[8,8,24,384]{3,2,1,0:T(8,128)(2,1)}), bf16[8,8,24,384]{3,2,1,0:T(8,128)(2,1)S(1)}, u32[]{:S(2)}, u32[]{:S(2)}) async-start(bf16[8,8,24,384]{3,2,1,0:T(8,128)(2,1)} %forward.1), calls=%async_computation.1 | async-start | bytes 2359296 | tf_op jit(solution)/shard_map/all_to_all | solution.py:33
  39.8 12.4 %collective-permute-start.1 = (bf16[1,8,24,384]{3,2,1,0:T(8,128)(2,1)S(1)}, bf16[1,8,24,384]{3,2,1,0:T(8,128)(2,1)S(1)}, u32[]{:S(2)}, u32[]{:S(2)}) collective-permute-start(bf16[1,8,24,384]{3,2,1,0:T(8,128)(2,1)S(1)} %bitcast.3), channel_id=1, source_target_pairs={{0,128},{32,160},{64,192},{96,224},{128,0},{160,32},{192,64},{224,... | collective-permute-start | bytes 442376 | tf_op jit(solution)/shard_map/ppermute | solution.py:40
  52.3 12.5 %collective-permute-start.2 = (bf16[2,8,24,384]{3,2,1,0:T(8,128)(2,1)S(1)}, bf16[2,8,24,384]{3,2,1,0:T(8,128)(2,1)S(1)}, u32[]{:S(2)}, u32[]{:S(2)}) collective-permute-start(bf16[2,8,24,384]{3,2,1,0:T(8,128)(2,1)S(1)} %pad_maximum_fusion.refs_5_), channel_id=1, source_target_pairs={{0,64},{32,96},{64,0},{96,32},{128,192},{160,224},{192,128},{224,1... | collective-permute-start | bytes 884744 | tf_op jit(solution)/shard_map/ppermute | solution.py:40
  57.2 10.7 %collective-permute-start.3 = (bf16[2,8,24,384]{3,2,1,0:T(8,128)(2,1)S(1)}, bf16[2,8,24,384]{3,2,1,0:T(8,128)(2,1)S(1)}, u32[]{:S(2)}, u32[]{:S(2)}) collective-permute-start(bf16[2,8,24,384]{3,2,1,0:T(8,128)(2,1)S(1)} %pad_maximum_fusion.refs_5_), channel_id=1, source_target_pairs={{0,32},{32,0},{64,96},{96,64},{128,160},{160,128},{192,224},{224,1... | collective-permute-start | bytes 884744 | tf_op jit(solution)/shard_map/ppermute | solution.py:40
  64.8 8.6 %collective-permute-start.4 = (bf16[2,8,24,384]{3,2,1,0:T(8,128)(2,1)S(1)}, bf16[2,8,24,384]{3,2,1,0:T(8,128)(2,1)S(1)}, u32[]{:S(2)}, u32[]{:S(2)}) collective-permute-start(bf16[2,8,24,384]{3,2,1,0:T(8,128)(2,1)S(1)} %collective-permute-done.2.refs_6_), channel_id=1, source_target_pairs={{0,32},{32,0},{64,96},{96,64},{128,160},{160,128},{192,224},{224,1... | collective-permute-start | bytes 884744 | tf_op jit(solution)/shard_map/ppermute | solution.py:40
  78.5 15.3 %collective-permute-start.5 = (bf16[1,2,256,384]{3,2,1,0:T(8,128)(2,1)S(1)}, bf16[1,2,256,384]{3,2,1,0:T(8,128)(2,1)S(1)}, u32[]{:S(2)}, u32[]{:S(2)}) collective-permute-start(bf16[1,2,256,384]{3,2,1,0:T(8,128)(2,1)S(1)} %get-tuple-element.10), channel_id=1, source_target_pairs={{0,768},{256,0},{512,256},{768,512},{1,769},{257,1},{513,257},{769... | collective-permute-start | bytes 1179656 | tf_op jit(solution)/shard_map/ppermute | solution.py:18
  81.2 16.0 %all-to-all-start.2 = ((bf16[8,24,384]{2,1,0:T(8,128)(2,1)}), bf16[8,24,384]{2,1,0:T(8,128)(2,1)S(1)}, u32[]{:S(2)}, u32[]{:S(2)}) async-start(bf16[8,24,384]{2,1,0:T(8,128)(2,1)} %fold.2), calls=%async_computation.2 | async-start | bytes 294912 | tf_op jit(solution)/shard_map/all_to_all | solution.py:33

commit v5 on v4

--- a/solution.py
+++ b/solution.py
@@ -41,14 +41,8 @@
 
 
 def gather_slots(near):
-    pieces = [(near[None], [0])]
-    distance = len(lines(False)[0]) // 2
-    while distance:
-        if len(pieces) == 2 and distance > 1:
-            pieces = [(jnp.concatenate([a for a, _ in pieces]), [s for _, k in pieces for s in k])]
-        pieces += [(mirror(a, distance), [s ^ distance for s in k]) for a, k in pieces]
-        distance //= 2
-    return pieces
+    own = near[None]
+    return [(own, [0])] + [(mirror(own, k), [k]) for k in range(1, len(lines(False)[0]))]
 
 
 def dot(a, b, dims):
@@ -205,7 +199,6 @@
 
     used = from_behind(context, "segment", 1)
     near = swap(jnp.broadcast_to(w_out, (nz, rows, width)), True)
-    used, near = lax.optimization_barrier((used, near))
     fixed = [pltpu.with_memory_space_constraint(a, pltpu.HBM) for a in (vis_blocks, vis_count, queries)]
     cotan = pltpu.with_memory_space_constraint(grad_out, pltpu.HBM)
 

time: 99.8 us -> 95.6 us (0.958)
  starting transfers between devices: 34.3 us -> 61.4 us
  blocking collectives: 25.7 us -> 0 us
  waiting for transfers between devices: 25.8 us -> 19.1 us
    all_to_all x1 -> x0, blocking collectives: 25.7 us -> none  [swap(): lax.all_to_all(x, PLANE, split_axis=0, concat_axis=0, axis_index_groups=l...]
    all_to_all x2 -> x3, starting transfers between devices: 10.3 us -> 25.7 us  [swap(): lax.all_to_all(x, PLANE, split_axis=0, concat_axis=0, axis_index_groups=l...]
    ppermute x4 -> x7, waiting for transfers between devices: 16.6 us -> 4.67 us  [mirror(): return lax.ppermute(x, PLANE, pairs)]
    ppermute x4 -> x7, starting transfers between devices: 17 us -> 28.6 us  [mirror(): return lax.ppermute(x, PLANE, pairs)]
    all_to_all x2 -> x3, waiting for transfers between devices: 3.48 us -> 7.69 us  [swap(): lax.all_to_all(x, PLANE, split_axis=0, concat_axis=0, axis_index_groups=l...]
  transfers between devices with their start and end apart: 8 -> 12, of which waited for: 6 -> 6; matrix products, arithmetic and copies ran while one was open for 1% -> 1% of each run, Pallas kernels for 6% -> 11%
where the time goes in v5:
time: 95.6 us; the launch traced here: 94 us
  starting transfers between devices  61.4 us (64%)
  waiting for transfers between devices  19.1 us (20%)
  Pallas kernels  10.6 us (11%)
  local copies, waits for them, and re-layouts  2.14 us (2%)
    ppermute x7, starting transfers between devices, mirror(): return lax.ppermute(x, PLANE, pairs)  28.6 us
    all_to_all x3, starting transfers between devices, swap(): lax.all_to_all(x, PLANE, split_axis=0, concat_axis=0, axis_index_groups=l...  25.7 us
    all_to_all x3, waiting for transfers between devices, swap(): lax.all_to_all(x, PLANE, split_axis=0, concat_axis=0, axis_index_groups=l...  7.69 us
    ppermute x2, starting transfers between devices, from_behind(): return lax.ppermute(x, axis, [(i, (i + by) % count) for i in range(count)])  7 us
    ppermute x2, waiting for transfers between devices, from_behind(): return lax.ppermute(x, axis, [(i, (i + by) % count) for i in range(count)])  6.75 us
    pallas_call x1, Pallas kernels, shards(): pl.pallas_call(lambda *refs: backward_kernel(slots, *refs), name='backwar...  5.05 us
    ppermute x7, waiting for transfers between devices, mirror(): return lax.ppermute(x, PLANE, pairs)  4.67 us
    pallas_call x1, Pallas kernels, shards(): pl.pallas_call(forward_kernel, name='forward', out_shape=jax.ShapeDtypeSt...  4.06 us
  transfers between devices with their start and end apart: 12, of which 6 were waited for; matrix products, arithmetic and copies ran while one was open for 1% of the time, Pallas kernels for 11%

profile of v5, /device:TPU:14, one launch (start us, length us, event | category | flops | bytes accessed | tf_op | source)
XLA Modules:
  0.0 94.0 jit_solution(15730809360164409660)
XLA Ops:
  0.6 5.1 %collective-permute-start = (bf16[1,2,256,384]{3,2,1,0:T(8,128)(2,1)}, bf16[1,2,256,384]{3,2,1,0:T(8,128)(2,1)S(1)}, u32[]{:S(2)}, u32[]{:S(2)}) collective-permute-start(bf16[1,2,256,384]{3,2,1,0:T(8,128)(2,1)} %param.7), channel_id=1, source_target_pairs={{0,256},{256,512},{512,768},{768,0},{1,257},{257,513},{513,769},{7... | collective-permute-start | bytes 1179656 | tf_op jit(solution)/shard_map/ppermute | solution.py:18
  5.7 1.4 %broadcast_in_dim.14 = bf16[8,24,384]{2,1,0:T(8,128)(2,1)} broadcast(bf16[24,384]{1,0:T(8,128)(2,1)} %bitcast.12), dimensions={1,2} | broadcast | bytes 165888 | tf_op jit(solution)/shard_map/broadcast_in_dim | solution.py:201
  7.1 16.7 %all-to-all-start = ((bf16[8,24,384]{2,1,0:T(8,128)(2,1)}), bf16[8,24,384]{2,1,0:T(8,128)(2,1)S(1)}, u32[]{:S(2)}, u32[]{:S(2)}) async-start(bf16[8,24,384]{2,1,0:T(8,128)(2,1)} %broadcast_in_dim.14), calls=%async_computation | async-start | bytes 294912 | tf_op jit(solution)/shard_map/all_to_all | solution.py:33
  23.8 0.0 collective-permute-done.refs_3_.kv_hbm
  23.8 4.1 %forward.1 = bf16[8,8,24,384]{3,2,1,0:T(8,128)(2,1)} custom-call(s32[1,2,2]{2,1,0:T(2,128)} %ids_hbm.1, s32[1,2]{1,0:T(1,128)} %cnt_hbm.1, bf16[1,256,384]{2,1,0:T(8,128)(2,1)} %q_hbm.1, bf16[1,2,256,384]{3,2,1,0:T(8,128)(2,1)S(1)} %collective-permute-done.refs_3_.kv_hbm, bf16[1,256,1536]{2,1,0:T(8,128)(2,1)} %cot_hbm.1), custom_call_target="tpu_custom_call" | custom-call | flops 402653184 | bytes 3145728 | tf_op jit(solution)/shard_map/forward/pallas_call | solution.py:205
  27.9 5.2 %all-to-all-done = bf16[8,24,384]{2,1,0:T(8,128)(2,1)S(1)} async-done(((bf16[8,24,384]{2,1,0:T(8,128)(2,1)}), bf16[8,24,384]{2,1,0:T(8,128)(2,1)S(1)}, u32[]{:S(2)}, u32[]{:S(2)}) %all-to-all-start) | async-done | bytes 147488 | tf_op jit(solution)/shard_map/all_to_all | solution.py:33
  33.1 3.6 %all-to-all-start.1 = ((bf16[8,8,24,384]{3,2,1,0:T(8,128)(2,1)}), bf16[8,8,24,384]{3,2,1,0:T(8,128)(2,1)S(1)}, u32[]{:S(2)}, u32[]{:S(2)}) async-start(bf16[8,8,24,384]{3,2,1,0:T(8,128)(2,1)} %forward.1), calls=%async_computation.1 | async-start | bytes 2359296 | tf_op jit(solution)/shard_map/all_to_all | solution.py:33
  36.6 6.2 %collective-permute-start.7 = (bf16[1,8,24,384]{3,2,1,0:T(8,128)(2,1)S(1)}, bf16[1,8,24,384]{3,2,1,0:T(8,128)(2,1)S(1)}, u32[]{:S(2)}, u32[]{:S(2)}) collective-permute-start(bf16[1,8,24,384]{3,2,1,0:T(8,128)(2,1)S(1)} %bitcast.3), channel_id=1, source_target_pairs={{0,224},{32,192},{64,160},{96,128},{128,96},{160,64},{192,32},{224... | collective-permute-start | bytes 442376 | tf_op jit(solution)/shard_map/ppermute | solution.py:40
  42.8 2.9 %collective-permute-start.6 = (bf16[1,8,24,384]{3,2,1,0:T(8,128)(2,1)S(1)}, bf16[1,8,24,384]{3,2,1,0:T(8,128)(2,1)S(1)}, u32[]{:S(2)}, u32[]{:S(2)}) collective-permute-start(bf16[1,8,24,384]{3,2,1,0:T(8,128)(2,1)S(1)} %bitcast.4), channel_id=1, source_target_pairs={{0,192},{32,224},{64,128},{96,160},{128,64},{160,96},{192,0},{224,... | collective-permute-start | bytes 442376 | tf_op jit(solution)/shard_map/ppermute | solution.py:40
  45.7 6.2 %collective-permute-start.5 = (bf16[1,8,24,384]{3,2,1,0:T(8,128)(2,1)S(1)}, bf16[1,8,24,384]{3,2,1,0:T(8,128)(2,1)S(1)}, u32[]{:S(2)}, u32[]{:S(2)}) collective-permute-start(bf16[1,8,24,384]{3,2,1,0:T(8,128)(2,1)S(1)} %bitcast.5), channel_id=1, source_target_pairs={{0,160},{32,128},{64,224},{96,192},{128,32},{160,0},{192,96},{224,... | collective-permute-start | bytes 442376 | tf_op jit(solution)/shard_map/ppermute | solution.py:40
  51.9 3.3 %collective-permute-start.4 = (bf16[1,8,24,384]{3,2,1,0:T(8,128)(2,1)S(1)}, bf16[1,8,24,384]{3,2,1,0:T(8,128)(2,1)S(1)}, u32[]{:S(2)}, u32[]{:S(2)}) collective-permute-start(bf16[1,8,24,384]{3,2,1,0:T(8,128)(2,1)S(1)} %bitcast.6), channel_id=1, source_target_pairs={{0,128},{32,160},{64,192},{96,224},{128,0},{160,32},{192,64},{224,... | collective-permute-start | bytes 442376 | tf_op jit(solution)/shard_map/ppermute | solution.py:40
  55.2 4.1 %collective-permute-start.3 = (bf16[1,8,24,384]{3,2,1,0:T(8,128)(2,1)S(1)}, bf16[1,8,24,384]{3,2,1,0:T(8,128)(2,1)S(1)}, u32[]{:S(2)}, u32[]{:S(2)}) collective-permute-start(bf16[1,8,24,384]{3,2,1,0:T(8,128)(2,1)S(1)} %bitcast.7), channel_id=1, source_target_pairs={{0,96},{32,64},{64,32},{96,0},{128,224},{160,192},{192,160},{224,1... | collective-permute-start | bytes 442376 | tf_op jit(solution)/shard_map/ppermute | solution.py:40
  59.3 0.0 collective-permute-done.7.refs_12_
  59.3 2.0 %collective-permute-start.2 = (bf16[1,8,24,384]{3,2,1,0:T(8,128)(2,1)S(1)}, bf16[1,8,24,384]{3,2,1,0:T(8,128)(2,1)S(1)}, u32[]{:S(2)}, u32[]{:S(2)}) collective-permute-start(bf16[1,8,24,384]{3,2,1,0:T(8,128)(2,1)S(1)} %bitcast.8), channel_id=1, source_target_pairs={{0,64},{32,96},{64,0},{96,32},{128,192},{160,224},{192,128},{224,1... | collective-permute-start | bytes 442376 | tf_op jit(solution)/shard_map/ppermute | solution.py:40
  61.4 0.0 collective-permute-done.6.refs_11_
  61.4 4.0 %collective-permute-start.1 = (bf16[1,8,24,384]{3,2,1,0:T(8,128)(2,1)S(1)}, bf16[1,8,24,384]{3,2,1,0:T(8,128)(2,1)S(1)}, u32[]{:S(2)}, u32[]{:S(2)}) collective-permute-start(bf16[1,8,24,384]{3,2,1,0:T(8,128)(2,1)S(1)} %bitcast.9), channel_id=1, source_target_pairs={{0,32},{32,0},{64,96},{96,64},{128,160},{160,128},{192,224},{224,1... | collective-permute-start | bytes 442376 | tf_op jit(solution)/shard_map/ppermute | solution.py:40
  65.3 0.0 collective-permute-done.5.refs_10_
  65.3 0.0 collective-permute-done.4.refs_9_
  65.4 0.3 collective-permute-done.3.refs_8_
  65.7 3.3 %collective-permute-done.2.refs_7_ = bf16[1,8,24,384]{3,2,1,0:T(8,128)(2,1)S(1)} collective-permute-done((bf16[1,8,24,384]{3,2,1,0:T(8,128)(2,1)S(1)}, bf16[1,8,24,384]{3,2,1,0:T(8,128)(2,1)S(1)}, u32[]{:S(2)}, u32[]{:S(2)}) %collective-permute-start.2) | collective-permute-done | bytes 147488 | tf_op jit(solution)/shard_map/ppermute | solution.py:40
  69.0 1.1 %collective-permute-done.1.refs_6_ = bf16[1,8,24,384]{3,2,1,0:T(8,128)(2,1)S(1)} collective-permute-done((bf16[1,8,24,384]{3,2,1,0:T(8,128)(2,1)S(1)}, bf16[1,8,24,384]{3,2,1,0:T(8,128)(2,1)S(1)}, u32[]{:S(2)}, u32[]{:S(2)}) %collective-permute-start.1) | collective-permute-done | bytes 147488 | tf_op jit(solution)/shard_map/ppermute | solution.py:40
  70.0 5.0 %backward.1 = (bf16[1,256,384]{2,1,0:T(8,128)(2,1)}, bf16[1,2,256,384]{3,2,1,0:T(8,128)(2,1)S(1)}) custom-call(s32[1,2,2]{2,1,0:T(2,128)} %ids_hbm.1, s32[1,2]{1,0:T(1,128)} %cnt_hbm.1, bf16[1,256,384]{2,1,0:T(8,128)(2,1)} %q_hbm.1, bf16[1,2,256,384]{3,2,1,0:T(8,128)(2,1)S(1)} %collective-permute-done.refs_3_.kv_hbm, bf16[1,256,1536]{2,1,0:T(8,128)(2,1)} %cot_hbm.1, ...), custom_call_target="tpu_custom_call" | custom-call | flops 603979776 | bytes 4194304 | tf_op jit(solution)/shard_map/backward/pallas_call | solution.py:223
  75.1 1.9 %collective-permute-start.8 = (bf16[1,2,256,384]{3,2,1,0:T(8,128)(2,1)S(1)}, bf16[1,2,256,384]{3,2,1,0:T(8,128)(2,1)S(1)}, u32[]{:S(2)}, u32[]{:S(2)}) collective-permute-start(bf16[1,2,256,384]{3,2,1,0:T(8,128)(2,1)S(1)} %get-tuple-element.6), channel_id=1, source_target_pairs={{0,768},{256,0},{512,256},{768,512},{1,769},{257,1},{513,257},{769... | collective-permute-start | bytes 1179656 | tf_op jit(solution)/shard_map/ppermute | solution.py:18
  77.0 0.0 all-to-all-done.1.parts_ref
  77.0 0.8 fold.2
  77.8 5.5 %all-to-all-start.2 = ((bf16[8,24,384]{2,1,0:T(8,128)(2,1)}), bf16[8,24,384]{2,1,0:T(8,128)(2,1)S(1)}, u32[]{:S(2)}, u32[]{:S(2)}) async-start(bf16[8,24,384]{2,1,0:T(8,128)(2,1)} %fold.2), calls=%async_computation.2 | async-start | bytes 294912 | tf_op jit(solution)/shard_map/all_to_all | solution.py:33
  83.3 6.7 %collective-permute-done.8 = bf16[1,2,256,384]{3,2,1,0:T(8,128)(2,1)S(1)} collective-permute-done((bf16[1,2,256,384]{3,2,1,0:T(8,128)(2,1)S(1)}, bf16[1,2,256,384]{3,2,1,0:T(8,128)(2,1)S(1)}, u32[]{:S(2)}, u32[]{:S(2)}) %collective-permute-start.8) | collective-permute-done | bytes 393248 | tf_op jit(solution)/shard_map/ppermute | solution.py:18
  90.1 2.5 %all-to-all-done.2.parts_ref = bf16[8,24,384]{2,1,0:T(8,128)(2,1)S(1)} async-done(((bf16[8,24,384]{2,1,0:T(8,128)(2,1)}), bf16[8,24,384]{2,1,0:T(8,128)(2,1)S(1)}, u32[]{:S(2)}, u32[]{:S(2)}) %all-to-all-start.2) | async-done | bytes 147488 | tf_op jit(solution)/shard_map/all_to_all | solution.py:33
  92.6 0.6 fold.3
  93.2 0.7 copy.10
Async XLA Ops:
  0.6 23.2 %collective-permute-start = (bf16[1,2,256,384]{3,2,1,0:T(8,128)(2,1)}, bf16[1,2,256,384]{3,2,1,0:T(8,128)(2,1)S(1)}, u32[]{:S(2)}, u32[]{:S(2)}) collective-permute-start(bf16[1,2,256,384]{3,2,1,0:T(8,128)(2,1)} %param.7), channel_id=1, source_target_pairs={{0,256},{256,512},{512,768},{768,0},{1,257},{257,513},{513,769},{7... | collective-permute-start | bytes 1179656 | tf_op jit(solution)/shard_map/ppermute | solution.py:18
  7.1 25.9 %all-to-all-start = ((bf16[8,24,384]{2,1,0:T(8,128)(2,1)}), bf16[8,24,384]{2,1,0:T(8,128)(2,1)S(1)}, u32[]{:S(2)}, u32[]{:S(2)}) async-start(bf16[8,24,384]{2,1,0:T(8,128)(2,1)} %broadcast_in_dim.14), calls=%async_computation | async-start | bytes 294912 | tf_op jit(solution)/shard_map/all_to_all | solution.py:33
  33.1 44.0 %all-to-all-start.1 = ((bf16[8,8,24,384]{3,2,1,0:T(8,128)(2,1)}), bf16[8,8,24,384]{3,2,1,0:T(8,128)(2,1)S(1)}, u32[]{:S(2)}, u32[]{:S(2)}) async-start(bf16[8,8,24,384]{3,2,1,0:T(8,128)(2,1)} %forward.1), calls=%async_computation.1 | async-start | bytes 2359296 | tf_op jit(solution)/shard_map/all_to_all | solution.py:33
  36.6 22.7 %collective-permute-start.7 = (bf16[1,8,24,384]{3,2,1,0:T(8,128)(2,1)S(1)}, bf16[1,8,24,384]{3,2,1,0:T(8,128)(2,1)S(1)}, u32[]{:S(2)}, u32[]{:S(2)}) collective-permute-start(bf16[1,8,24,384]{3,2,1,0:T(8,128)(2,1)S(1)} %bitcast.3), channel_id=1, source_target_pairs={{0,224},{32,192},{64,160},{96,128},{128,96},{160,64},{192,32},{224... | collective-permute-start | bytes 442376 | tf_op jit(solution)/shard_map/ppermute | solution.py:40
  42.8 18.5 %collective-permute-start.6 = (bf16[1,8,24,384]{3,2,1,0:T(8,128)(2,1)S(1)}, bf16[1,8,24,384]{3,2,1,0:T(8,128)(2,1)S(1)}, u32[]{:S(2)}, u32[]{:S(2)}) collective-permute-start(bf16[1,8,24,384]{3,2,1,0:T(8,128)(2,1)S(1)} %bitcast.4), channel_id=1, source_target_pairs={{0,192},{32,224},{64,128},{96,160},{128,64},{160,96},{192,0},{224,... | collective-permute-start | bytes 442376 | tf_op jit(solution)/shard_map/ppermute | solution.py:40
  45.7 19.6 %collective-permute-start.5 = (bf16[1,8,24,384]{3,2,1,0:T(8,128)(2,1)S(1)}, bf16[1,8,24,384]{3,2,1,0:T(8,128)(2,1)S(1)}, u32[]{:S(2)}, u32[]{:S(2)}) collective-permute-start(bf16[1,8,24,384]{3,2,1,0:T(8,128)(2,1)S(1)} %bitcast.5), channel_id=1, source_target_pairs={{0,160},{32,128},{64,224},{96,192},{128,32},{160,0},{192,96},{224,... | collective-permute-start | bytes 442376 | tf_op jit(solution)/shard_map/ppermute | solution.py:40
  51.9 13.5 %collective-permute-start.4 = (bf16[1,8,24,384]{3,2,1,0:T(8,128)(2,1)S(1)}, bf16[1,8,24,384]{3,2,1,0:T(8,128)(2,1)S(1)}, u32[]{:S(2)}, u32[]{:S(2)}) collective-permute-start(bf16[1,8,24,384]{3,2,1,0:T(8,128)(2,1)S(1)} %bitcast.6), channel_id=1, source_target_pairs={{0,128},{32,160},{64,192},{96,224},{128,0},{160,32},{192,64},{224,... | collective-permute-start | bytes 442376 | tf_op jit(solution)/shard_map/ppermute | solution.py:40
  55.2 10.5 %collective-permute-start.3 = (bf16[1,8,24,384]{3,2,1,0:T(8,128)(2,1)S(1)}, bf16[1,8,24,384]{3,2,1,0:T(8,128)(2,1)S(1)}, u32[]{:S(2)}, u32[]{:S(2)}) collective-permute-start(bf16[1,8,24,384]{3,2,1,0:T(8,128)(2,1)S(1)} %bitcast.7), channel_id=1, source_target_pairs={{0,96},{32,64},{64,32},{96,0},{128,224},{160,192},{192,160},{224,1... | collective-permute-start | bytes 442376 | tf_op jit(solution)/shard_map/ppermute | solution.py:40
  59.3 9.6 %collective-permute-start.2 = (bf16[1,8,24,384]{3,2,1,0:T(8,128)(2,1)S(1)}, bf16[1,8,24,384]{3,2,1,0:T(8,128)(2,1)S(1)}, u32[]{:S(2)}, u32[]{:S(2)}) collective-permute-start(bf16[1,8,24,384]{3,2,1,0:T(8,128)(2,1)S(1)} %bitcast.8), channel_id=1, source_target_pairs={{0,64},{32,96},{64,0},{96,32},{128,192},{160,224},{192,128},{224,1... | collective-permute-start | bytes 442376 | tf_op jit(solution)/shard_map/ppermute | solution.py:40
  61.4 8.7 %collective-permute-start.1 = (bf16[1,8,24,384]{3,2,1,0:T(8,128)(2,1)S(1)}, bf16[1,8,24,384]{3,2,1,0:T(8,128)(2,1)S(1)}, u32[]{:S(2)}, u32[]{:S(2)}) collective-permute-start(bf16[1,8,24,384]{3,2,1,0:T(8,128)(2,1)S(1)} %bitcast.9), channel_id=1, source_target_pairs={{0,32},{32,0},{64,96},{96,64},{128,160},{160,128},{192,224},{224,1... | collective-permute-start | bytes 442376 | tf_op jit(solution)/shard_map/ppermute | solution.py:40
  75.1 15.0 %collective-permute-start.8 = (bf16[1,2,256,384]{3,2,1,0:T(8,128)(2,1)S(1)}, bf16[1,2,256,384]{3,2,1,0:T(8,128)(2,1)S(1)}, u32[]{:S(2)}, u32[]{:S(2)}) collective-permute-start(bf16[1,2,256,384]{3,2,1,0:T(8,128)(2,1)S(1)} %get-tuple-element.6), channel_id=1, source_target_pairs={{0,768},{256,0},{512,256},{768,512},{1,769},{257,1},{513,257},{769... | collective-permute-start | bytes 1179656 | tf_op jit(solution)/shard_map/ppermute | solution.py:18
  77.8 14.7 %all-to-all-start.2 = ((bf16[8,24,384]{2,1,0:T(8,128)(2,1)}), bf16[8,24,384]{2,1,0:T(8,128)(2,1)S(1)}, u32[]{:S(2)}, u32[]{:S(2)}) async-start(bf16[8,24,384]{2,1,0:T(8,128)(2,1)} %fold.2), calls=%async_computation.2 | async-start | bytes 294912 | tf_op jit(solution)/shard_map/all_to_all | solution.py:33

commit v6 on v5

--- a/solution.py
+++ b/solution.py
@@ -29,20 +29,17 @@
     return groups
 
 
-def swap(x, first):
-    return lax.all_to_all(
-        x, PLANE, split_axis=0, concat_axis=0, axis_index_groups=lines(first), tiled=True
-    )
-
-
-def mirror(x, distance):
-    pairs = [(line[i], line[i ^ distance]) for line in lines(False) for i in range(len(line))]
+def swap(x, groups):
+    return lax.all_to_all(x, PLANE, split_axis=0, concat_axis=0, axis_index_groups=groups, tiled=True)
+
+
+def classes(first):
+    return [line[parity::2] for line in lines(first) for parity in range(2)]
+
+
+def mirror(x, first):
+    pairs = [(line[i], line[i ^ 1]) for line in lines(first) for i in range(len(line))]
     return lax.ppermute(x, PLANE, pairs)
-
-
-def gather_slots(near):
-    own = near[None]
-    return [(own, [0])] + [(mirror(own, k), [k]) for k in range(1, len(lines(False)[0]))]
 
 
 def dot(a, b, dims):
@@ -68,7 +65,8 @@
 
 
 def forward_kernel(
-    ids_hbm, cnt_hbm, q_hbm, kv_hbm, cot_hbm, part_ref, ids_ref, cnt_ref, q_ref, kv_ref, cot_ref, attn_ref, sem
+    ids_hbm, cnt_hbm, q_hbm, kv_hbm, cot_hbm, keep_hbm, send_hbm,
+    ids_ref, cnt_ref, q_ref, kv_ref, cot_ref, attn_ref, part_ref, sem, out_sem,
 ):
     copies = [
         pltpu.make_async_copy(src, dst, sem.at[i])
@@ -87,20 +85,31 @@
         prob = softmax(q_ref[0, :, cols], kv_ref[0, 0, :, cols], live).astype(jnp.bfloat16)
         attn_ref[:, cols] = dot(prob, kv_ref[0, 1, :, cols], ((1,), (0,))).astype(jnp.bfloat16)
     copies[4].wait()
-    side, _, rows, _ = part_ref.shape
+    _, _, side, rows, _ = part_ref.shape
     attn = attn_ref[...]
     odd = lax.axis_index("tensor") % 2 == 1
+    place = jnp.where(odd, lax.axis_index(DP[0]), lax.axis_index(DP[1]))
+    parity = place % 2
     for y in range(side):
         span = side * rows
         part = dot(cot_ref[0, :, y * span : (y + 1) * span], attn, ((0,), (0,)))
         for z in range(side):
             block = part[z * rows : (z + 1) * rows].astype(jnp.bfloat16)
-            part_ref[jnp.where(odd, y, z), jnp.where(odd, z, y)] = block
-
-
-def backward_kernel(slots, ids_hbm, cnt_hbm, q_hbm, kv_hbm, cot_hbm, *refs):
-    pieces = refs[: len(slots)]
-    gq_ref, gkv_ref, ids_ref, cnt_ref, q_ref, kv_ref, cot_ref, rows_ref, sem, slot_sem = refs[len(slots) :]
+            other = (jnp.where(odd, y, z) + parity) % 2
+            part_ref[other, jnp.where(odd, y // 2, z // 2), jnp.where(odd, z, y)] = block
+    outs = [
+        pltpu.make_async_copy(part_ref.at[i], out, out_sem.at[i]) for i, out in enumerate((keep_hbm, send_hbm))
+    ]
+    for out in outs:
+        out.start()
+    for out in outs:
+        out.wait()
+
+
+def backward_kernel(
+    ids_hbm, cnt_hbm, q_hbm, kv_hbm, cot_hbm, same_hbm, other_hbm, gq_ref, gkv_ref,
+    ids_ref, cnt_ref, q_ref, kv_ref, cot_ref, rows_ref, sem, row_sem,
+):
     copies = [
         pltpu.make_async_copy(src, dst, sem.at[i])
         for i, (src, dst) in enumerate(
@@ -112,13 +121,13 @@
     odd = lax.axis_index("tensor") % 2 == 1
     placed = []
     for turned in range(2):
-        place = lax.axis_index(DP[1] if turned else DP[0])
+        parity = lax.axis_index(DP[1] if turned else DP[0]) % 2
         moves = []
-        for piece, held in zip(pieces, slots):
-            for i, k in enumerate(held):
-                at = place ^ k
+        for n, half in enumerate((same_hbm, other_hbm)):
+            for j in range(half.shape[0]):
+                at = 2 * j + (parity + n) % 2
                 target = rows_ref.at[:, at] if turned else rows_ref.at[at]
-                moves.append(pltpu.make_async_copy(piece.at[i], target, slot_sem.at[k]))
+                moves.append(pltpu.make_async_copy(half.at[j], target, row_sem.at[n * half.shape[0] + j]))
         placed.append(moves)
 
         @pl.when(odd == (turned == 1))
@@ -198,36 +207,44 @@
     ]
 
     used = from_behind(context, "segment", 1)
-    near = swap(jnp.broadcast_to(w_out, (nz, rows, width)), True)
+    near = swap(jnp.broadcast_to(w_out, (nz, rows, width)), lines(True))
+    same = swap(jnp.broadcast_to(near[None], (ny // 2, nz, rows, width)), classes(False))
+    other = mirror(same, False)
     fixed = [pltpu.with_memory_space_constraint(a, pltpu.HBM) for a in (vis_blocks, vis_count, queries)]
     cotan = pltpu.with_memory_space_constraint(grad_out, pltpu.HBM)
 
-    part = pl.pallas_call(
+    half = jax.ShapeDtypeStruct((nz // 2, ny, rows, width), jnp.bfloat16)
+    keep, send = pl.pallas_call(
         forward_kernel,
         name="forward",
-        out_shape=jax.ShapeDtypeStruct((nz, ny, rows, width), jnp.bfloat16),
+        out_shape=(half, half),
         in_specs=[hbm, hbm, hbm, anywhere, hbm],
-        out_specs=vmem,
-        scratch_shapes=small + [pltpu.VMEM((tokens, width), jnp.bfloat16), pltpu.SemaphoreType.DMA((5,))],
+        out_specs=(anywhere, anywhere),
+        scratch_shapes=small
+        + [
+            pltpu.VMEM((tokens, width), jnp.bfloat16),
+            pltpu.VMEM((2, *half.shape), jnp.bfloat16),
+            pltpu.SemaphoreType.DMA((5,)),
+            pltpu.SemaphoreType.DMA((2,)),
+        ],
         compiler_params=params,
         cost_estimate=pl.CostEstimate(
             flops=2 * tokens * width * (2 * ctx + model), bytes_accessed=3 << 20, transcendentals=heads * tokens * ctx
         ),
     )(*fixed, used, cotan)
 
-    once = fold(swap(part, True), jnp.bfloat16)
-    grad_weight = fold(swap(once, False), jnp.float32)[None]
-
-    pieces = gather_slots(near)
-    slots = [k for _, k in pieces]
+    pair = keep.astype(jnp.float32) + mirror(send, True).astype(jnp.float32)
+    once = fold(swap(pair.astype(jnp.bfloat16), classes(True)), jnp.bfloat16)
+    grad_weight = fold(swap(once, lines(False)), jnp.float32)[None]
+
     grad_q, grad_used = pl.pallas_call(
-        lambda *refs: backward_kernel(slots, *refs),
+        backward_kernel,
         name="backward",
         out_shape=(
             jax.ShapeDtypeStruct(queries.shape, jnp.bfloat16),
             jax.ShapeDtypeStruct(context.shape, jnp.bfloat16),
         ),
-        in_specs=[hbm, hbm, hbm, anywhere, hbm] + [anywhere] * len(pieces),
+        in_specs=[hbm, hbm, hbm, anywhere, hbm, anywhere, anywhere],
         out_specs=(vmem, vmem),
         scratch_shapes=small
         + [
@@ -239,7 +256,7 @@
         cost_estimate=pl.CostEstimate(
             flops=2 * tokens * width * (6 * ctx + model), bytes_accessed=4 << 20, transcendentals=heads * tokens * ctx
         ),
-    )(*fixed, used, cotan, *(a for a, _ in pieces))
+    )(*fixed, used, cotan, same, other)
     grad_context = from_behind(grad_used, "segment", -1)
     return grad_q, grad_context, grad_weight
 

time: 95.6 us -> 101 us (1.056)
  blocking collectives: 0 us -> 41.4 us
  starting transfers between devices: 61.4 us -> 23.6 us
  waiting for transfers between devices: 19.1 us -> 21.5 us
  Pallas kernels: 10.6 us -> 9.09 us
    all_to_all x0 -> x2, blocking collectives: none -> 41.4 us  [swap(): lax.all_to_all(x, PLANE, split_axis=0, concat_axis=0, axis_index_groups=g...]
    ppermute x7 -> x2, starting transfers between devices: 28.6 us -> 5.57 us  [mirror(): return lax.ppermute(x, PLANE, pairs)]
    ppermute x7 -> x2, waiting for transfers between devices: 4.67 us -> 20.9 us  [mirror(): return lax.ppermute(x, PLANE, pairs)]
    all_to_all x3 -> x2, starting transfers between devices: 25.7 us -> 11.1 us  [swap(): lax.all_to_all(x, PLANE, split_axis=0, concat_axis=0, axis_index_groups=g...]
    all_to_all x3 -> x2, waiting for transfers between devices: 7.69 us -> 0.62 us  [swap(): lax.all_to_all(x, PLANE, split_axis=0, concat_axis=0, axis_index_groups=g...]
    ppermute x2, waiting for transfers between devices: 6.75 us -> 0.01 us  [from_behind(): return lax.ppermute(x, axis, [(i, (i + by) % count) for i in range(count)])]
  transfers between devices with their start and end apart: 12 -> 6, of which waited for: 6 -> 3; matrix products, arithmetic and copies ran while one was open for 1% -> 3% of each run, Pallas kernels for 11% -> 9%
where the time goes in v6:
time: 101 us; the launch traced here: 99.7 us
  blocking collectives  41.4 us (41%)
  starting transfers between devices  23.6 us (23%)
  waiting for transfers between devices  21.5 us (21%)
  Pallas kernels  9.09 us (9%)
  local copies, waits for them, and re-layouts  2.35 us (2%)
    all_to_all x2, blocking collectives, swap(): lax.all_to_all(x, PLANE, split_axis=0, concat_axis=0, axis_index_groups=g...  41.4 us
    ppermute x2, waiting for transfers between devices, mirror(): return lax.ppermute(x, PLANE, pairs)  20.9 us
    all_to_all x2, starting transfers between devices, swap(): lax.all_to_all(x, PLANE, split_axis=0, concat_axis=0, axis_index_groups=g...  11.1 us
    ppermute x2, starting transfers between devices, from_behind(): return lax.ppermute(x, axis, [(i, (i + by) % count) for i in range(count)])  7 us
    ppermute x2, starting transfers between devices, mirror(): return lax.ppermute(x, PLANE, pairs)  5.57 us
    pallas_call x1, Pallas kernels, shards(): pl.pallas_call(backward_kernel, name='backward', out_shape=(jax.ShapeDtyp...  5.07 us
    pallas_call x1, Pallas kernels, shards(): pl.pallas_call(forward_kernel, name='forward', out_shape=(half, half), in...  3.31 us
  transfers between devices with their start and end apart: 6, of which 3 were waited for; matrix products, arithmetic and copies ran while one was open for 3% of the time, Pallas kernels for 9%

profile of v6, /device:TPU:14, one launch (start us, length us, event | category | flops | bytes accessed | tf_op | source)
XLA Modules:
  0.0 99.7 jit_solution(17027423325530868834)
XLA Ops:
  0.6 5.1 %collective-permute-start = (bf16[1,2,256,384]{3,2,1,0:T(8,128)(2,1)}, bf16[1,2,256,384]{3,2,1,0:T(8,128)(2,1)S(1)}, u32[]{:S(2)}, u32[]{:S(2)}) collective-permute-start(bf16[1,2,256,384]{3,2,1,0:T(8,128)(2,1)} %param.7), channel_id=1, source_target_pairs={{0,256},{256,512},{512,768},{768,0},{1,257},{257,513},{513,769},{7... | collective-permute-start | bytes 1179656 | tf_op jit(solution)/shard_map/ppermute | solution.py:18
  5.7 0.7 broadcast_in_dim.17
  6.5 25.7 %all_to_all.20 = bf16[8,24,384]{2,1,0:T(8,128)(2,1)S(1)} all-to-all(bf16[8,24,384]{2,1,0:T(8,128)(2,1)S(1)} %broadcast_in_dim.17), channel_id=1, replica_groups={{0,4,8,12,16,20,24,28},{32,36,40,44,48,52,56,60},{64,68,72,76,80,84,88,..., dimensions={0} | all-to-all | bytes 294912 | tf_op jit(solution)/shard_map/all_to_all | solution.py:33
  32.2 0.9 broadcast_in_dim.18
  33.1 7.6 %all-to-all-start.1 = ((bf16[4,8,24,384]{3,2,1,0:T(8,128)(2,1)}), bf16[4,8,24,384]{3,2,1,0:T(8,128)(2,1)S(1)}, u32[]{:S(2)}, u32[]{:S(2)}) async-start(bf16[4,8,24,384]{3,2,1,0:T(8,128)(2,1)} %broadcast_in_dim.18), calls=%async_computation.1 | async-start | bytes 1179648 | tf_op jit(solution)/shard_map/all_to_all | solution.py:33
  40.6 0.0 collective-permute-done.kv_hbm
  40.6 3.3 %forward.1 = (bf16[4,8,24,384]{3,2,1,0:T(8,128)(2,1)S(1)}, bf16[4,8,24,384]{3,2,1,0:T(8,128)(2,1)S(1)}) custom-call(s32[1,2,2]{2,1,0:T(2,128)} %ids_hbm.3, s32[1,2]{1,0:T(1,128)} %cnt_hbm.3, bf16[1,256,384]{2,1,0:T(8,128)(2,1)} %q_hbm.3, bf16[1,2,256,384]{3,2,1,0:T(8,128)(2,1)S(1)} %collective-permute-done.kv_hbm, bf16[1,256,1536]{2,1,0:T(8,128)(2,1)} %cot_hbm.3), custom_call_target="tpu_custom_call" | custom-call | flops 402653184 | bytes 3145728 | tf_op jit(solution)/shard_map/forward/pallas_call | solution.py:217
  44.0 2.5 %collective-permute-start.3 = (bf16[4,8,24,384]{3,2,1,0:T(8,128)(2,1)S(1)}, bf16[4,8,24,384]{3,2,1,0:T(8,128)(2,1)S(1)}, u32[]{:S(2)}, u32[]{:S(2)}) collective-permute-start(bf16[4,8,24,384]{3,2,1,0:T(8,128)(2,1)S(1)} %get-tuple-element.10), channel_id=1, source_target_pairs={{0,4},{4,0},{8,12},{12,8},{16,20},{20,16},{24,28},{28,24},{32,36},... | collective-permute-start | bytes 1769480 | tf_op jit(solution)/shard_map/ppermute | solution.py:42
  46.4 9.3 %collective-permute-done.3 = bf16[4,8,24,384]{3,2,1,0:T(8,128)(2,1)S(1)} collective-permute-done((bf16[4,8,24,384]{3,2,1,0:T(8,128)(2,1)S(1)}, bf16[4,8,24,384]{3,2,1,0:T(8,128)(2,1)S(1)}, u32[]{:S(2)}, u32[]{:S(2)}) %collective-permute-start.3) | collective-permute-done | bytes 589856 | tf_op jit(solution)/shard_map/ppermute | solution.py:42
  55.7 1.0 add_convert_fusion
  56.7 0.6 all-to-all-done.1.same_hbm
  57.3 3.5 %all-to-all-start.2 = ((bf16[4,8,24,384]{3,2,1,0:T(8,128)(2,1)}), bf16[4,8,24,384]{3,2,1,0:T(8,128)(2,1)S(1)}, u32[]{:S(2)}, u32[]{:S(2)}) async-start(bf16[4,8,24,384]{3,2,1,0:T(8,128)(2,1)} %add_convert_fusion), calls=%async_computation.2 | async-start | bytes 1179648 | tf_op jit(solution)/shard_map/all_to_all | solution.py:33
  60.8 3.1 %collective-permute-start.1 = (bf16[4,8,24,384]{3,2,1,0:T(8,128)(2,1)S(1)}, bf16[4,8,24,384]{3,2,1,0:T(8,128)(2,1)S(1)}, u32[]{:S(2)}, u32[]{:S(2)}) collective-permute-start(bf16[4,8,24,384]{3,2,1,0:T(8,128)(2,1)S(1)} %all-to-all-done.1.same_hbm), channel_id=1, source_target_pairs={{0,32},{32,0},{64,96},{96,64},{128,160},{160,128},{192,224},{224,1... | collective-permute-start | bytes 1769480 | tf_op jit(solution)/shard_map/ppermute | solution.py:42
  63.9 11.6 %collective-permute-done.1.other_hbm = bf16[4,8,24,384]{3,2,1,0:T(8,128)(2,1)S(1)} collective-permute-done((bf16[4,8,24,384]{3,2,1,0:T(8,128)(2,1)S(1)}, bf16[4,8,24,384]{3,2,1,0:T(8,128)(2,1)S(1)}, u32[]{:S(2)}, u32[]{:S(2)}) %collective-permute-start.1) | collective-permute-done | bytes 589856 | tf_op jit(solution)/shard_map/ppermute | solution.py:42
  75.5 5.1 %backward.1 = (bf16[1,256,384]{2,1,0:T(8,128)(2,1)}, bf16[1,2,256,384]{3,2,1,0:T(8,128)(2,1)S(1)}) custom-call(s32[1,2,2]{2,1,0:T(2,128)} %ids_hbm.3, s32[1,2]{1,0:T(1,128)} %cnt_hbm.3, bf16[1,256,384]{2,1,0:T(8,128)(2,1)} %q_hbm.3, bf16[1,2,256,384]{3,2,1,0:T(8,128)(2,1)S(1)} %collective-permute-done.kv_hbm, bf16[1,256,1536]{2,1,0:T(8,128)(2,1)} %cot_hbm.3, ...), custom_call_target="tpu_custom_call" | custom-call | flops 603979776 | bytes 4194304 | tf_op jit(solution)/shard_map/backward/pallas_call | solution.py:240
  80.6 1.9 %collective-permute-start.2 = (bf16[1,2,256,384]{3,2,1,0:T(8,128)(2,1)S(1)}, bf16[1,2,256,384]{3,2,1,0:T(8,128)(2,1)S(1)}, u32[]{:S(2)}, u32[]{:S(2)}) collective-permute-start(bf16[1,2,256,384]{3,2,1,0:T(8,128)(2,1)S(1)} %get-tuple-element.8), channel_id=1, source_target_pairs={{0,768},{256,0},{512,256},{768,512},{1,769},{257,1},{513,257},{769... | collective-permute-start | bytes 1179656 | tf_op jit(solution)/shard_map/ppermute | solution.py:18
  82.5 0.0 all-to-all-done.2.parts_ref
  82.5 0.1 fold.2
  82.6 15.6 %all_to_all.21.parts_ref = bf16[8,24,384]{2,1,0:T(8,128)(2,1)S(1)} all-to-all(bf16[8,24,384]{2,1,0:T(8,128)(2,1)S(1)} %fold.2), channel_id=1, replica_groups={{0,32,64,96,128,160,192,224},{4,36,68,100,132,164,196,228},{8,40,72,104..., dimensions={0} | all-to-all | bytes 294912 | tf_op jit(solution)/shard_map/all_to_all | solution.py:33
  98.3 0.6 fold.3
  98.9 0.0 collective-permute-done.2
  98.9 0.7 copy.10
Async XLA Ops:
  0.6 40.0 %collective-permute-start = (bf16[1,2,256,384]{3,2,1,0:T(8,128)(2,1)}, bf16[1,2,256,384]{3,2,1,0:T(8,128)(2,1)S(1)}, u32[]{:S(2)}, u32[]{:S(2)}) collective-permute-start(bf16[1,2,256,384]{3,2,1,0:T(8,128)(2,1)} %param.7), channel_id=1, source_target_pairs={{0,256},{256,512},{512,768},{768,0},{1,257},{257,513},{513,769},{7... | collective-permute-start | bytes 1179656 | tf_op jit(solution)/shard_map/ppermute | solution.py:18
  33.1 24.3 %all-to-all-start.1 = ((bf16[4,8,24,384]{3,2,1,0:T(8,128)(2,1)}), bf16[4,8,24,384]{3,2,1,0:T(8,128)(2,1)S(1)}, u32[]{:S(2)}, u32[]{:S(2)}) async-start(bf16[4,8,24,384]{3,2,1,0:T(8,128)(2,1)} %broadcast_in_dim.18), calls=%async_computation.1 | async-start | bytes 1179648 | tf_op jit(solution)/shard_map/all_to_all | solution.py:33
  44.0 11.8 %collective-permute-start.3 = (bf16[4,8,24,384]{3,2,1,0:T(8,128)(2,1)S(1)}, bf16[4,8,24,384]{3,2,1,0:T(8,128)(2,1)S(1)}, u32[]{:S(2)}, u32[]{:S(2)}) collective-permute-start(bf16[4,8,24,384]{3,2,1,0:T(8,128)(2,1)S(1)} %get-tuple-element.10), channel_id=1, source_target_pairs={{0,4},{4,0},{8,12},{12,8},{16,20},{20,16},{24,28},{28,24},{32,36},... | collective-permute-start | bytes 1769480 | tf_op jit(solution)/shard_map/ppermute | solution.py:42
  57.3 25.2 %all-to-all-start.2 = ((bf16[4,8,24,384]{3,2,1,0:T(8,128)(2,1)}), bf16[4,8,24,384]{3,2,1,0:T(8,128)(2,1)S(1)}, u32[]{:S(2)}, u32[]{:S(2)}) async-start(bf16[4,8,24,384]{3,2,1,0:T(8,128)(2,1)} %add_convert_fusion), calls=%async_computation.2 | async-start | bytes 1179648 | tf_op jit(solution)/shard_map/all_to_all | solution.py:33
  60.8 14.7 %collective-permute-start.1 = (bf16[4,8,24,384]{3,2,1,0:T(8,128)(2,1)S(1)}, bf16[4,8,24,384]{3,2,1,0:T(8,128)(2,1)S(1)}, u32[]{:S(2)}, u32[]{:S(2)}) collective-permute-start(bf16[4,8,24,384]{3,2,1,0:T(8,128)(2,1)S(1)} %all-to-all-done.1.same_hbm), channel_id=1, source_target_pairs={{0,32},{32,0},{64,96},{96,64},{128,160},{160,128},{192,224},{224,1... | collective-permute-start | bytes 1769480 | tf_op jit(solution)/shard_map/ppermute | solution.py:42
  80.6 18.3 %collective-permute-start.2 = (bf16[1,2,256,384]{3,2,1,0:T(8,128)(2,1)S(1)}, bf16[1,2,256,384]{3,2,1,0:T(8,128)(2,1)S(1)}, u32[]{:S(2)}, u32[]{:S(2)}) collective-permute-start(bf16[1,2,256,384]{3,2,1,0:T(8,128)(2,1)S(1)} %get-tuple-element.8), channel_id=1, source_target_pairs={{0,768},{256,0},{512,256},{768,512},{1,769},{257,1},{513,257},{769... | collective-permute-start | bytes 1179656 | tf_op jit(solution)/shard_map/ppermute | solution.py:18

commit v7 on v5

--- a/solution.py
+++ b/solution.py
@@ -33,16 +33,6 @@
     return lax.all_to_all(
         x, PLANE, split_axis=0, concat_axis=0, axis_index_groups=lines(first), tiled=True
     )
-
-
-def mirror(x, distance):
-    pairs = [(line[i], line[i ^ distance]) for line in lines(False) for i in range(len(line))]
-    return lax.ppermute(x, PLANE, pairs)
-
-
-def gather_slots(near):
-    own = near[None]
-    return [(own, [0])] + [(mirror(own, k), [k]) for k in range(1, len(lines(False)[0]))]
 
 
 def dot(a, b, dims):
@@ -98,9 +88,10 @@
             part_ref[jnp.where(odd, y, z), jnp.where(odd, z, y)] = block
 
 
-def backward_kernel(slots, ids_hbm, cnt_hbm, q_hbm, kv_hbm, cot_hbm, *refs):
-    pieces = refs[: len(slots)]
-    gq_ref, gkv_ref, ids_ref, cnt_ref, q_ref, kv_ref, cot_ref, rows_ref, sem, slot_sem = refs[len(slots) :]
+def backward_kernel(
+    ids_hbm, cnt_hbm, q_hbm, kv_hbm, cot_hbm, far_hbm, gq_ref, gkv_ref,
+    ids_ref, cnt_ref, q_ref, kv_ref, cot_ref, rows_ref, sem, row_sem,
+):
     copies = [
         pltpu.make_async_copy(src, dst, sem.at[i])
         for i, (src, dst) in enumerate(
@@ -110,27 +101,27 @@
     for copy in copies:
         copy.start()
     odd = lax.axis_index("tensor") % 2 == 1
-    placed = []
+    side, _, rows, _ = rows_ref.shape
+    moves = [
+        [
+            pltpu.make_async_copy(
+                far_hbm.at[:, y] if turned else far_hbm.at[y], rows_ref.at[y], row_sem.at[y]
+            )
+            for y in range(side)
+        ]
+        for turned in range(2)
+    ]
     for turned in range(2):
-        place = lax.axis_index(DP[1] if turned else DP[0])
-        moves = []
-        for piece, held in zip(pieces, slots):
-            for i, k in enumerate(held):
-                at = place ^ k
-                target = rows_ref.at[:, at] if turned else rows_ref.at[at]
-                moves.append(pltpu.make_async_copy(piece.at[i], target, slot_sem.at[k]))
-        placed.append(moves)
 
         @pl.when(odd == (turned == 1))
-        def _(moves=moves):
-            for move in moves:
+        def _(turned=turned):
+            for move in moves[turned]:
                 move.start()
 
     tokens, width = q_ref.shape[1:]
     for copy in copies[:4]:
         copy.wait()
     live = live_mask(ids_ref, cnt_ref, tokens, kv_ref.shape[2])
-    side, _, rows, _ = rows_ref.shape
     probs = []
     attns = []
     for h in range(width // HD):
@@ -141,7 +132,7 @@
             dot(prob.astype(jnp.bfloat16), kv_ref[0, 1, :, cols], ((1,), (0,))).astype(jnp.bfloat16)
         )
     copies[4].wait()
-    for move in placed[0]:
+    for move in moves[0]:
         move.wait()
     weight = rows_ref[...].reshape(side * side * rows, width)
     d_attn = dot(cot_ref[0], weight, ((1,), (0,))).astype(jnp.bfloat16)
@@ -199,6 +190,8 @@
 
     used = from_behind(context, "segment", 1)
     near = swap(jnp.broadcast_to(w_out, (nz, rows, width)), True)
+    near, used = lax.optimization_barrier((near, used))
+    far = swap(jnp.broadcast_to(near[None], (ny, nz, rows, width)), False)
     fixed = [pltpu.with_memory_space_constraint(a, pltpu.HBM) for a in (vis_blocks, vis_count, queries)]
     cotan = pltpu.with_memory_space_constraint(grad_out, pltpu.HBM)
 
@@ -218,16 +211,14 @@
     once = fold(swap(part, True), jnp.bfloat16)
     grad_weight = fold(swap(once, False), jnp.float32)[None]
 
-    pieces = gather_slots(near)
-    slots = [k for _, k in pieces]
     grad_q, grad_used = pl.pallas_call(
-        lambda *refs: backward_kernel(slots, *refs),
+        backward_kernel,
         name="backward",
         out_shape=(
             jax.ShapeDtypeStruct(queries.shape, jnp.bfloat16),
             jax.ShapeDtypeStruct(context.shape, jnp.bfloat16),
         ),
-        in_specs=[hbm, hbm, hbm, anywhere, hbm] + [anywhere] * len(pieces),
+        in_specs=[hbm, hbm, hbm, anywhere, hbm] + [anywhere],
         out_specs=(vmem, vmem),
         scratch_shapes=small
         + [
@@ -239,7 +230,7 @@
         cost_estimate=pl.CostEstimate(
             flops=2 * tokens * width * (6 * ctx + model), bytes_accessed=4 << 20, transcendentals=heads * tokens * ctx
         ),
-    )(*fixed, used, cotan, *(a for a, _ in pieces))
+    )(*fixed, used, cotan, far)
     grad_context = from_behind(grad_used, "segment", -1)
     return grad_q, grad_context, grad_weight
 

time: 95.6 us -> 98.8 us (1.033); the launches traced: 94 us -> 98.3 us
  starting transfers between devices: 61.4 us -> 18.2 us
  blocking collectives: 0 us -> 37.4 us
  waiting for transfers between devices: 19.1 us -> 29.6 us
    all_to_all x0 -> x2, blocking collectives: none -> 37.4 us  [swap(): lax.all_to_all(x, PLANE, split_axis=0, concat_axis=0, axis_index_groups=l...]
    ppermute x7 -> x0, starting transfers between devices: 28.6 us -> none  [mirror(): return lax.ppermute(x, PLANE, pairs)]
    all_to_all x3 -> x2, waiting for transfers between devices: 7.69 us -> 29.6 us  [swap(): lax.all_to_all(x, PLANE, split_axis=0, concat_axis=0, axis_index_groups=l...]
    all_to_all x3 -> x2, starting transfers between devices: 25.7 us -> 11.1 us  [swap(): lax.all_to_all(x, PLANE, split_axis=0, concat_axis=0, axis_index_groups=l...]
    ppermute x2, waiting for transfers between devices: 6.75 us -> 0.01 us  [from_behind(): return lax.ppermute(x, axis, [(i, (i + by) % count) for i in range(count)])]
    ppermute x7 -> x0, waiting for transfers between devices: 4.67 us -> none  [mirror(): return lax.ppermute(x, PLANE, pairs)]
    broadcast_in_dim x0 -> x1, local copies, waits for them, and re-layouts: none -> 1.17 us  [shards(): far = swap(jnp.broadcast_to(near[None], (ny, nz, rows, width)), False)]
  transfers between devices with their start and end apart: 12 -> 4, of which waited for: 6 -> 2; matrix products, arithmetic and copies ran while one was open for 1% -> 1% of each run, Pallas kernels for 11% -> 10%
where the time goes in v7:
time: 98.8 us; the launch traced here: 98.3 us
  blocking collectives  37.4 us (38%)
  waiting for transfers between devices  29.6 us (30%)
  starting transfers between devices  18.2 us (18%)
  Pallas kernels  9.88 us (10%)
  local copies, waits for them, and re-layouts  2.65 us (3%)
    all_to_all x2, blocking collectives, swap(): lax.all_to_all(x, PLANE, split_axis=0, concat_axis=0, axis_index_groups=l...  37.4 us
    all_to_all x2, waiting for transfers between devices, swap(): lax.all_to_all(x, PLANE, split_axis=0, concat_axis=0, axis_index_groups=l...  29.6 us
    all_to_all x2, starting transfers between devices, swap(): lax.all_to_all(x, PLANE, split_axis=0, concat_axis=0, axis_index_groups=l...  11.1 us
    ppermute x2, starting transfers between devices, from_behind(): return lax.ppermute(x, axis, [(i, (i + by) % count) for i in range(count)])  7 us
    pallas_call x1, Pallas kernels, shards(): pl.pallas_call(backward_kernel, name='backward', out_shape=(jax.ShapeDtyp...  5.05 us
    pallas_call x1, Pallas kernels, shards(): pl.pallas_call(forward_kernel, name='forward', out_shape=jax.ShapeDtypeSt...  4.03 us
  transfers between devices with their start and end apart: 4, of which 2 were waited for; matrix products, arithmetic and copies ran while one was open for 1% of the time, Pallas kernels for 10%

profile of v7, /device:TPU:14, one launch (start us, length us, event | category | flops | bytes accessed | tf_op | source)
XLA Modules:
  0.0 98.3 jit_solution(4284435895628167583)
XLA Ops:
  0.6 5.1 %collective-permute-start = (bf16[1,2,256,384]{3,2,1,0:T(8,128)(2,1)}, bf16[1,2,256,384]{3,2,1,0:T(8,128)(2,1)S(1)}, u32[]{:S(2)}, u32[]{:S(2)}) collective-permute-start(bf16[1,2,256,384]{3,2,1,0:T(8,128)(2,1)} %param.7), channel_id=1, source_target_pairs={{0,256},{256,512},{512,768},{768,0},{1,257},{257,513},{513,769},{7... | collective-permute-start | bytes 1179656 | tf_op jit(solution)/shard_map/ppermute | solution.py:18
  5.7 0.7 broadcast_in_dim.17
  6.5 25.7 %all_to_all.20 = bf16[8,24,384]{2,1,0:T(8,128)(2,1)S(1)} all-to-all(bf16[8,24,384]{2,1,0:T(8,128)(2,1)S(1)} %broadcast_in_dim.17), channel_id=1, replica_groups={{0,4,8,12,16,20,24,28},{32,36,40,44,48,52,56,60},{64,68,72,76,80,84,88,..., dimensions={0} | all-to-all | bytes 294912 | tf_op jit(solution)/shard_map/all_to_all | solution.py:33
  32.2 0.0 collective-permute-done.kv_hbm
  32.2 1.2 %broadcast_in_dim.18 = bf16[8,8,24,384]{3,2,1,0:T(8,128)(2,1)} broadcast(bf16[8,24,384]{2,1,0:T(8,128)(2,1)S(1)} %all_to_all.20), dimensions={1,2,3} | broadcast | bytes 1327104 | tf_op jit(solution)/shard_map/broadcast_in_dim | solution.py:194
  33.4 7.6 %all-to-all-start.1 = ((bf16[8,8,24,384]{3,2,1,0:T(8,128)(2,1)}), bf16[8,8,24,384]{3,2,1,0:T(8,128)(2,1)S(1)}, u32[]{:S(2)}, u32[]{:S(2)}) async-start(bf16[8,8,24,384]{3,2,1,0:T(8,128)(2,1)} %broadcast_in_dim.18), calls=%async_computation.1 | async-start | bytes 2359296 | tf_op jit(solution)/shard_map/all_to_all | solution.py:33
  41.0 4.0 %forward.1 = bf16[8,8,24,384]{3,2,1,0:T(8,128)(2,1)} custom-call(s32[1,2,2]{2,1,0:T(2,128)} %ids_hbm.3, s32[1,2]{1,0:T(1,128)} %cnt_hbm.3, bf16[1,256,384]{2,1,0:T(8,128)(2,1)} %q_hbm.3, bf16[1,2,256,384]{3,2,1,0:T(8,128)(2,1)S(1)} %collective-permute-done.kv_hbm, bf16[1,256,1536]{2,1,0:T(8,128)(2,1)} %cot_hbm.3), custom_call_target="tpu_custom_call" | custom-call | flops 402653184 | bytes 3145728 | tf_op jit(solution)/shard_map/forward/pallas_call | solution.py:198
  45.0 16.3 %all-to-all-done.1.far_hbm = bf16[8,8,24,384]{3,2,1,0:T(8,128)(2,1)S(1)} async-done(((bf16[8,8,24,384]{3,2,1,0:T(8,128)(2,1)}), bf16[8,8,24,384]{3,2,1,0:T(8,128)(2,1)S(1)}, u32[]{:S(2)}, u32[]{:S(2)}) %all-to-all-start.1) | async-done | bytes 1179680 | tf_op jit(solution)/shard_map/all_to_all | solution.py:33
  61.3 3.6 %all-to-all-start.2 = ((bf16[8,8,24,384]{3,2,1,0:T(8,128)(2,1)}), bf16[8,8,24,384]{3,2,1,0:T(8,128)(2,1)S(1)}, u32[]{:S(2)}, u32[]{:S(2)}) async-start(bf16[8,8,24,384]{3,2,1,0:T(8,128)(2,1)} %forward.1), calls=%async_computation.2 | async-start | bytes 2359296 | tf_op jit(solution)/shard_map/all_to_all | solution.py:33
  64.9 5.1 %backward.1 = (bf16[1,256,384]{2,1,0:T(8,128)(2,1)}, bf16[1,2,256,384]{3,2,1,0:T(8,128)(2,1)S(1)}) custom-call(s32[1,2,2]{2,1,0:T(2,128)} %ids_hbm.3, s32[1,2]{1,0:T(1,128)} %cnt_hbm.3, bf16[1,256,384]{2,1,0:T(8,128)(2,1)} %q_hbm.3, bf16[1,2,256,384]{3,2,1,0:T(8,128)(2,1)S(1)} %collective-permute-done.kv_hbm, bf16[1,256,1536]{2,1,0:T(8,128)(2,1)} %cot_hbm.3, ...), custom_call_target="tpu_custom_call" | custom-call | flops 603979776 | bytes 4194304 | tf_op jit(solution)/shard_map/backward/pallas_call | solution.py:214
  69.9 1.9 %collective-permute-start.1 = (bf16[1,2,256,384]{3,2,1,0:T(8,128)(2,1)S(1)}, bf16[1,2,256,384]{3,2,1,0:T(8,128)(2,1)S(1)}, u32[]{:S(2)}, u32[]{:S(2)}) collective-permute-start(bf16[1,2,256,384]{3,2,1,0:T(8,128)(2,1)S(1)} %get-tuple-element.10), channel_id=1, source_target_pairs={{0,768},{256,0},{512,256},{768,512},{1,769},{257,1},{513,257},{769... | collective-permute-start | bytes 1179656 | tf_op jit(solution)/shard_map/ppermute | solution.py:18
  71.9 13.3 %all-to-all-done.2.parts_ref = bf16[8,8,24,384]{3,2,1,0:T(8,128)(2,1)S(1)} async-done(((bf16[8,8,24,384]{3,2,1,0:T(8,128)(2,1)}), bf16[8,8,24,384]{3,2,1,0:T(8,128)(2,1)S(1)}, u32[]{:S(2)}, u32[]{:S(2)}) %all-to-all-start.2) | async-done | bytes 1179680 | tf_op jit(solution)/shard_map/all_to_all | solution.py:33
  85.2 0.2 fold.2
  85.3 11.6 %all_to_all.21.parts_ref = bf16[8,24,384]{2,1,0:T(8,128)(2,1)S(1)} all-to-all(bf16[8,24,384]{2,1,0:T(8,128)(2,1)S(1)} %fold.2), channel_id=1, replica_groups={{0,32,64,96,128,160,192,224},{4,36,68,100,132,164,196,228},{8,40,72,104..., dimensions={0} | all-to-all | bytes 294912 | tf_op jit(solution)/shard_map/all_to_all | solution.py:33
  97.0 0.6 fold.3
  97.6 0.0 collective-permute-done.1
  97.6 0.7 copy.10
Async XLA Ops:
  0.6 31.6 %collective-permute-start = (bf16[1,2,256,384]{3,2,1,0:T(8,128)(2,1)}, bf16[1,2,256,384]{3,2,1,0:T(8,128)(2,1)S(1)}, u32[]{:S(2)}, u32[]{:S(2)}) collective-permute-start(bf16[1,2,256,384]{3,2,1,0:T(8,128)(2,1)} %param.7), channel_id=1, source_target_pairs={{0,256},{256,512},{512,768},{768,0},{1,257},{257,513},{513,769},{7... | collective-permute-start | bytes 1179656 | tf_op jit(solution)/shard_map/ppermute | solution.py:18
  33.4 27.9 %all-to-all-start.1 = ((bf16[8,8,24,384]{3,2,1,0:T(8,128)(2,1)}), bf16[8,8,24,384]{3,2,1,0:T(8,128)(2,1)S(1)}, u32[]{:S(2)}, u32[]{:S(2)}) async-start(bf16[8,8,24,384]{3,2,1,0:T(8,128)(2,1)} %broadcast_in_dim.18), calls=%async_computation.1 | async-start | bytes 2359296 | tf_op jit(solution)/shard_map/all_to_all | solution.py:33
  61.3 23.8 %all-to-all-start.2 = ((bf16[8,8,24,384]{3,2,1,0:T(8,128)(2,1)}), bf16[8,8,24,384]{3,2,1,0:T(8,128)(2,1)S(1)}, u32[]{:S(2)}, u32[]{:S(2)}) async-start(bf16[8,8,24,384]{3,2,1,0:T(8,128)(2,1)} %forward.1), calls=%async_computation.2 | async-start | bytes 2359296 | tf_op jit(solution)/shard_map/all_to_all | solution.py:33
  69.9 27.7 %collective-permute-start.1 = (bf16[1,2,256,384]{3,2,1,0:T(8,128)(2,1)S(1)}, bf16[1,2,256,384]{3,2,1,0:T(8,128)(2,1)S(1)}, u32[]{:S(2)}, u32[]{:S(2)}) collective-permute-start(bf16[1,2,256,384]{3,2,1,0:T(8,128)(2,1)S(1)} %get-tuple-element.10), channel_id=1, source_target_pairs={{0,768},{256,0},{512,256},{768,512},{1,769},{257,1},{513,257},{769... | collective-permute-start | bytes 1179656 | tf_op jit(solution)/shard_map/ppermute | solution.py:18

commit v8 on v5

--- a/solution.py
+++ b/solution.py
@@ -29,10 +29,8 @@
     return groups
 
 
-def swap(x, first):
-    return lax.all_to_all(
-        x, PLANE, split_axis=0, concat_axis=0, axis_index_groups=lines(first), tiled=True
-    )
+def swap(x, groups):
+    return lax.all_to_all(x, PLANE, split_axis=0, concat_axis=0, axis_index_groups=groups, tiled=True)
 
 
 def mirror(x, distance):
@@ -40,9 +38,9 @@
     return lax.ppermute(x, PLANE, pairs)
 
 
-def gather_slots(near):
-    own = near[None]
-    return [(own, [0])] + [(mirror(own, k), [k]) for k in range(1, len(lines(False)[0]))]
+def pairs_of_lines():
+    alone = lines(True)
+    return [alone[i] + alone[i + 1] for i in range(0, len(alone), 2)]
 
 
 def dot(a, b, dims):
@@ -98,9 +96,9 @@
             part_ref[jnp.where(odd, y, z), jnp.where(odd, z, y)] = block
 
 
-def backward_kernel(slots, ids_hbm, cnt_hbm, q_hbm, kv_hbm, cot_hbm, *refs):
-    pieces = refs[: len(slots)]
-    gq_ref, gkv_ref, ids_ref, cnt_ref, q_ref, kv_ref, cot_ref, rows_ref, sem, slot_sem = refs[len(slots) :]
+def backward_kernel(ids_hbm, cnt_hbm, q_hbm, kv_hbm, cot_hbm, *refs):
+    pieces = refs[:-10]
+    gq_ref, gkv_ref, ids_ref, cnt_ref, q_ref, kv_ref, cot_ref, rows_ref, sem, slot_sem = refs[-10:]
     copies = [
         pltpu.make_async_copy(src, dst, sem.at[i])
         for i, (src, dst) in enumerate(
@@ -112,13 +110,13 @@
     odd = lax.axis_index("tensor") % 2 == 1
     placed = []
     for turned in range(2):
-        place = lax.axis_index(DP[1] if turned else DP[0])
+        place = lax.axis_index(DP[1] if turned else DP[0]) // 2
         moves = []
-        for piece, held in zip(pieces, slots):
-            for i, k in enumerate(held):
-                at = place ^ k
+        for k, piece in enumerate(pieces):
+            for i in range(2):
+                at = 2 * (place ^ k) + i
                 target = rows_ref.at[:, at] if turned else rows_ref.at[at]
-                moves.append(pltpu.make_async_copy(piece.at[i], target, slot_sem.at[k]))
+                moves.append(pltpu.make_async_copy(piece.at[i], target, slot_sem.at[2 * k + i]))
         placed.append(moves)
 
         @pl.when(odd == (turned == 1))
@@ -198,7 +196,7 @@
     ]
 
     used = from_behind(context, "segment", 1)
-    near = swap(jnp.broadcast_to(w_out, (nz, rows, width)), True)
+    near = swap(jnp.broadcast_to(w_out, (2 * nz, rows, width)), pairs_of_lines())
     fixed = [pltpu.with_memory_space_constraint(a, pltpu.HBM) for a in (vis_blocks, vis_count, queries)]
     cotan = pltpu.with_memory_space_constraint(grad_out, pltpu.HBM)
 
@@ -215,13 +213,13 @@
         ),
     )(*fixed, used, cotan)
 
-    once = fold(swap(part, True), jnp.bfloat16)
-    grad_weight = fold(swap(once, False), jnp.float32)[None]
-
-    pieces = gather_slots(near)
-    slots = [k for _, k in pieces]
+    once = fold(swap(part, lines(True)), jnp.bfloat16)
+    grad_weight = fold(swap(once, lines(False)), jnp.float32)[None]
+
+    pair = near.reshape(2, nz, rows, width)
+    pieces = [pair] + [mirror(pair, k) for k in range(2, ny, 2)]
     grad_q, grad_used = pl.pallas_call(
-        lambda *refs: backward_kernel(slots, *refs),
+        backward_kernel,
         name="backward",
         out_shape=(
             jax.ShapeDtypeStruct(queries.shape, jnp.bfloat16),
@@ -239,7 +237,7 @@
         cost_estimate=pl.CostEstimate(
             flops=2 * tokens * width * (6 * ctx + model), bytes_accessed=4 << 20, transcendentals=heads * tokens * ctx
         ),
-    )(*fixed, used, cotan, *(a for a, _ in pieces))
+    )(*fixed, used, cotan, *pieces)
     grad_context = from_behind(grad_used, "segment", -1)
     return grad_q, grad_context, grad_weight
 

time: 95.6 us -> 98.7 us (1.032)
  the two profiles are of different devices: /device:TPU:14 before, /device:TPU:1 now
where the time goes in v8:
time: 98.7 us; the launch traced here: 98.1 us
  starting transfers between devices  56.5 us (57%)
  waiting for transfers between devices  29 us (29%)
  Pallas kernels  9.72 us (10%)
  local copies, waits for them, and re-layouts  2.21 us (2%)
    all_to_all x3, starting transfers between devices, swap(): lax.all_to_all(x, PLANE, split_axis=0, concat_axis=0, axis_index_groups=g...  25.6 us
    ppermute x3, starting transfers between devices, mirror(): return lax.ppermute(x, PLANE, pairs)  24.6 us
    ppermute x3, waiting for transfers between devices, mirror(): return lax.ppermute(x, PLANE, pairs)  13.2 us
    all_to_all x3, waiting for transfers between devices, swap(): lax.all_to_all(x, PLANE, split_axis=0, concat_axis=0, axis_index_groups=g...  8.4 us
    ppermute x2, waiting for transfers between devices, from_behind(): return lax.ppermute(x, axis, [(i, (i + by) % count) for i in range(count)])  7.4 us
    ppermute x2, starting transfers between devices, from_behind(): return lax.ppermute(x, axis, [(i, (i + by) % count) for i in range(count)])  6.25 us
    pallas_call x1, Pallas kernels, shards(): pl.pallas_call(backward_kernel, name='backward', out_shape=(jax.ShapeDtyp...  4.23 us
    pallas_call x1, Pallas kernels, shards(): pl.pallas_call(forward_kernel, name='forward', out_shape=jax.ShapeDtypeSt...  4.03 us
  transfers between devices with their start and end apart: 8, of which 4 were waited for; matrix products, arithmetic and copies ran while one was open for 0% of the time, Pallas kernels for 9%

profile of v8, /device:TPU:1, one launch (start us, length us, event | category | flops | bytes accessed | tf_op | source)
XLA Modules:
  0.0 98.1 jit_solution(7368821195826695934)
XLA Ops:
  0.6 1.5 %broadcast_in_dim.11 = bf16[16,24,384]{2,1,0:T(8,128)(2,1)} broadcast(bf16[24,384]{1,0:T(8,128)(2,1)} %bitcast.8), dimensions={1,2} | broadcast | bytes 313344 | tf_op jit(solution)/shard_map/broadcast_in_dim | solution.py:199
  2.1 10.9 %all-to-all-start = ((bf16[16,24,384]{2,1,0:T(8,128)(2,1)}), bf16[16,24,384]{2,1,0:T(8,128)(2,1)S(1)}, u32[]{:S(2)}, u32[]{:S(2)}) async-start(bf16[16,24,384]{2,1,0:T(8,128)(2,1)} %broadcast_in_dim.11), calls=%async_computation | async-start | bytes 589824 | tf_op jit(solution)/shard_map/all_to_all | solution.py:33
  13.0 3.1 %collective-permute-start = (bf16[1,2,256,384]{3,2,1,0:T(8,128)(2,1)}, bf16[1,2,256,384]{3,2,1,0:T(8,128)(2,1)S(1)}, u32[]{:S(2)}, u32[]{:S(2)}) collective-permute-start(bf16[1,2,256,384]{3,2,1,0:T(8,128)(2,1)} %param.7), channel_id=1, source_target_pairs={{0,256},{256,512},{512,768},{768,0},{1,257},{257,513},{513,769},{7... | collective-permute-start | bytes 1179656 | tf_op jit(solution)/shard_map/ppermute | solution.py:18
  16.2 7.4 %collective-permute-done.kv_hbm = bf16[1,2,256,384]{3,2,1,0:T(8,128)(2,1)S(1)} collective-permute-done((bf16[1,2,256,384]{3,2,1,0:T(8,128)(2,1)}, bf16[1,2,256,384]{3,2,1,0:T(8,128)(2,1)S(1)}, u32[]{:S(2)}, u32[]{:S(2)}) %collective-permute-start) | collective-permute-done | bytes 393248 | tf_op jit(solution)/shard_map/ppermute | solution.py:18
  23.6 4.0 %forward.1 = bf16[8,8,24,384]{3,2,1,0:T(8,128)(2,1)} custom-call(s32[1,2,2]{2,1,0:T(2,128)} %ids_hbm.3, s32[1,2]{1,0:T(1,128)} %cnt_hbm.3, bf16[1,256,384]{2,1,0:T(8,128)(2,1)} %q_hbm.3, bf16[1,2,256,384]{3,2,1,0:T(8,128)(2,1)S(1)} %collective-permute-done.kv_hbm, bf16[1,256,1536]{2,1,0:T(8,128)(2,1)} %cot_hbm.3), custom_call_target="tpu_custom_call" | custom-call | flops 402653184 | bytes 3145728 | tf_op jit(solution)/shard_map/forward/pallas_call | solution.py:203
  27.6 0.0 all-to-all-done
  27.6 6.6 %all-to-all-start.1 = ((bf16[8,8,24,384]{3,2,1,0:T(8,128)(2,1)}), bf16[8,8,24,384]{3,2,1,0:T(8,128)(2,1)S(1)}, u32[]{:S(2)}, u32[]{:S(2)}) async-start(bf16[8,8,24,384]{3,2,1,0:T(8,128)(2,1)} %forward.1), calls=%async_computation.1 | async-start | bytes 2359296 | tf_op jit(solution)/shard_map/all_to_all | solution.py:33
  34.2 18.7 %collective-permute-start.3 = (bf16[2,8,24,384]{3,2,1,0:T(8,128)(2,1)S(1)}, bf16[2,8,24,384]{3,2,1,0:T(8,128)(2,1)S(1)}, u32[]{:S(2)}, u32[]{:S(2)}) collective-permute-start(bf16[2,8,24,384]{3,2,1,0:T(8,128)(2,1)S(1)} %bitcast.3), channel_id=1, source_target_pairs={{0,192},{32,224},{64,128},{96,160},{128,64},{160,96},{192,0},{224,... | collective-permute-start | bytes 884744 | tf_op jit(solution)/shard_map/ppermute | solution.py:38
  52.8 1.9 %collective-permute-start.2 = (bf16[2,8,24,384]{3,2,1,0:T(8,128)(2,1)S(1)}, bf16[2,8,24,384]{3,2,1,0:T(8,128)(2,1)S(1)}, u32[]{:S(2)}, u32[]{:S(2)}) collective-permute-start(bf16[2,8,24,384]{3,2,1,0:T(8,128)(2,1)S(1)} %bitcast.4), channel_id=1, source_target_pairs={{0,128},{32,160},{64,192},{96,224},{128,0},{160,32},{192,64},{224,... | collective-permute-start | bytes 884744 | tf_op jit(solution)/shard_map/ppermute | solution.py:38
  54.8 4.0 %collective-permute-start.1 = (bf16[2,8,24,384]{3,2,1,0:T(8,128)(2,1)S(1)}, bf16[2,8,24,384]{3,2,1,0:T(8,128)(2,1)S(1)}, u32[]{:S(2)}, u32[]{:S(2)}) collective-permute-start(bf16[2,8,24,384]{3,2,1,0:T(8,128)(2,1)S(1)} %bitcast.5), channel_id=1, source_target_pairs={{0,64},{32,96},{64,0},{96,32},{128,192},{160,224},{192,128},{224,1... | collective-permute-start | bytes 884744 | tf_op jit(solution)/shard_map/ppermute | solution.py:38
  58.8 12.3 %collective-permute-done.3.refs_3_ = bf16[2,8,24,384]{3,2,1,0:T(8,128)(2,1)S(1)} collective-permute-done((bf16[2,8,24,384]{3,2,1,0:T(8,128)(2,1)S(1)}, bf16[2,8,24,384]{3,2,1,0:T(8,128)(2,1)S(1)}, u32[]{:S(2)}, u32[]{:S(2)}) %collective-permute-start.3) | collective-permute-done | bytes 294944 | tf_op jit(solution)/shard_map/ppermute | solution.py:38
  71.0 0.0 collective-permute-done.2.refs_2_
  71.0 0.9 collective-permute-done.1.refs_1_
  72.0 4.2 %backward.1 = (bf16[1,256,384]{2,1,0:T(8,128)(2,1)}, bf16[1,2,256,384]{3,2,1,0:T(8,128)(2,1)S(1)}) custom-call(s32[1,2,2]{2,1,0:T(2,128)} %ids_hbm.3, s32[1,2]{1,0:T(1,128)} %cnt_hbm.3, bf16[1,256,384]{2,1,0:T(8,128)(2,1)} %q_hbm.3, bf16[1,2,256,384]{3,2,1,0:T(8,128)(2,1)S(1)} %collective-permute-done.kv_hbm, bf16[1,256,1536]{2,1,0:T(8,128)(2,1)} %cot_hbm.3, ...), custom_call_target="tpu_custom_call" | custom-call | flops 603979776 | bytes 4194304 | tf_op jit(solution)/shard_map/backward/pallas_call | solution.py:221
  76.2 3.1 %collective-permute-start.4 = (bf16[1,2,256,384]{3,2,1,0:T(8,128)(2,1)S(1)}, bf16[1,2,256,384]{3,2,1,0:T(8,128)(2,1)S(1)}, u32[]{:S(2)}, u32[]{:S(2)}) collective-permute-start(bf16[1,2,256,384]{3,2,1,0:T(8,128)(2,1)S(1)} %get-tuple-element.6), channel_id=1, source_target_pairs={{0,768},{256,0},{512,256},{768,512},{1,769},{257,1},{513,257},{769... | collective-permute-start | bytes 1179656 | tf_op jit(solution)/shard_map/ppermute | solution.py:18
  79.4 0.0 all-to-all-done.1.parts_ref
  79.4 0.8 fold.2
  80.2 8.2 %all-to-all-start.2 = ((bf16[8,24,384]{2,1,0:T(8,128)(2,1)}), bf16[8,24,384]{2,1,0:T(8,128)(2,1)S(1)}, u32[]{:S(2)}, u32[]{:S(2)}) async-start(bf16[8,24,384]{2,1,0:T(8,128)(2,1)} %fold.2), calls=%async_computation.2 | async-start | bytes 294912 | tf_op jit(solution)/shard_map/all_to_all | solution.py:33
  88.3 0.0 collective-permute-done.4
  88.4 8.4 %all-to-all-done.2.parts_ref = bf16[8,24,384]{2,1,0:T(8,128)(2,1)S(1)} async-done(((bf16[8,24,384]{2,1,0:T(8,128)(2,1)}), bf16[8,24,384]{2,1,0:T(8,128)(2,1)S(1)}, u32[]{:S(2)}, u32[]{:S(2)}) %all-to-all-start.2) | async-done | bytes 147488 | tf_op jit(solution)/shard_map/all_to_all | solution.py:33
  96.7 0.6 fold.3
  97.4 0.7 copy.10
Async XLA Ops:
  2.1 25.5 %all-to-all-start = ((bf16[16,24,384]{2,1,0:T(8,128)(2,1)}), bf16[16,24,384]{2,1,0:T(8,128)(2,1)S(1)}, u32[]{:S(2)}, u32[]{:S(2)}) async-start(bf16[16,24,384]{2,1,0:T(8,128)(2,1)} %broadcast_in_dim.11), calls=%async_computation | async-start | bytes 589824 | tf_op jit(solution)/shard_map/all_to_all | solution.py:33
  13.0 10.5 %collective-permute-start = (bf16[1,2,256,384]{3,2,1,0:T(8,128)(2,1)}, bf16[1,2,256,384]{3,2,1,0:T(8,128)(2,1)S(1)}, u32[]{:S(2)}, u32[]{:S(2)}) collective-permute-start(bf16[1,2,256,384]{3,2,1,0:T(8,128)(2,1)} %param.7), channel_id=1, source_target_pairs={{0,256},{256,512},{512,768},{768,0},{1,257},{257,513},{513,769},{7... | collective-permute-start | bytes 1179656 | tf_op jit(solution)/shard_map/ppermute | solution.py:18
  27.6 51.7 %all-to-all-start.1 = ((bf16[8,8,24,384]{3,2,1,0:T(8,128)(2,1)}), bf16[8,8,24,384]{3,2,1,0:T(8,128)(2,1)S(1)}, u32[]{:S(2)}, u32[]{:S(2)}) async-start(bf16[8,8,24,384]{3,2,1,0:T(8,128)(2,1)} %forward.1), calls=%async_computation.1 | async-start | bytes 2359296 | tf_op jit(solution)/shard_map/all_to_all | solution.py:33
  34.2 36.9 %collective-permute-start.3 = (bf16[2,8,24,384]{3,2,1,0:T(8,128)(2,1)S(1)}, bf16[2,8,24,384]{3,2,1,0:T(8,128)(2,1)S(1)}, u32[]{:S(2)}, u32[]{:S(2)}) collective-permute-start(bf16[2,8,24,384]{3,2,1,0:T(8,128)(2,1)S(1)} %bitcast.3), channel_id=1, source_target_pairs={{0,192},{32,224},{64,128},{96,160},{128,64},{160,96},{192,0},{224,... | collective-permute-start | bytes 884744 | tf_op jit(solution)/shard_map/ppermute | solution.py:38
  52.8 18.2 %collective-permute-start.2 = (bf16[2,8,24,384]{3,2,1,0:T(8,128)(2,1)S(1)}, bf16[2,8,24,384]{3,2,1,0:T(8,128)(2,1)S(1)}, u32[]{:S(2)}, u32[]{:S(2)}) collective-permute-start(bf16[2,8,24,384]{3,2,1,0:T(8,128)(2,1)S(1)} %bitcast.4), channel_id=1, source_target_pairs={{0,128},{32,160},{64,192},{96,224},{128,0},{160,32},{192,64},{224,... | collective-permute-start | bytes 884744 | tf_op jit(solution)/shard_map/ppermute | solution.py:38
  54.8 17.2 %collective-permute-start.1 = (bf16[2,8,24,384]{3,2,1,0:T(8,128)(2,1)S(1)}, bf16[2,8,24,384]{3,2,1,0:T(8,128)(2,1)S(1)}, u32[]{:S(2)}, u32[]{:S(2)}) collective-permute-start(bf16[2,8,24,384]{3,2,1,0:T(8,128)(2,1)S(1)} %bitcast.5), channel_id=1, source_target_pairs={{0,64},{32,96},{64,0},{96,32},{128,192},{160,224},{192,128},{224,1... | collective-permute-start | bytes 884744 | tf_op jit(solution)/shard_map/ppermute | solution.py:38
  76.2 12.1 %collective-permute-start.4 = (bf16[1,2,256,384]{3,2,1,0:T(8,128)(2,1)S(1)}, bf16[1,2,256,384]{3,2,1,0:T(8,128)(2,1)S(1)}, u32[]{:S(2)}, u32[]{:S(2)}) collective-permute-start(bf16[1,2,256,384]{3,2,1,0:T(8,128)(2,1)S(1)} %get-tuple-element.6), channel_id=1, source_target_pairs={{0,768},{256,0},{512,256},{768,512},{1,769},{257,1},{513,257},{769... | collective-permute-start | bytes 1179656 | tf_op jit(solution)/shard_map/ppermute | solution.py:18
  80.2 16.6 %all-to-all-start.2 = ((bf16[8,24,384]{2,1,0:T(8,128)(2,1)}), bf16[8,24,384]{2,1,0:T(8,128)(2,1)S(1)}, u32[]{:S(2)}, u32[]{:S(2)}) async-start(bf16[8,24,384]{2,1,0:T(8,128)(2,1)} %fold.2), calls=%async_computation.2 | async-start | bytes 294912 | tf_op jit(solution)/shard_map/all_to_all | solution.py:33

commit v9 on v7

--- a/solution.py
+++ b/solution.py
@@ -190,8 +190,6 @@
 
     used = from_behind(context, "segment", 1)
     near = swap(jnp.broadcast_to(w_out, (nz, rows, width)), True)
-    near, used = lax.optimization_barrier((near, used))
-    far = swap(jnp.broadcast_to(near[None], (ny, nz, rows, width)), False)
     fixed = [pltpu.with_memory_space_constraint(a, pltpu.HBM) for a in (vis_blocks, vis_count, queries)]
     cotan = pltpu.with_memory_space_constraint(grad_out, pltpu.HBM)
 
@@ -211,6 +209,7 @@
     once = fold(swap(part, True), jnp.bfloat16)
     grad_weight = fold(swap(once, False), jnp.float32)[None]
 
+    far = swap(jnp.broadcast_to(near[None], (ny, nz, rows, width)), False)
     grad_q, grad_used = pl.pallas_call(
         backward_kernel,
         name="backward",

time: 98.8 us -> 95.4 us (0.966)
  blocking collectives: 37.4 us -> 25.7 us
  starting transfers between devices: 18.2 us -> 23.1 us
  waiting for transfers between devices: 29.6 us -> 32.2 us
    all_to_all x2 -> x1, blocking collectives: 37.4 us -> 25.7 us  [swap(): lax.all_to_all(x, PLANE, split_axis=0, concat_axis=0, axis_index_groups=l...]
    ppermute x2, waiting for transfers between devices: 0.01 us -> 6.65 us  [from_behind(): return lax.ppermute(x, axis, [(i, (i + by) % count) for i in range(count)])]
    all_to_all x2 -> x3, waiting for transfers between devices: 29.6 us -> 25.6 us  [swap(): lax.all_to_all(x, PLANE, split_axis=0, concat_axis=0, axis_index_groups=l...]
    all_to_all x2 -> x3, starting transfers between devices: 11.1 us -> 14.6 us  [swap(): lax.all_to_all(x, PLANE, split_axis=0, concat_axis=0, axis_index_groups=l...]
    ppermute x2, starting transfers between devices: 7 us -> 8.43 us  [from_behind(): return lax.ppermute(x, axis, [(i, (i + by) % count) for i in range(count)])]
  transfers between devices with their start and end apart: 4 -> 5, of which waited for: 2 -> 4; matrix products, arithmetic and copies ran while one was open for 1% -> 0% of each run, Pallas kernels for 10% -> 10%
where the time goes in v9:
time: 95.4 us; the launch traced here: 94.9 us
  waiting for transfers between devices  32.2 us (34%)
  blocking collectives  25.7 us (27%)
  starting transfers between devices  23.1 us (24%)
  Pallas kernels  10.6 us (11%)
  local copies, waits for them, and re-layouts  2.66 us (3%)
    all_to_all x1, blocking collectives, swap(): lax.all_to_all(x, PLANE, split_axis=0, concat_axis=0, axis_index_groups=l...  25.7 us
    all_to_all x3, waiting for transfers between devices, swap(): lax.all_to_all(x, PLANE, split_axis=0, concat_axis=0, axis_index_groups=l...  25.6 us
    all_to_all x3, starting transfers between devices, swap(): lax.all_to_all(x, PLANE, split_axis=0, concat_axis=0, axis_index_groups=l...  14.6 us
    ppermute x2, starting transfers between devices, from_behind(): return lax.ppermute(x, axis, [(i, (i + by) % count) for i in range(count)])  8.43 us
    ppermute x2, waiting for transfers between devices, from_behind(): return lax.ppermute(x, axis, [(i, (i + by) % count) for i in range(count)])  6.65 us
    pallas_call x1, Pallas kernels, shards(): pl.pallas_call(backward_kernel, name='backward', out_shape=(jax.ShapeDtyp...  5.05 us
    pallas_call x1, Pallas kernels, shards(): pl.pallas_call(forward_kernel, name='forward', out_shape=jax.ShapeDtypeSt...  4.05 us
  transfers between devices with their start and end apart: 5, of which 4 were waited for; matrix products, arithmetic and copies ran while one was open for 0% of the time, Pallas kernels for 10%

profile of v9, /device:TPU:14, one launch (start us, length us, event | category | flops | bytes accessed | tf_op | source)
XLA Modules:
  0.0 94.9 jit_solution(8013555614708277075)
XLA Ops:
  0.6 0.7 broadcast_in_dim.17
  1.4 25.7 %all_to_all.20 = bf16[8,24,384]{2,1,0:T(8,128)(2,1)S(1)} all-to-all(bf16[8,24,384]{2,1,0:T(8,128)(2,1)S(1)} %broadcast_in_dim.17), channel_id=1, replica_groups={{0,4,8,12,16,20,24,28},{32,36,40,44,48,52,56,60},{64,68,72,76,80,84,88,..., dimensions={0} | all-to-all | bytes 294912 | tf_op jit(solution)/shard_map/all_to_all | solution.py:33
  27.1 1.2 %broadcast_in_dim.18 = bf16[8,8,24,384]{3,2,1,0:T(8,128)(2,1)} broadcast(bf16[8,24,384]{2,1,0:T(8,128)(2,1)S(1)} %all_to_all.20), dimensions={1,2,3} | broadcast | bytes 1327104 | tf_op jit(solution)/shard_map/broadcast_in_dim | solution.py:212
  28.3 0.0 copy-start
  28.3 7.7 %all-to-all-start.1 = ((bf16[8,8,24,384]{3,2,1,0:T(8,128)(2,1)}), bf16[8,8,24,384]{3,2,1,0:T(8,128)(2,1)S(1)}, u32[]{:S(2)}, u32[]{:S(2)}) async-start(bf16[8,8,24,384]{3,2,1,0:T(8,128)(2,1)} %broadcast_in_dim.18), calls=%async_computation.1 | async-start | bytes 2359296 | tf_op jit(solution)/shard_map/all_to_all | solution.py:33
  36.0 0.0 copy-done
  36.0 5.1 %collective-permute-start = (bf16[1,2,256,384]{3,2,1,0:T(8,128)(2,1)S(1)}, bf16[1,2,256,384]{3,2,1,0:T(8,128)(2,1)S(1)}, u32[]{:S(2)}, u32[]{:S(2)}) collective-permute-start(bf16[1,2,256,384]{3,2,1,0:T(8,128)(2,1)S(1)} %copy-done), channel_id=1, source_target_pairs={{0,256},{256,512},{512,768},{768,0},{1,257},{257,513},{513,769},{7... | collective-permute-start | bytes 1179656 | tf_op jit(solution)/shard_map/ppermute | solution.py:18
  41.1 6.6 %collective-permute-done.kv_hbm = bf16[1,2,256,384]{3,2,1,0:T(8,128)(2,1)S(1)} collective-permute-done((bf16[1,2,256,384]{3,2,1,0:T(8,128)(2,1)S(1)}, bf16[1,2,256,384]{3,2,1,0:T(8,128)(2,1)S(1)}, u32[]{:S(2)}, u32[]{:S(2)}) %collective-permute-start) | collective-permute-done | bytes 393248 | tf_op jit(solution)/shard_map/ppermute | solution.py:18
  47.7 4.1 %forward.1 = bf16[8,8,24,384]{3,2,1,0:T(8,128)(2,1)} custom-call(s32[1,2,2]{2,1,0:T(2,128)} %ids_hbm.3, s32[1,2]{1,0:T(1,128)} %cnt_hbm.3, bf16[1,256,384]{2,1,0:T(8,128)(2,1)} %q_hbm.3, bf16[1,2,256,384]{3,2,1,0:T(8,128)(2,1)S(1)} %collective-permute-done.kv_hbm, bf16[1,256,1536]{2,1,0:T(8,128)(2,1)} %cot_hbm.3), custom_call_target="tpu_custom_call" | custom-call | flops 402653184 | bytes 3145728 | tf_op jit(solution)/shard_map/forward/pallas_call | solution.py:196
  51.8 4.6 %all-to-all-done.1.far_hbm = bf16[8,8,24,384]{3,2,1,0:T(8,128)(2,1)S(1)} async-done(((bf16[8,8,24,384]{3,2,1,0:T(8,128)(2,1)}), bf16[8,8,24,384]{3,2,1,0:T(8,128)(2,1)S(1)}, u32[]{:S(2)}, u32[]{:S(2)}) %all-to-all-start.1) | async-done | bytes 1179680 | tf_op jit(solution)/shard_map/all_to_all | solution.py:33
  56.3 3.6 %all-to-all-start.2 = ((bf16[8,8,24,384]{3,2,1,0:T(8,128)(2,1)}), bf16[8,8,24,384]{3,2,1,0:T(8,128)(2,1)S(1)}, u32[]{:S(2)}, u32[]{:S(2)}) async-start(bf16[8,8,24,384]{3,2,1,0:T(8,128)(2,1)} %forward.1), calls=%async_computation.2 | async-start | bytes 2359296 | tf_op jit(solution)/shard_map/all_to_all | solution.py:33
  59.9 5.1 %backward.1 = (bf16[1,256,384]{2,1,0:T(8,128)(2,1)}, bf16[1,2,256,384]{3,2,1,0:T(8,128)(2,1)S(1)}) custom-call(s32[1,2,2]{2,1,0:T(2,128)} %ids_hbm.3, s32[1,2]{1,0:T(1,128)} %cnt_hbm.3, bf16[1,256,384]{2,1,0:T(8,128)(2,1)} %q_hbm.3, bf16[1,2,256,384]{3,2,1,0:T(8,128)(2,1)S(1)} %collective-permute-done.kv_hbm, bf16[1,256,1536]{2,1,0:T(8,128)(2,1)} %cot_hbm.3, ...), custom_call_target="tpu_custom_call" | custom-call | flops 603979776 | bytes 4194304 | tf_op jit(solution)/shard_map/backward/pallas_call | solution.py:213
  65.0 3.3 %collective-permute-start.1 = (bf16[1,2,256,384]{3,2,1,0:T(8,128)(2,1)S(1)}, bf16[1,2,256,384]{3,2,1,0:T(8,128)(2,1)S(1)}, u32[]{:S(2)}, u32[]{:S(2)}) collective-permute-start(bf16[1,2,256,384]{3,2,1,0:T(8,128)(2,1)S(1)} %get-tuple-element.6), channel_id=1, source_target_pairs={{0,768},{256,0},{512,256},{768,512},{1,769},{257,1},{513,257},{769... | collective-permute-start | bytes 1179656 | tf_op jit(solution)/shard_map/ppermute | solution.py:18
  68.3 11.9 %all-to-all-done.2.parts_ref = bf16[8,8,24,384]{3,2,1,0:T(8,128)(2,1)S(1)} async-done(((bf16[8,8,24,384]{3,2,1,0:T(8,128)(2,1)}), bf16[8,8,24,384]{3,2,1,0:T(8,128)(2,1)S(1)}, u32[]{:S(2)}, u32[]{:S(2)}) %all-to-all-start.2) | async-done | bytes 1179680 | tf_op jit(solution)/shard_map/all_to_all | solution.py:33
  80.2 0.8 fold.2
  81.0 3.4 %all-to-all-start.3 = ((bf16[8,24,384]{2,1,0:T(8,128)(2,1)}), bf16[8,24,384]{2,1,0:T(8,128)(2,1)S(1)}, u32[]{:S(2)}, u32[]{:S(2)}) async-start(bf16[8,24,384]{2,1,0:T(8,128)(2,1)} %fold.2), calls=%async_computation.3 | async-start | bytes 294912 | tf_op jit(solution)/shard_map/all_to_all | solution.py:33
  84.4 0.0 collective-permute-done.1
  84.4 9.2 %all-to-all-done.3.parts_ref = bf16[8,24,384]{2,1,0:T(8,128)(2,1)S(1)} async-done(((bf16[8,24,384]{2,1,0:T(8,128)(2,1)}), bf16[8,24,384]{2,1,0:T(8,128)(2,1)S(1)}, u32[]{:S(2)}, u32[]{:S(2)}) %all-to-all-start.3) | async-done | bytes 147488 | tf_op jit(solution)/shard_map/all_to_all | solution.py:33
  93.6 0.6 fold.3
  94.2 0.7 copy.10
Async XLA Ops:
  28.3 7.7 %copy-start = (bf16[1,2,256,384]{3,2,1,0:T(8,128)(2,1)S(1)}, bf16[1,2,256,384]{3,2,1,0:T(8,128)(2,1)}, u32[]{:S(2)}) copy-start(bf16[1,2,256,384]{3,2,1,0:T(8,128)(2,1)} %param.7) | copy-start | bytes 1179652
  28.3 28.1 %all-to-all-start.1 = ((bf16[8,8,24,384]{3,2,1,0:T(8,128)(2,1)}), bf16[8,8,24,384]{3,2,1,0:T(8,128)(2,1)S(1)}, u32[]{:S(2)}, u32[]{:S(2)}) async-start(bf16[8,8,24,384]{3,2,1,0:T(8,128)(2,1)} %broadcast_in_dim.18), calls=%async_computation.1 | async-start | bytes 2359296 | tf_op jit(solution)/shard_map/all_to_all | solution.py:33
  36.0 11.7 %collective-permute-start = (bf16[1,2,256,384]{3,2,1,0:T(8,128)(2,1)S(1)}, bf16[1,2,256,384]{3,2,1,0:T(8,128)(2,1)S(1)}, u32[]{:S(2)}, u32[]{:S(2)}) collective-permute-start(bf16[1,2,256,384]{3,2,1,0:T(8,128)(2,1)S(1)} %copy-done), channel_id=1, source_target_pairs={{0,256},{256,512},{512,768},{768,0},{1,257},{257,513},{513,769},{7... | collective-permute-start | bytes 1179656 | tf_op jit(solution)/shard_map/ppermute | solution.py:18
  56.3 23.8 %all-to-all-start.2 = ((bf16[8,8,24,384]{3,2,1,0:T(8,128)(2,1)}), bf16[8,8,24,384]{3,2,1,0:T(8,128)(2,1)S(1)}, u32[]{:S(2)}, u32[]{:S(2)}) async-start(bf16[8,8,24,384]{3,2,1,0:T(8,128)(2,1)} %forward.1), calls=%async_computation.2 | async-start | bytes 2359296 | tf_op jit(solution)/shard_map/all_to_all | solution.py:33
  65.0 19.4 %collective-permute-start.1 = (bf16[1,2,256,384]{3,2,1,0:T(8,128)(2,1)S(1)}, bf16[1,2,256,384]{3,2,1,0:T(8,128)(2,1)S(1)}, u32[]{:S(2)}, u32[]{:S(2)}) collective-permute-start(bf16[1,2,256,384]{3,2,1,0:T(8,128)(2,1)S(1)} %get-tuple-element.6), channel_id=1, source_target_pairs={{0,768},{256,0},{512,256},{768,512},{1,769},{257,1},{513,257},{769... | collective-permute-start | bytes 1179656 | tf_op jit(solution)/shard_map/ppermute | solution.py:18
  81.0 12.6 %all-to-all-start.3 = ((bf16[8,24,384]{2,1,0:T(8,128)(2,1)}), bf16[8,24,384]{2,1,0:T(8,128)(2,1)S(1)}, u32[]{:S(2)}, u32[]{:S(2)}) async-start(bf16[8,24,384]{2,1,0:T(8,128)(2,1)} %fold.2), calls=%async_computation.3 | async-start | bytes 294912 | tf_op jit(solution)/shard_map/all_to_all | solution.py:33

commit v10 on v9

--- a/solution.py
+++ b/solution.py
@@ -190,6 +190,7 @@
 
     used = from_behind(context, "segment", 1)
     near = swap(jnp.broadcast_to(w_out, (nz, rows, width)), True)
+    used, _ = lax.optimization_barrier((used, near))
     fixed = [pltpu.with_memory_space_constraint(a, pltpu.HBM) for a in (vis_blocks, vis_count, queries)]
     cotan = pltpu.with_memory_space_constraint(grad_out, pltpu.HBM)
 

time: 95.4 us -> 93.8 us (0.983)
  blocking collectives: 25.7 us -> 37.4 us
  waiting for transfers between devices: 32.2 us -> 23.1 us
  starting transfers between devices: 23.1 us -> 19.7 us
    all_to_all x1 -> x2, blocking collectives: 25.7 us -> 37.4 us  [swap(): lax.all_to_all(x, PLANE, split_axis=0, concat_axis=0, axis_index_groups=l...]
    all_to_all x3 -> x2, waiting for transfers between devices: 25.6 us -> 16.4 us  [swap(): lax.all_to_all(x, PLANE, split_axis=0, concat_axis=0, axis_index_groups=l...]
    all_to_all x3 -> x2, starting transfers between devices: 14.6 us -> 11.3 us  [swap(): lax.all_to_all(x, PLANE, split_axis=0, concat_axis=0, axis_index_groups=l...]
  transfers between devices with their start and end apart: 5 -> 4, of which waited for: 4 -> 3; matrix products, arithmetic and copies ran while one was open for 0% -> 0% of each run, Pallas kernels for 10% -> 11%
where the time goes in v10:
time: 93.8 us; the launch traced here: 93.4 us
  blocking collectives  37.4 us (40%)
  waiting for transfers between devices  23.1 us (25%)
  starting transfers between devices  19.7 us (21%)
  Pallas kernels  9.9 us (11%)
  local copies, waits for them, and re-layouts  2.65 us (3%)
    all_to_all x2, blocking collectives, swap(): lax.all_to_all(x, PLANE, split_axis=0, concat_axis=0, axis_index_groups=l...  37.4 us
    all_to_all x2, waiting for transfers between devices, swap(): lax.all_to_all(x, PLANE, split_axis=0, concat_axis=0, axis_index_groups=l...  16.4 us
    all_to_all x2, starting transfers between devices, swap(): lax.all_to_all(x, PLANE, split_axis=0, concat_axis=0, axis_index_groups=l...  11.3 us
    ppermute x2, starting transfers between devices, from_behind(): return lax.ppermute(x, axis, [(i, (i + by) % count) for i in range(count)])  8.42 us
    ppermute x2, waiting for transfers between devices, from_behind(): return lax.ppermute(x, axis, [(i, (i + by) % count) for i in range(count)])  6.65 us
    pallas_call x1, Pallas kernels, shards(): pl.pallas_call(backward_kernel, name='backward', out_shape=(jax.ShapeDtyp...  5.06 us
    pallas_call x1, Pallas kernels, shards(): pl.pallas_call(forward_kernel, name='forward', out_shape=jax.ShapeDtypeSt...  4.04 us
  transfers between devices with their start and end apart: 4, of which 3 were waited for; matrix products, arithmetic and copies ran while one was open for 0% of the time, Pallas kernels for 11%

profile of v10, /device:TPU:14, one launch (start us, length us, event | category | flops | bytes accessed | tf_op | source)
XLA Modules:
  0.0 93.4 jit_solution(5807040206082774571)
XLA Ops:
  0.6 0.7 broadcast_in_dim.17
  1.4 25.7 %all_to_all.20 = bf16[8,24,384]{2,1,0:T(8,128)(2,1)S(1)} all-to-all(bf16[8,24,384]{2,1,0:T(8,128)(2,1)S(1)} %broadcast_in_dim.17), channel_id=1, replica_groups={{0,4,8,12,16,20,24,28},{32,36,40,44,48,52,56,60},{64,68,72,76,80,84,88,..., dimensions={0} | all-to-all | bytes 294912 | tf_op jit(solution)/shard_map/all_to_all | solution.py:33
  27.1 1.2 %broadcast_in_dim.18 = bf16[8,8,24,384]{3,2,1,0:T(8,128)(2,1)} broadcast(bf16[8,24,384]{2,1,0:T(8,128)(2,1)S(1)} %all_to_all.20), dimensions={1,2,3} | broadcast | bytes 1327104 | tf_op jit(solution)/shard_map/broadcast_in_dim | solution.py:213
  28.3 0.0 copy-start
  28.3 7.7 %all-to-all-start.1 = ((bf16[8,8,24,384]{3,2,1,0:T(8,128)(2,1)}), bf16[8,8,24,384]{3,2,1,0:T(8,128)(2,1)S(1)}, u32[]{:S(2)}, u32[]{:S(2)}) async-start(bf16[8,8,24,384]{3,2,1,0:T(8,128)(2,1)} %broadcast_in_dim.18), calls=%async_computation.1 | async-start | bytes 2359296 | tf_op jit(solution)/shard_map/all_to_all | solution.py:33
  36.0 0.0 copy-done
  36.0 5.1 %collective-permute-start = (bf16[1,2,256,384]{3,2,1,0:T(8,128)(2,1)S(1)}, bf16[1,2,256,384]{3,2,1,0:T(8,128)(2,1)S(1)}, u32[]{:S(2)}, u32[]{:S(2)}) collective-permute-start(bf16[1,2,256,384]{3,2,1,0:T(8,128)(2,1)S(1)} %copy-done), channel_id=1, source_target_pairs={{0,256},{256,512},{512,768},{768,0},{1,257},{257,513},{513,769},{7... | collective-permute-start | bytes 1179656 | tf_op jit(solution)/shard_map/ppermute | solution.py:18
  41.1 6.6 %collective-permute-done.kv_hbm = bf16[1,2,256,384]{3,2,1,0:T(8,128)(2,1)S(1)} collective-permute-done((bf16[1,2,256,384]{3,2,1,0:T(8,128)(2,1)S(1)}, bf16[1,2,256,384]{3,2,1,0:T(8,128)(2,1)S(1)}, u32[]{:S(2)}, u32[]{:S(2)}) %collective-permute-start) | collective-permute-done | bytes 393248 | tf_op jit(solution)/shard_map/ppermute | solution.py:18
  47.7 4.0 %forward.1 = bf16[8,8,24,384]{3,2,1,0:T(8,128)(2,1)} custom-call(s32[1,2,2]{2,1,0:T(2,128)} %ids_hbm.3, s32[1,2]{1,0:T(1,128)} %cnt_hbm.3, bf16[1,256,384]{2,1,0:T(8,128)(2,1)} %q_hbm.3, bf16[1,2,256,384]{3,2,1,0:T(8,128)(2,1)S(1)} %collective-permute-done.kv_hbm, bf16[1,256,1536]{2,1,0:T(8,128)(2,1)} %cot_hbm.3), custom_call_target="tpu_custom_call" | custom-call | flops 402653184 | bytes 3145728 | tf_op jit(solution)/shard_map/forward/pallas_call | solution.py:197
  51.8 4.6 %all-to-all-done.1.far_hbm = bf16[8,8,24,384]{3,2,1,0:T(8,128)(2,1)S(1)} async-done(((bf16[8,8,24,384]{3,2,1,0:T(8,128)(2,1)}), bf16[8,8,24,384]{3,2,1,0:T(8,128)(2,1)S(1)}, u32[]{:S(2)}, u32[]{:S(2)}) %all-to-all-start.1) | async-done | bytes 1179680 | tf_op jit(solution)/shard_map/all_to_all | solution.py:33
  56.3 3.6 %all-to-all-start.2 = ((bf16[8,8,24,384]{3,2,1,0:T(8,128)(2,1)}), bf16[8,8,24,384]{3,2,1,0:T(8,128)(2,1)S(1)}, u32[]{:S(2)}, u32[]{:S(2)}) async-start(bf16[8,8,24,384]{3,2,1,0:T(8,128)(2,1)} %forward.1), calls=%async_computation.2 | async-start | bytes 2359296 | tf_op jit(solution)/shard_map/all_to_all | solution.py:33
  59.9 5.1 %backward.1 = (bf16[1,256,384]{2,1,0:T(8,128)(2,1)}, bf16[1,2,256,384]{3,2,1,0:T(8,128)(2,1)S(1)}) custom-call(s32[1,2,2]{2,1,0:T(2,128)} %ids_hbm.3, s32[1,2]{1,0:T(1,128)} %cnt_hbm.3, bf16[1,256,384]{2,1,0:T(8,128)(2,1)} %q_hbm.3, bf16[1,2,256,384]{3,2,1,0:T(8,128)(2,1)S(1)} %collective-permute-done.kv_hbm, bf16[1,256,1536]{2,1,0:T(8,128)(2,1)} %cot_hbm.3, ...), custom_call_target="tpu_custom_call" | custom-call | flops 603979776 | bytes 4194304 | tf_op jit(solution)/shard_map/backward/pallas_call | solution.py:214
  65.0 3.3 %collective-permute-start.1 = (bf16[1,2,256,384]{3,2,1,0:T(8,128)(2,1)S(1)}, bf16[1,2,256,384]{3,2,1,0:T(8,128)(2,1)S(1)}, u32[]{:S(2)}, u32[]{:S(2)}) collective-permute-start(bf16[1,2,256,384]{3,2,1,0:T(8,128)(2,1)S(1)} %get-tuple-element.8), channel_id=1, source_target_pairs={{0,768},{256,0},{512,256},{768,512},{1,769},{257,1},{513,257},{769... | collective-permute-start | bytes 1179656 | tf_op jit(solution)/shard_map/ppermute | solution.py:18
  68.3 11.9 %all-to-all-done.2.parts_ref = bf16[8,8,24,384]{3,2,1,0:T(8,128)(2,1)S(1)} async-done(((bf16[8,8,24,384]{3,2,1,0:T(8,128)(2,1)}), bf16[8,8,24,384]{3,2,1,0:T(8,128)(2,1)S(1)}, u32[]{:S(2)}, u32[]{:S(2)}) %all-to-all-start.2) | async-done | bytes 1179680 | tf_op jit(solution)/shard_map/all_to_all | solution.py:33
  80.2 0.2 fold.2
  80.3 11.6 %all_to_all.21.parts_ref = bf16[8,24,384]{2,1,0:T(8,128)(2,1)S(1)} all-to-all(bf16[8,24,384]{2,1,0:T(8,128)(2,1)S(1)} %fold.2), channel_id=1, replica_groups={{0,32,64,96,128,160,192,224},{4,36,68,100,132,164,196,228},{8,40,72,104..., dimensions={0} | all-to-all | bytes 294912 | tf_op jit(solution)/shard_map/all_to_all | solution.py:33
  92.0 0.6 fold.3
  92.6 0.0 collective-permute-done.1
  92.6 0.7 copy.10
Async XLA Ops:
  28.3 7.7 %copy-start = (bf16[1,2,256,384]{3,2,1,0:T(8,128)(2,1)S(1)}, bf16[1,2,256,384]{3,2,1,0:T(8,128)(2,1)}, u32[]{:S(2)}) copy-start(bf16[1,2,256,384]{3,2,1,0:T(8,128)(2,1)} %param.7) | copy-start | bytes 1179652
  28.3 28.1 %all-to-all-start.1 = ((bf16[8,8,24,384]{3,2,1,0:T(8,128)(2,1)}), bf16[8,8,24,384]{3,2,1,0:T(8,128)(2,1)S(1)}, u32[]{:S(2)}, u32[]{:S(2)}) async-start(bf16[8,8,24,384]{3,2,1,0:T(8,128)(2,1)} %broadcast_in_dim.18), calls=%async_computation.1 | async-start | bytes 2359296 | tf_op jit(solution)/shard_map/all_to_all | solution.py:33
  36.0 11.7 %collective-permute-start = (bf16[1,2,256,384]{3,2,1,0:T(8,128)(2,1)S(1)}, bf16[1,2,256,384]{3,2,1,0:T(8,128)(2,1)S(1)}, u32[]{:S(2)}, u32[]{:S(2)}) collective-permute-start(bf16[1,2,256,384]{3,2,1,0:T(8,128)(2,1)S(1)} %copy-done), channel_id=1, source_target_pairs={{0,256},{256,512},{512,768},{768,0},{1,257},{257,513},{513,769},{7... | collective-permute-start | bytes 1179656 | tf_op jit(solution)/shard_map/ppermute | solution.py:18
  56.3 23.8 %all-to-all-start.2 = ((bf16[8,8,24,384]{3,2,1,0:T(8,128)(2,1)}), bf16[8,8,24,384]{3,2,1,0:T(8,128)(2,1)S(1)}, u32[]{:S(2)}, u32[]{:S(2)}) async-start(bf16[8,8,24,384]{3,2,1,0:T(8,128)(2,1)} %forward.1), calls=%async_computation.2 | async-start | bytes 2359296 | tf_op jit(solution)/shard_map/all_to_all | solution.py:33
  65.0 27.6 %collective-permute-start.1 = (bf16[1,2,256,384]{3,2,1,0:T(8,128)(2,1)S(1)}, bf16[1,2,256,384]{3,2,1,0:T(8,128)(2,1)S(1)}, u32[]{:S(2)}, u32[]{:S(2)}) collective-permute-start(bf16[1,2,256,384]{3,2,1,0:T(8,128)(2,1)S(1)} %get-tuple-element.8), channel_id=1, source_target_pairs={{0,768},{256,0},{512,256},{768,512},{1,769},{257,1},{513,257},{769... | collective-permute-start | bytes 1179656 | tf_op jit(solution)/shard_map/ppermute | solution.py:18
